TPU v7x, 512 devices: a whole 4x8x8 slice. The times are simulated.
512 devices in a mesh: seq: 16 (over y, core), doc: 32 (over z, x).
Axes of the slice: x: 4, y: 8, z: 8, core: 2. Of those that a mesh axis runs over, the one named last changes fastest.
Arguments:
- queries: bfloat16 [262144, 512], P(('doc', 'seq')), parts along dimension 0, may hold values from -64 to 64
- keys: bfloat16 [262144, 512], P(('doc', 'seq')), parts along dimension 0, may hold values from -6 to 6
- values: bfloat16 [262144, 512], P(('doc', 'seq')), parts along dimension 0, may hold values from -6 to 6
- rates: float32 [262144], P(('doc', 'seq')), parts along dimension 0, may hold values from 0.1 to 1
- lengths: int32 [128], P('doc'), parts along dimension 0, may hold values from 1 to 4096, 8192 in all
- norm_gain: float32 [16384], P('doc'), parts along dimension 0, may hold values from 0.5 to 1.5
- w_gate: bfloat16 [16384, 512], P('doc'), parts along dimension 0, may hold values from -0.25 to 0.25
- w_up: bfloat16 [16384, 512], P('doc'), parts along dimension 0, may hold values from -0.25 to 0.25
- w_down: bfloat16 [16384, 512], P('doc'), parts along dimension 0, may hold values from -0.25 to 0.25
- mom_gate: float32 [16384, 512], P('doc', 'seq'), parts along dimension 0, may hold values from -3 to 3
- mom_up: float32 [16384, 512], P('doc', 'seq'), parts along dimension 0, may hold values from -3 to 3
- mom_down: float32 [16384, 512], P('doc', 'seq'), parts along dimension 0, may hold values from -3 to 3
Outputs:
- mixed: bfloat16 [262144, 512], P(('doc', 'seq')), parts along dimension 0
- new_mom_gate: float32 [16384, 512], P('doc', 'seq'), parts along dimension 0
- new_mom_up: float32 [16384, 512], P('doc', 'seq'), parts along dimension 0
- new_mom_down: float32 [16384, 512], P('doc', 'seq'), parts along dimension 0
There are 32 independent parts, one for each index of `doc`. A program takes and returns all parts, laid end to end along the dimension named above; each array names one. Nothing has to cross between parts.
All inputs are finite; a program needn't handle non-finite values.
Results may differ from a plain program's by a relative error of at most 0.019.
Values may be sent and summed in bfloat16 or wider, within the bound.
No kernel may reach another device: no remote copies, remote signals or barrier semaphores. Data moves between devices by JAX's collectives and lax.ppermute only.
A program may use at most 64 MiB of HBM per device.

v0:
```python
import jax
import jax.numpy as jnp
from jax import lax
from jax.sharding import PartitionSpec as P

WIN = 1024


momentum_decay = 0.9
step_size = 0.5


def shifted(block, axis, distance):
    devices = range(lax.axis_size(axis))
    route = [(i - distance, i) for i in devices if i - distance in devices]
    return lax.ppermute(block, axis, route)


def doc_ids(positions, ends):
    return jnp.sum((positions[:, None] >= ends[None, :]).astype(jnp.int32), axis=1)


def window_attention(qblk, kblk, vblk, qpos, kpos, ends):
    scores = jnp.dot(qblk, kblk.T, preferred_element_type=jnp.float32) * qblk.shape[1] ** (-0.5)
    same = doc_ids(qpos, ends)[:, None] == doc_ids(kpos, ends)[None, :]
    delta = qpos[:, None] - kpos[None, :]
    live = same & (delta >= 0) & (delta < WIN) & (kpos[None, :] >= 0)
    scores = jnp.where(live, scores, jnp.float32(-1e30))
    top = jnp.max(scores, axis=1, keepdims=True)
    weights = jnp.where(live, jnp.exp(scores - top), jnp.float32(0.0))
    total = jnp.sum(weights, axis=1, keepdims=True)
    probs = (weights / total).astype(jnp.bfloat16)
    return jnp.dot(probs, vblk, preferred_element_type=jnp.float32)


def silu_parts(gate):
    sig = jax.nn.sigmoid(gate)
    return (gate * sig, sig * (1.0 + gate * (1.0 - sig)))


def step_weight(weight, moment):
    normed = moment * lax.rsqrt(jnp.sum(moment * moment, axis=0, keepdims=True) + 1e-06)
    return (weight.astype(jnp.float32) - step_size * normed).astype(jnp.bfloat16)


def local(
    queries,
    keys,
    values,
    rates,
    lengths,
    norm_gain,
    w_gate,
    w_up,
    w_down,
    mom_gate,
    mom_up,
    mom_down,
):
    tok, width = queries.shape
    index = lax.axis_index("seq")
    ends = jnp.cumsum(lengths)
    reach = (WIN + tok - 1) // tok
    paired = jnp.stack((keys, values))
    earlier = [shifted(paired, "seq", hops) for hops in range(reach, 0, -1)]
    buffer = jnp.concatenate(earlier + [paired], axis=1)
    halo_len = reach * tok
    first = index * tok
    begin = halo_len - WIN
    qpos = first + 0 + jnp.arange(tok, dtype=jnp.int32)
    kpos = first + 0 - WIN + jnp.arange(tok + WIN, dtype=jnp.int32)
    pieces = window_attention(
        queries,
        buffer[0, begin : begin + tok + WIN],
        buffer[1, begin : begin + tok + WIN],
        qpos,
        kpos,
        ends,
    )
    gate = jnp.dot(keys, w_gate, preferred_element_type=jnp.float32)
    upper = jnp.dot(keys, w_up, preferred_element_type=jnp.float32)
    act, slope = silu_parts(gate)
    hidden = (act * upper).astype(jnp.bfloat16)
    err = (-(rates[:, None] * values.astype(jnp.float32))).astype(jnp.bfloat16)
    back = jnp.dot(err, w_down.T, preferred_element_type=jnp.float32)
    d_up = (back * act).astype(jnp.bfloat16)
    d_gate = (back * upper * slope).astype(jnp.bfloat16)
    part_gate = jnp.dot(keys.T, d_gate, preferred_element_type=jnp.float32)
    part_up = jnp.dot(keys.T, d_up, preferred_element_type=jnp.float32)
    part_down = jnp.dot(hidden.T, err, preferred_element_type=jnp.float32)
    scale = float(tok * lax.axis_size("seq")) ** (-0.5)
    hid_cols = mom_gate.shape[1]
    out_cols = mom_down.shape[1]
    sum_gate, sum_up, sum_down = (
        lax.psum_scatter(
            part_gate.astype(jnp.bfloat16), "seq", scatter_dimension=1, tiled=True
        ).astype(jnp.float32),
        lax.psum_scatter(
            part_up.astype(jnp.bfloat16), "seq", scatter_dimension=1, tiled=True
        ).astype(jnp.float32),
        lax.psum_scatter(
            part_down.astype(jnp.bfloat16), "seq", scatter_dimension=1, tiled=True
        ).astype(jnp.float32),
    )
    new_mom_gate = momentum_decay * mom_gate + sum_gate * scale
    new_mom_up = momentum_decay * mom_up + sum_up * scale
    new_mom_down = momentum_decay * mom_down + sum_down * scale
    shard_gate = step_weight(
        lax.dynamic_slice_in_dim(w_gate, index * hid_cols, hid_cols, 1), new_mom_gate
    )
    shard_up = step_weight(
        lax.dynamic_slice_in_dim(w_up, index * hid_cols, hid_cols, 1), new_mom_up
    )
    shard_down = step_weight(
        lax.dynamic_slice_in_dim(w_down, index * out_cols, out_cols, 1), new_mom_down
    )
    gate_new, up_new, down_new = (
        lax.all_gather(shard_gate, "seq", axis=1, tiled=True),
        lax.all_gather(shard_up, "seq", axis=1, tiled=True),
        lax.all_gather(shard_down, "seq", axis=1, tiled=True),
    )
    qa = jnp.dot(queries, gate_new, preferred_element_type=jnp.float32)
    qb = jnp.dot(queries, up_new, preferred_element_type=jnp.float32)
    qh = (jax.nn.silu(qa) * qb).astype(jnp.bfloat16)
    fast = jnp.dot(qh, down_new, preferred_element_type=jnp.float32)
    normed = fast * lax.rsqrt(jnp.mean(fast * fast, axis=1, keepdims=True) + 1e-06) * norm_gain
    mixed = (pieces + normed).astype(jnp.bfloat16)
    return (mixed, new_mom_gate, new_mom_up, new_mom_down)


def solution(mesh):
    in_specs = (
        P(("doc", "seq"), None),
        P(("doc", "seq"), None),
        P(("doc", "seq"), None),
        P(("doc", "seq")),
        P("doc"),
        P("doc"),
        P("doc", None),
        P("doc", None),
        P("doc", None),
        P("doc", "seq"),
        P("doc", "seq"),
        P("doc", "seq"),
    )
    out_specs = (P(("doc", "seq"), None), P("doc", "seq"), P("doc", "seq"), P("doc", "seq"))
    return jax.shard_map(local, mesh=mesh, in_specs=in_specs, out_specs=out_specs, check_vma=False)
```

profile of v0, /device:TPU:1, one launch (start us, length us, event | category | flops | bytes accessed | tf_op | source)
XLA Modules:
  0.0 261.2 jit_solution(15479746361720381000)
XLA Ops:
  7.2 0.0 copy-start
  7.2 0.0 reduce-scatter.6.cloned.1.call-start
  7.2 1.7 fusion.32
  9.0 2.1 fusion.23
  11.1 0.0 copy-start.6
  11.1 1.3 fusion.13
  12.4 0.0 reduce-scatter.6.cloned.1.call-update
  12.4 0.0 reduce-scatter.4.cloned.1.call-start
  12.5 0.4 fusion.31
  13.0 1.0 copy-done.5
  13.9 2.9 %fusion.12 = bf16[512,512]{0,1:T(8,128)(2,1)} fusion(bf16[512,512]{1,0:T(8,128)(2,1)S(1)} %copy-done.1, f32[512,512]{1,0:T(8,128)} %copy-done.3, f32[512,512]{1,0:T(8,128)S(1)} %fusion.23, f32[512,512]{1,0:T(8,128)S(1)} %fusion.31), kind=kOutput, calls=%fused_computation.25 | convolution fusion | flops 271319040 | bytes 4194304 | tf_op jit(solution)/shard_map/dot_general | solution.py:88
  16.8 0.0 reduce-scatter.4.cloned.1.call-update
  16.8 0.0 reduce-scatter.8.cloned.1.call-start
  16.9 0.1 pad_maximum_fusion
  17.0 0.0 copy-start.16
  17.0 4.6 %collective-permute-start.1 = (bf16[2,512,512]{2,1,0:T(8,128)(2,1)S(1)}, bf16[2,512,512]{2,1,0:T(8,128)(2,1)}, u32[]{:S(2)}, u32[]{:S(2)}) collective-permute-start(bf16[2,512,512]{2,1,0:T(8,128)(2,1)S(1)} %pad_maximum_fusion), channel_id=1, source_target_pairs={{0,32},{32,64},{64,96},{96,128},{128,160},{160,192},{192,224},{224... | collective-permute-start | bytes 3145736 | tf_op jit(solution)/shard_map/ppermute | solution.py:16
  21.6 4.2 %collective-permute-start = (bf16[2,512,512]{2,1,0:T(8,128)(2,1)S(1)}, bf16[2,512,512]{2,1,0:T(8,128)(2,1)}, u32[]{:S(2)}, u32[]{:S(2)}) collective-permute-start(bf16[2,512,512]{2,1,0:T(8,128)(2,1)S(1)} %pad_maximum_fusion), channel_id=1, source_target_pairs={{0,64},{32,96},{64,128},{96,160},{128,192},{160,224},{192,256},{22... | collective-permute-start | bytes 3145736 | tf_op jit(solution)/shard_map/ppermute | solution.py:16
  25.8 3.1 %convolution_convert_fusion = bf16[512,512]{0,1:T(8,128)(2,1)} fusion(f32[512,512]{1,0:T(8,128)} %copy-done.5, f32[512,512]{1,0:T(8,128)} %copy-done.3, bf16[512,512]{1,0:T(8,128)(2,1)S(1)} %copy-done.2, f32[512]{0:T(512)S(1)} %copy-done.14), kind=kOutput, calls=%fused_computation.20 | convolution fusion | flops 271319040 | bytes 3147776 | tf_op jit(solution)/shard_map/dot_general | solution.py:90
  28.9 0.0 reduce-scatter.8.cloned.1.call-update
  28.9 0.6 broadcast_compare_fusion
  29.5 1.0 constant_dynamic-slice_fusion.2
  30.5 1.0 constant_dynamic-slice_fusion
  31.6 0.2 reduce-window.8
  31.7 0.7 convert_reduce_fusion.1
  32.4 0.1 convert_reduce_fusion
  32.5 0.7 copy.27
  33.2 0.1 copy.29
  33.3 0.1 copy.28
  33.4 42.8 %reduce-scatter.6.cloned.1.call-done = bf16[512,32]{0,1:T(8,128)(2,1)} async-done(((bf16[512,512]{0,1:T(8,128)(2,1)}), bf16[512,32]{0,1:T(8,128)(2,1)}) %reduce-scatter.6.cloned.1.call-update) | async-done | bytes 32784 | tf_op jit(solution)/shard_map/reduce_scatter | solution.py:98
  76.2 1.0 multiply_reduce_fusion.2
  77.2 60.9 %reduce-scatter.4.cloned.1.call-done = bf16[512,32]{0,1:T(8,128)(2,1)} async-done(((bf16[512,512]{0,1:T(8,128)(2,1)}), bf16[512,32]{0,1:T(8,128)(2,1)}) %reduce-scatter.4.cloned.1.call-update) | async-done | bytes 32784 | tf_op jit(solution)/shard_map/reduce_scatter | solution.py:95
  138.1 1.0 multiply_reduce_fusion.3
  139.1 0.1 subtract_convert_fusion.1
  139.2 17.9 %all_gather.10 = bf16[512,512]{0,1:T(8,128)(2,1)S(1)} all-gather(bf16[512,32]{0,1:T(8,128)(2,1)S(1)} %subtract_convert_fusion.1), channel_id=1, replica_groups=mesh['seq'=16,'doc'=32] {'seq'}, dimensions={1}, use_global_device_ids=true | all-gather | bytes 557056 | tf_op jit(solution)/shard_map/all_gather | solution.py:119
  157.1 43.1 %reduce-scatter.8.cloned.1.call-done = bf16[512,32]{0,1:T(8,128)(2,1)} async-done(((bf16[512,512]{0,1:T(8,128)(2,1)}), bf16[512,32]{0,1:T(8,128)(2,1)}) %reduce-scatter.8.cloned.1.call-update) | async-done | bytes 32784 | tf_op jit(solution)/shard_map/reduce_scatter | solution.py:101
  200.2 1.0 multiply_reduce_fusion.1
  201.2 0.1 subtract_convert_fusion
  201.2 19.3 %all_gather.11 = bf16[512,512]{0,1:T(8,128)(2,1)} all-gather(bf16[512,32]{0,1:T(8,128)(2,1)S(1)} %subtract_convert_fusion), channel_id=1, replica_groups=mesh['seq'=16,'doc'=32] {'seq'}, dimensions={1}, use_global_device_ids=true | all-gather | bytes 557056 | tf_op jit(solution)/shard_map/all_gather | solution.py:120
  220.5 0.8 subtract_convert_fusion.2
  221.3 17.4 %all_gather.9 = bf16[512,512]{0,1:T(8,128)(2,1)S(1)} all-gather(bf16[512,32]{0,1:T(8,128)(2,1)S(1)} %subtract_convert_fusion.2), channel_id=1, replica_groups=mesh['seq'=16,'doc'=32] {'seq'}, dimensions={1}, use_global_device_ids=true | all-gather | bytes 557056 | tf_op jit(solution)/shard_map/all_gather | solution.py:118
  238.7 1.5 convolution_bitcast_fusion.1
  240.2 3.3 %multiply_reduce_fusion = (f32[512]{0:T(512)S(1)}, f32[512,512]{0,1:T(8,128)}) fusion(bf16[512,512]{0,1:T(8,128)(2,1)} %all_gather.11, bf16[512,512]{0,1:T(8,128)(2,1)S(1)} %all_gather.10, bf16[512,512]{1,0:T(8,128)(2,1)S(1)} %copy-done, f32[512,512]{1,0:T(8,128)} %convolution_bitcast_fusion.1), kind=kOutput, calls=%fused_computation.28 | convolution fusion | flops 538967552 | bytes 3672064 | tf_op jit(solution)/shard_map/dot_general | solution.py:125
  243.4 2.5 copy.25
  246.0 1.7 maximum_maximum_fusion
  247.8 1.8 fusion.30
  249.6 0.0 copy-start.15
  249.6 1.9 fusion.5
  251.6 3.1 %fusion.9 = bf16[512,512]{1,0:T(8,128)(2,1)} fusion(bf16[2,1536,512]{2,1,0:T(8,128)(2,1)S(1)} %maximum_maximum_fusion, f32[512,1536]{0,1:T(8,128)S(1)} %get-tuple-element.11, f32[512]{0:T(512)S(1)} %fusion.5, f32[512]{0:T(512)S(1)} %get-tuple-element.10, f32[512,512]{1,0:T(8,128)S(1)} %copy-done.4, f32[512]{0:T(512)S(1)} %copy-done.15, ...), kind=kOutput, calls=%fused_computation.19 | convolution fusion | flops 815005696 | bytes 6322176 | tf_op jit(solution)/shard_map/dot_general | solution.py:33
  (37 shorter events, 0.1 us)
Async XLA Ops:
  7.2 231.5 %copy-start = (bf16[512,512]{1,0:T(8,128)(2,1)S(1)}, bf16[512,512]{1,0:T(8,128)(2,1)}, u32[]{:S(2)}) copy-start(bf16[512,512]{1,0:T(8,128)(2,1)} %param.12) | copy-start | bytes 1572868
  7.2 3.9 %copy-start.1 = (bf16[512,512]{1,0:T(8,128)(2,1)S(1)}, bf16[512,512]{1,0:T(8,128)(2,1)}, u32[]{:S(2)}) copy-start(bf16[512,512]{1,0:T(8,128)(2,1)} %param.13) | copy-start | bytes 1572868
  7.2 69.0 %reduce-scatter.6.cloned.1.call-start = ((), (), s32[]{:S(2)}) async-start(), calls=%async_computation.4 | async-start | bytes 557056 | tf_op jit(solution)/shard_map/reduce_scatter | solution.py:98
  9.0 2.1 copy-start.3
  11.1 1.4 copy-start.6
  12.4 125.7 %reduce-scatter.4.cloned.1.call-start = ((), (), s32[]{:S(2)}) async-start(), calls=%async_computation.3 | async-start | bytes 557056 | tf_op jit(solution)/shard_map/reduce_scatter | solution.py:95
  12.9 1.0 copy-start.5
  13.9 2.9 %copy-start.2 = (bf16[512,512]{1,0:T(8,128)(2,1)S(1)}, bf16[512,512]{1,0:T(8,128)(2,1)}, u32[]{:S(2)}) copy-start(bf16[512,512]{1,0:T(8,128)(2,1)} %param.14) | copy-start | bytes 1572868
  13.9 11.9 %copy-start.14 = (f32[512]{0:T(512)S(1)}, f32[512]{0:T(512)}, u32[]{:S(2)}) copy-start(f32[512]{0:T(512)} %param.15) | copy-start | bytes 6148
  16.8 183.3 %reduce-scatter.8.cloned.1.call-start = ((), (), s32[]{:S(2)}) async-start(), calls=%async_computation.5 | async-start | bytes 557056 | tf_op jit(solution)/shard_map/reduce_scatter | solution.py:101
  17.0 14.6 %copy-start.16 = (s32[4]{0:T(128)S(1)}, s32[4]{0:T(128)}, u32[]{:S(2)}) copy-start(s32[4]{0:T(128)} %param.16) | copy-start | bytes 52
  17.0 229.0 %collective-permute-start.1 = (bf16[2,512,512]{2,1,0:T(8,128)(2,1)S(1)}, bf16[2,512,512]{2,1,0:T(8,128)(2,1)}, u32[]{:S(2)}, u32[]{:S(2)}) collective-permute-start(bf16[2,512,512]{2,1,0:T(8,128)(2,1)S(1)} %pad_maximum_fusion), channel_id=1, source_target_pairs={{0,32},{32,64},{64,96},{96,128},{128,160},{160,192},{192,224},{224... | collective-permute-start | bytes 3145736 | tf_op jit(solution)/shard_map/ppermute | solution.py:16
  21.6 224.5 %collective-permute-start = (bf16[2,512,512]{2,1,0:T(8,128)(2,1)S(1)}, bf16[2,512,512]{2,1,0:T(8,128)(2,1)}, u32[]{:S(2)}, u32[]{:S(2)}) collective-permute-start(bf16[2,512,512]{2,1,0:T(8,128)(2,1)S(1)} %pad_maximum_fusion), channel_id=1, source_target_pairs={{0,64},{32,96},{64,128},{96,160},{128,192},{160,224},{192,256},{22... | collective-permute-start | bytes 3145736 | tf_op jit(solution)/shard_map/ppermute | solution.py:16
  28.9 2.8 %copy-start.10 = (s32[512]{0:T(512)}, s32[512]{0:T(512)S(1)}, u32[]{:S(2)}) copy-start(s32[512]{0:T(512)S(1)} %iota_add_fusion.1) | copy-start | bytes 6148
  77.2 166.2 %copy-start.7 = (f32[512,32]{0,1:T(8,128)}, f32[512,32]{0,1:T(8,128)S(1)}, u32[]{:S(2)}) copy-start(f32[512,32]{0,1:T(8,128)S(1)} %get-tuple-element.7) | copy-start | bytes 196612
  139.1 104.3 %copy-start.8 = (f32[512,32]{0,1:T(8,128)}, f32[512,32]{0,1:T(8,128)S(1)}, u32[]{:S(2)}) copy-start(f32[512,32]{0,1:T(8,128)S(1)} %get-tuple-element.5) | copy-start | bytes 196612
  201.1 42.3 %copy-start.9 = (f32[512,32]{0,1:T(8,128)}, f32[512,32]{0,1:T(8,128)S(1)}, u32[]{:S(2)}) copy-start(f32[512,32]{0,1:T(8,128)S(1)} %get-tuple-element.9) | copy-start | bytes 196612
  246.0 1.8 copy-start.11
  246.0 1.8 copy-start.12
  246.0 1.8 copy-start.13
  249.6 1.9 copy-start.4
  249.6 1.9 copy-start.15
Sparse Core Ops, SparseCore 0:
  12.6 63.6 reduce-scatter.5
  79.0 59.0 reduce-scatter.3
  141.5 58.6 reduce-scatter.7
where the time goes:
time: 262 us; the launch traced here: 261 us
  waiting for transfers between devices  147 us (56%)
  blocking collectives  54.5 us (21%)
  matrix products  21.2 us (8%)
  between operations  14.1 us (5%)
  other arithmetic  9.19 us (4%)
  starting transfers between devices  8.92 us (3%)
  local copies, waits for them, and re-layouts  6.51 us (2%)
    reduce_scatter x1, waiting for transfers between devices, local(): lax.psum_scatter(part_gate.astype(jnp.bfloat16), 'seq', scatter_dimension...  60.9 us
    reduce_scatter x1, waiting for transfers between devices, local(): lax.psum_scatter(part_down.astype(jnp.bfloat16), 'seq', scatter_dimension...  43.1 us
    reduce_scatter x1, waiting for transfers between devices, local(): lax.psum_scatter(part_up.astype(jnp.bfloat16), 'seq', scatter_dimension=1...  42.8 us
    all_gather x1, blocking collectives, local(): lax.all_gather(shard_down, 'seq', axis=1, tiled=True)  19.3 us
    all_gather x1, blocking collectives, local(): lax.all_gather(shard_up, 'seq', axis=1, tiled=True)  17.9 us
    all_gather x1, blocking collectives, local(): lax.all_gather(shard_gate, 'seq', axis=1, tiled=True)  17.4 us
    ppermute x2, starting transfers between devices, shifted(): return lax.ppermute(block, axis, route)  8.8 us
  transfers between devices with their start and end apart: 5, of which 3 were waited for; matrix products, arithmetic and copies ran while one was open for 8% of the time, Pallas kernels for 0%

commit v1 on v0

--- a/solution.py
+++ b/solution.py
@@ -38,9 +38,8 @@
     return (gate * sig, sig * (1.0 + gate * (1.0 - sig)))
 
 
-def step_weight(weight, moment):
-    normed = moment * lax.rsqrt(jnp.sum(moment * moment, axis=0, keepdims=True) + 1e-06)
-    return (weight.astype(jnp.float32) - step_size * normed).astype(jnp.bfloat16)
+PARTNER = [(i, i ^ 1) for i in range(16)]
+SAME_CORE = [[c + 2 * k for k in range(8)] for c in range(2)]
 
 
 def local(
@@ -85,40 +84,41 @@
     back = jnp.dot(err, w_down.T, preferred_element_type=jnp.float32)
     d_up = (back * act).astype(jnp.bfloat16)
     d_gate = (back * upper * slope).astype(jnp.bfloat16)
-    part_gate = jnp.dot(keys.T, d_gate, preferred_element_type=jnp.float32)
-    part_up = jnp.dot(keys.T, d_up, preferred_element_type=jnp.float32)
-    part_down = jnp.dot(hidden.T, err, preferred_element_type=jnp.float32)
+    parts = [
+        lax.dot_general(x, y, (((0,), (0,)), ((), ())), preferred_element_type=jnp.float32)
+        .astype(jnp.bfloat16)
+        .reshape(8, 2, 32, width)
+        for x, y in ((d_gate, keys), (d_up, keys), (err, hidden))
+    ]
+    parts = jnp.concatenate(parts, axis=2)
+    core = index % 2
+    mine = lax.dynamic_index_in_dim(parts, core, 1, keepdims=False)
+    other = lax.dynamic_index_in_dim(parts, 1 - core, 1, keepdims=False)
+    got = lax.ppermute(other, "seq", PARTNER)
+    both = (mine.astype(jnp.float32) + got.astype(jnp.float32)).astype(jnp.bfloat16)
+    came = lax.all_to_all(both, "seq", 0, 0, axis_index_groups=SAME_CORE)
+    total = jnp.sum(came.astype(jnp.float32), axis=0)
     scale = float(tok * lax.axis_size("seq")) ** (-0.5)
-    hid_cols = mom_gate.shape[1]
-    out_cols = mom_down.shape[1]
-    sum_gate, sum_up, sum_down = (
-        lax.psum_scatter(
-            part_gate.astype(jnp.bfloat16), "seq", scatter_dimension=1, tiled=True
-        ).astype(jnp.float32),
-        lax.psum_scatter(
-            part_up.astype(jnp.bfloat16), "seq", scatter_dimension=1, tiled=True
-        ).astype(jnp.float32),
-        lax.psum_scatter(
-            part_down.astype(jnp.bfloat16), "seq", scatter_dimension=1, tiled=True
-        ).astype(jnp.float32),
+    cols = mom_gate.shape[1]
+    moms = jnp.concatenate((mom_gate.T, mom_up.T, mom_down.T), axis=0)
+    weights = jnp.concatenate(
+        [lax.dynamic_slice_in_dim(w, index * cols, cols, 1).T for w in (w_gate, w_up, w_down)], axis=0
     )
-    new_mom_gate = momentum_decay * mom_gate + sum_gate * scale
-    new_mom_up = momentum_decay * mom_up + sum_up * scale
-    new_mom_down = momentum_decay * mom_down + sum_down * scale
-    shard_gate = step_weight(
-        lax.dynamic_slice_in_dim(w_gate, index * hid_cols, hid_cols, 1), new_mom_gate
+    new_moms = momentum_decay * moms + total * scale
+    new_mom_gate, new_mom_up, new_mom_down = [
+        new_moms[k * cols : (k + 1) * cols].T for k in range(3)
+    ]
+    normed = new_moms * lax.rsqrt(jnp.sum(new_moms * new_moms, axis=1, keepdims=True) + 1e-06)
+    shard = (weights.astype(jnp.float32) - step_size * normed).astype(jnp.bfloat16)
+    spread = jnp.broadcast_to(shard[None], (8,) + shard.shape)
+    spread = lax.all_to_all(spread, "seq", 0, 0, axis_index_groups=SAME_CORE)
+    swapped = lax.ppermute(spread, "seq", PARTNER)
+    pair = jnp.stack(
+        (jnp.where(core == 0, spread, swapped), jnp.where(core == 0, swapped, spread)), axis=1
     )
-    shard_up = step_weight(
-        lax.dynamic_slice_in_dim(w_up, index * hid_cols, hid_cols, 1), new_mom_up
-    )
-    shard_down = step_weight(
-        lax.dynamic_slice_in_dim(w_down, index * out_cols, out_cols, 1), new_mom_down
-    )
-    gate_new, up_new, down_new = (
-        lax.all_gather(shard_gate, "seq", axis=1, tiled=True),
-        lax.all_gather(shard_up, "seq", axis=1, tiled=True),
-        lax.all_gather(shard_down, "seq", axis=1, tiled=True),
-    )
+    gate_new, up_new, down_new = [
+        pair[:, :, k * cols : (k + 1) * cols].reshape(width, width).T for k in range(3)
+    ]
     qa = jnp.dot(queries, gate_new, preferred_element_type=jnp.float32)
     qb = jnp.dot(queries, up_new, preferred_element_type=jnp.float32)
     qh = (jax.nn.silu(qa) * qb).astype(jnp.bfloat16)

time: 262 us -> 121 us (0.46)
  waiting for transfers between devices: 147 us -> 56.4 us
  blocking collectives: 54.5 us -> 0 us
  starting transfers between devices: 8.92 us -> 25.9 us
  between operations: 14.1 us -> 0.98 us
    reduce_scatter x3 -> x0, waiting for transfers between devices: 147 us -> none  [the longest x1 60.9 us: local(): lax.psum_scatter(part_gate.astype(jnp.bfloat16), 'seq', scatter_dimension...]
    all_gather x3 -> x0, blocking collectives: 54.5 us -> none  [the longest x1 19.3 us: local(): lax.all_gather(shard_down, 'seq', axis=1, tiled=True)]
    ppermute x2, waiting for transfers between devices: 0.01 us -> 33 us  [shifted(): return lax.ppermute(block, axis, route)]
    all_to_all x0 -> x2, waiting for transfers between devices: none -> 21.2 us  [the longest x1 12.1 us: local(): came = lax.all_to_all(both, 'seq', 0, 0, axis_index_groups=SAME_CORE)]
    ppermute x0 -> x2, starting transfers between devices: none -> 10.6 us  [the longest x1 8.74 us: local(): got = lax.ppermute(other, 'seq', PARTNER)]
    all_to_all x0 -> x2, starting transfers between devices: none -> 7.22 us  [the longest x1 3.68 us: local(): came = lax.all_to_all(both, 'seq', 0, 0, axis_index_groups=SAME_CORE)]
    dot_general x3, matrix products: 7.22 us -> 4.34 us  [local(): lax.dot_general(x, y, (((0,), (0,)), ((), ())), preferred_element_type=jn...]
    reduce_sum x3 -> x2, other arithmetic: 2.94 us -> 0.23 us  [the longest x1 0.13 us: local(): jnp.sum(new_moms * new_moms, axis=1, keepdims=True) + 1e-06]
  transfers between devices with their start and end apart: 5 -> 6, of which waited for: 3 -> 5; matrix products, arithmetic and copies ran while one was open for 8% -> 12% of each run, Pallas kernels for 0% -> 0%
where the time goes in v1:
time: 121 us; the launch traced here: 120 us
  waiting for transfers between devices  56.4 us (47%)
  starting transfers between devices  25.9 us (21%)
  matrix products  20 us (17%)
  other arithmetic  11.4 us (9%)
  local copies, waits for them, and re-layouts  5.4 us (4%)
    ppermute x2, waiting for transfers between devices, shifted(): return lax.ppermute(block, axis, route)  33 us
    all_to_all x1, waiting for transfers between devices, local(): came = lax.all_to_all(both, 'seq', 0, 0, axis_index_groups=SAME_CORE)  12.1 us
    all_to_all x1, waiting for transfers between devices, local(): spread = lax.all_to_all(spread, 'seq', 0, 0, axis_index_groups=SAME_CORE)  9.07 us
    ppermute x1, starting transfers between devices, local(): got = lax.ppermute(other, 'seq', PARTNER)  8.74 us
    ppermute x2, starting transfers between devices, shifted(): return lax.ppermute(block, axis, route)  8.01 us
    dot_general x1, matrix products, window_attention(): return jnp.dot(probs, vblk, preferred_element_type=jnp.float32)  5.43 us
    dot_general x3, matrix products, local(): lax.dot_general(x, y, (((0,), (0,)), ((), ())), preferred_element_type=jn...  4.34 us
    dot_general x1, matrix products, window_attention(): jnp.dot(qblk, kblk.T, preferred_element_type=jnp.float32)  3.82 us
  transfers between devices with their start and end apart: 6, of which 5 were waited for; matrix products, arithmetic and copies ran while one was open for 12% of the time, Pallas kernels for 0%

profile of v1, /device:TPU:1, one launch (start us, length us, event | category | flops | bytes accessed | tf_op | source)
XLA Modules:
  0.0 120.1 jit_solution(14951414274184607040)
XLA Ops:
  0.6 0.0 copy-start
  0.7 0.0 copy-start.4
  0.7 0.0 copy-start.1
  0.7 1.8 %fusion.35 = f32[512,512]{1,0:T(8,128)S(1)} fusion(bf16[512,512]{1,0:T(8,128)(2,1)} %param.13, bf16[512,512]{1,0:T(8,128)(2,1)} %param.18), kind=kOutput, calls=%fused_computation.78 | convolution fusion | flops 268435456 | bytes 2097152 | tf_op jit(solution)/shard_map/dot_general | solution.py:79
  2.5 1.6 %fusion.34 = f32[512,512]{1,0:T(8,128)S(1)} fusion(bf16[512,512]{1,0:T(8,128)(2,1)} %param.13, bf16[512,512]{1,0:T(8,128)(2,1)} %param.19), kind=kOutput, calls=%fused_computation.77 | convolution fusion | flops 268435456 | bytes 2097152 | tf_op jit(solution)/shard_map/dot_general | solution.py:80
  4.1 0.5 fusion.25
  4.7 1.3 %convolution_convert_fusion.1 = bf16[512,512]{1,0:T(8,128)(2,1)} fusion(bf16[512,512]{1,0:T(8,128)(2,1)S(1)} %copy-done.1, f32[512,512]{1,0:T(8,128)S(1)} %fusion.25, f32[512,512]{1,0:T(8,128)S(1)} %fusion.35), kind=kOutput, calls=%fused_computation.29 | convolution fusion | flops 270270464 | bytes 3145728 | tf_op jit(solution)/shard_map/dot_general | solution.py:88
  6.0 1.5 %convolution_convert_fusion.2 = bf16[512,512]{1,0:T(8,128)(2,1)} fusion(bf16[512,512]{1,0:T(8,128)(2,1)S(1)} %copy-done.1, f32[512,512]{1,0:T(8,128)S(1)} %fusion.35, f32[512,512]{1,0:T(8,128)S(1)} %fusion.25, f32[512,512]{1,0:T(8,128)S(1)} %fusion.34), kind=kOutput, calls=%fused_computation.30 | convolution fusion | flops 271319040 | bytes 4194304 | tf_op jit(solution)/shard_map/dot_general | solution.py:88
  7.5 1.5 %convolution_convert_fusion = bf16[512,512]{1,0:T(8,128)(2,1)} fusion(f32[512,512]{1,0:T(8,128)S(1)} %fusion.34, f32[512,512]{1,0:T(8,128)S(1)} %fusion.35, bf16[512,512]{1,0:T(8,128)(2,1)S(1)} %copy-done.2, f32[512]{0:T(512)S(1)} %copy-done.8), kind=kOutput, calls=%fused_computation.28 | convolution fusion | flops 271319040 | bytes 3147776 | tf_op jit(solution)/shard_map/dot_general | solution.py:88
  9.0 1.5 %pad_maximum_fusion = bf16[8,2,96,512]{3,2,1,0:T(8,128)(2,1)S(1)} fusion(bf16[8,2,32,512]{3,2,1,0:T(8,128)(2,1)} %bitcast.81, bf16[8,2,32,512]{3,2,1,0:T(8,128)(2,1)} %bitcast.79, bf16[8,2,32,512]{3,2,1,0:T(8,128)(2,1)} %bitcast.80), kind=kLoop, calls=%fused_computation.19 | loop fusion | flops 4718592 | bytes 3145728 | tf_op jit(solution)/shard_map/concatenate | solution.py:93
  10.5 1.0 dynamic-slice_bitcast_fusion
  11.5 8.7 %collective-permute-start.2 = (bf16[8,96,512]{2,1,0:T(8,128)(2,1)}, bf16[8,96,512]{2,1,0:T(8,128)(2,1)}, u32[]{:S(2)}, u32[]{:S(2)}) collective-permute-start(bf16[8,96,512]{2,1,0:T(8,128)(2,1)} %dynamic-slice_bitcast_fusion), channel_id=1, source_target_pairs={{0,32},{32,0},{64,96},{96,64},{128,160},{160,128},{192,224},{224,1... | collective-permute-start | bytes 2359304 | tf_op jit(solution)/shard_map/ppermute | solution.py:97
  20.3 2.2 %collective-permute-done.2 = bf16[8,96,512]{2,1,0:T(8,128)(2,1)} collective-permute-done((bf16[8,96,512]{2,1,0:T(8,128)(2,1)}, bf16[8,96,512]{2,1,0:T(8,128)(2,1)}, u32[]{:S(2)}, u32[]{:S(2)}) %collective-permute-start.2) | collective-permute-done | bytes 786464 | tf_op jit(solution)/shard_map/ppermute | solution.py:97
  22.5 2.3 %fusion.7 = bf16[8,96,512]{2,1,0:T(8,128)(2,1)} fusion(bf16[8,96,512]{2,1,0:T(8,128)(2,1)} %collective-permute-done.2, bf16[8,2,96,512]{3,2,1,0:T(8,128)(2,1)S(1)} %pad_maximum_fusion, s32[]{:T(128)S(6)} %select_n.43), kind=kLoop, calls=%fused_computation.21 | loop fusion | flops 1572864 | bytes 2359300 | tf_op jit(solution)/shard_map/convert_element_type | solution.py:98
  24.7 3.7 %all-to-all-start = ((bf16[8,96,512]{2,1,0:T(8,128)(2,1)}), bf16[8,96,512]{2,1,0:T(8,128)(2,1)S(1)}, u32[]{:S(2)}, u32[]{:S(2)}) async-start(bf16[8,96,512]{2,1,0:T(8,128)(2,1)} %fusion.7), calls=%async_computation | async-start | bytes 1572864 | tf_op jit(solution)/shard_map/all_to_all | solution.py:99
  28.4 1.1 pad_maximum_fusion.1
  29.5 3.9 %collective-permute-start.1 = (bf16[2,512,512]{2,1,0:T(8,128)(2,1)}, bf16[2,512,512]{2,1,0:T(8,128)(2,1)}, u32[]{:S(2)}, u32[]{:S(2)}) collective-permute-start(bf16[2,512,512]{2,1,0:T(8,128)(2,1)} %pad_maximum_fusion.1), channel_id=1, source_target_pairs={{0,32},{32,64},{64,96},{96,128},{128,160},{160,192},{192,224},{224... | collective-permute-start | bytes 3145736 | tf_op jit(solution)/shard_map/ppermute | solution.py:16
  33.4 4.1 %collective-permute-start = (bf16[2,512,512]{2,1,0:T(8,128)(2,1)}, bf16[2,512,512]{2,1,0:T(8,128)(2,1)}, u32[]{:S(2)}, u32[]{:S(2)}) collective-permute-start(bf16[2,512,512]{2,1,0:T(8,128)(2,1)} %pad_maximum_fusion.1), channel_id=1, source_target_pairs={{0,64},{32,96},{64,128},{96,160},{128,192},{160,224},{192,256},{22... | collective-permute-start | bytes 3145736 | tf_op jit(solution)/shard_map/ppermute | solution.py:16
  37.5 1.0 constant_dynamic-slice_fusion.2
  38.5 0.1 copy.36
  38.6 1.1 constant_dynamic-slice_fusion
  39.7 0.1 copy.38
  39.8 0.1 copy.37
  39.9 12.1 %all-to-all-done = bf16[8,96,512]{2,1,0:T(8,128)(2,1)S(1)} async-done(((bf16[8,96,512]{2,1,0:T(8,128)(2,1)}), bf16[8,96,512]{2,1,0:T(8,128)(2,1)S(1)}, u32[]{:S(2)}, u32[]{:S(2)}) %all-to-all-start) | async-done | bytes 786464 | tf_op jit(solution)/shard_map/all_to_all | solution.py:99
  52.0 0.1 convert_reduce_fusion
  52.1 0.1 multiply_reduce_fusion.1
  52.3 0.1 subtract_convert_fusion
  52.4 1.0 broadcast_in_dim.11
  53.4 3.5 %all-to-all-start.1 = ((bf16[8,96,512]{2,1,0:T(8,128)(2,1)}), bf16[8,96,512]{2,1,0:T(8,128)(2,1)S(1)}, u32[]{:S(2)}, u32[]{:S(2)}) async-start(bf16[8,96,512]{2,1,0:T(8,128)(2,1)} %broadcast_in_dim.11), calls=%async_computation.1 | async-start | bytes 1572864 | tf_op jit(solution)/shard_map/all_to_all | solution.py:114
  56.9 0.2 reduce-window.8
  57.1 0.1 convert_reduce_fusion.2
  57.2 0.1 convert_reduce_fusion.1
  57.3 14.9 %collective-permute-done.1 = bf16[2,512,512]{2,1,0:T(8,128)(2,1)} collective-permute-done((bf16[2,512,512]{2,1,0:T(8,128)(2,1)}, bf16[2,512,512]{2,1,0:T(8,128)(2,1)}, u32[]{:S(2)}, u32[]{:S(2)}) %collective-permute-start.1) | collective-permute-done | bytes 1048608 | tf_op jit(solution)/shard_map/ppermute | solution.py:16
  72.2 18.1 %collective-permute-done = bf16[2,512,512]{2,1,0:T(8,128)(2,1)} collective-permute-done((bf16[2,512,512]{2,1,0:T(8,128)(2,1)}, bf16[2,512,512]{2,1,0:T(8,128)(2,1)}, u32[]{:S(2)}, u32[]{:S(2)}) %collective-permute-start) | collective-permute-done | bytes 1048608 | tf_op jit(solution)/shard_map/ppermute | solution.py:16
  90.3 3.0 %maximum_maximum_fusion = bf16[2,1536,512]{2,1,0:T(8,128)(2,1)} fusion(bf16[1,512,512]{2,1,0:T(8,128)(2,1)S(1)} %bitcast.77, bf16[1,512,512]{2,1,0:T(8,128)(2,1)S(1)} %bitcast.75, bf16[2,512,512]{2,1,0:T(8,128)(2,1)} %collective-permute-done.1, bf16[2,512,512]{2,1,0:T(8,128)(2,1)} %collective-permute-done), kind=kLoop, calls=%fused_computation.5 | loop fusion | flops 12582912 | bytes 6291456 | tf_op jit(solution)/shard_map/concatenate | solution.py:65
  93.3 9.1 %all-to-all-done.1 = bf16[8,96,512]{2,1,0:T(8,128)(2,1)S(1)} async-done(((bf16[8,96,512]{2,1,0:T(8,128)(2,1)}), bf16[8,96,512]{2,1,0:T(8,128)(2,1)S(1)}, u32[]{:S(2)}, u32[]{:S(2)}) %all-to-all-start.1) | async-done | bytes 786464 | tf_op jit(solution)/shard_map/all_to_all | solution.py:114
  102.4 1.9 %collective-permute-start.3 = (bf16[8,96,512]{2,1,0:T(8,128)(2,1)S(1)}, bf16[8,96,512]{2,1,0:T(8,128)(2,1)S(1)}, u32[]{:S(2)}, u32[]{:S(2)}) collective-permute-start(bf16[8,96,512]{2,1,0:T(8,128)(2,1)S(1)} %all-to-all-done.1), channel_id=1, source_target_pairs={{0,32},{32,0},{64,96},{96,64},{128,160},{160,128},{192,224},{224,1... | collective-permute-start | bytes 2359304 | tf_op jit(solution)/shard_map/ppermute | solution.py:115
  104.3 3.8 %fusion.33 = (f32[512]{0:T(512)S(1)}, f32[512,1536]{0,1:T(8,128)S(1)}) fusion(bf16[512,512]{1,0:T(8,128)(2,1)S(1)} %copy-done, bf16[2,1536,512]{2,1,0:T(8,128)(2,1)} %maximum_maximum_fusion, pred[1536]{0:T(1024)(128)(4,1)S(1)} %broadcast_compare_fusion, s32[1536]{0:T(1024)S(1)} %iota_add_fusion, s32[512]{0:T(512)S(1)} %iota_add_fusion.1, ...), kind=kOutput, calls=%fused_computation.76 | convolution fusion | flops 813170176 | bytes 5262848 | tf_op jit(solution)/shard_map/dot_general | solution.py:24
  108.2 1.9 %fusion.5 = f32[512]{0:T(512)S(1)} fusion(f32[512,1536]{0,1:T(8,128)S(1)} %get-tuple-element.15, f32[512]{0:T(512)S(1)} %get-tuple-element.14, pred[1536]{0:T(1024)(128)(4,1)S(1)} %broadcast_compare_fusion, s32[1536]{0:T(1024)S(1)} %iota_add_fusion, s32[512]{0:T(512)S(1)} %iota_add_fusion.1, s32[1536]{0:T(1024)S(1)} %convert_reduce_fusion.1, ...), kind=kLoop, calls=%fused_computation.11 | loop fusion | flops 7863808 | bytes 3167744 | tf_op jit(solution)/shard_map/reduce_sum | solution.py:31
  110.1 0.7 slice_bitcast_fusion.8
  110.7 0.0 collective-permute-done.3
  110.7 0.1 select_bitcast_fusion.1
  110.9 0.9 fusion.20
  111.8 0.5 convolution_bitcast_fusion.1
  112.2 0.0 copy-start.9
  112.3 2.0 %multiply_reduce_fusion = (f32[512]{0:T(512)S(1)}, f32[512,512]{0,1:T(8,128)S(1)}) fusion(bf16[512,512]{1,0:T(8,128)(2,1)S(1)} %bitcast.82, bf16[512,512]{1,0:T(8,128)(2,1)} %bitcast.83, bf16[512,512]{1,0:T(8,128)(2,1)S(1)} %copy-done, f32[512,512]{1,0:T(8,128)S(1)} %convolution_bitcast_fusion.1), kind=kOutput, calls=%fused_computation.34 | convolution fusion | flops 538967552 | bytes 3672064 | tf_op jit(solution)/shard_map/dot_general | solution.py:125
  114.3 0.3 copy.33
  114.6 5.4 %fusion.10 = bf16[512,512]{1,0:T(8,128)(2,1)} fusion(bf16[2,1536,512]{2,1,0:T(8,128)(2,1)} %maximum_maximum_fusion, f32[512,1536]{0,1:T(8,128)} %copy-done.3, f32[512]{0:T(512)S(1)} %fusion.5, f32[512]{0:T(512)S(1)} %get-tuple-element.14, f32[512,512]{1,0:T(8,128)S(1)} %copy.33, f32[512]{0:T(512)S(1)} %copy-done.9, f32[512]{0:T(512)S(1)} %add_rsqrt_fusion, ...), kind=kOutput, calls=%fused_computation.27 | convolution fusion | flops 815005696 | bytes 6317568 | tf_op jit(solution)/shard_map/dot_general | solution.py:33
  (23 shorter events, 0.1 us)
Async XLA Ops:
  0.6 103.7 %copy-start = (bf16[512,512]{1,0:T(8,128)(2,1)S(1)}, bf16[512,512]{1,0:T(8,128)(2,1)}, u32[]{:S(2)}) copy-start(bf16[512,512]{1,0:T(8,128)(2,1)} %param.12) | copy-start | bytes 1572868
  0.6 3.5 %copy-start.2 = (bf16[512,512]{1,0:T(8,128)(2,1)S(1)}, bf16[512,512]{1,0:T(8,128)(2,1)}, u32[]{:S(2)}) copy-start(bf16[512,512]{1,0:T(8,128)(2,1)} %param.14) | copy-start | bytes 1572868
  0.7 3.5 %copy-start.4 = (bf16[512,512]{1,0:T(8,128)(2,1)S(1)}, bf16[512,512]{1,0:T(8,128)(2,1)}, u32[]{:S(2)}) copy-start(bf16[512,512]{1,0:T(8,128)(2,1)} %param.20) | copy-start | bytes 1572868
  0.7 3.5 %copy-start.8 = (f32[512]{0:T(512)S(1)}, f32[512]{0:T(512)}, u32[]{:S(2)}) copy-start(f32[512]{0:T(512)} %param.15) | copy-start | bytes 6148
  0.7 4.0 %copy-start.1 = (bf16[512,512]{1,0:T(8,128)(2,1)S(1)}, bf16[512,512]{1,0:T(8,128)(2,1)}, u32[]{:S(2)}) copy-start(bf16[512,512]{1,0:T(8,128)(2,1)} %param.13) | copy-start | bytes 1572868
  11.5 11.0 %collective-permute-start.2 = (bf16[8,96,512]{2,1,0:T(8,128)(2,1)}, bf16[8,96,512]{2,1,0:T(8,128)(2,1)}, u32[]{:S(2)}, u32[]{:S(2)}) collective-permute-start(bf16[8,96,512]{2,1,0:T(8,128)(2,1)} %dynamic-slice_bitcast_fusion), channel_id=1, source_target_pairs={{0,32},{32,0},{64,96},{96,64},{128,160},{160,128},{192,224},{224,1... | collective-permute-start | bytes 2359304 | tf_op jit(solution)/shard_map/ppermute | solution.py:97
  24.7 27.4 %copy-start.5 = (f32[512,32]{0,1:T(8,128)S(1)}, f32[512,32]{0,1:T(8,128)}, u32[]{:S(2)}) copy-start(f32[512,32]{0,1:T(8,128)} %param.23) | copy-start | bytes 196612
  24.7 27.4 %copy-start.6 = (f32[512,32]{0,1:T(8,128)S(1)}, f32[512,32]{0,1:T(8,128)}, u32[]{:S(2)}) copy-start(f32[512,32]{0,1:T(8,128)} %param.22) | copy-start | bytes 196612
  24.7 27.4 %copy-start.7 = (f32[512,32]{0,1:T(8,128)S(1)}, f32[512,32]{0,1:T(8,128)}, u32[]{:S(2)}) copy-start(f32[512,32]{0,1:T(8,128)} %param.21) | copy-start | bytes 196612
  24.7 27.3 %all-to-all-start = ((bf16[8,96,512]{2,1,0:T(8,128)(2,1)}), bf16[8,96,512]{2,1,0:T(8,128)(2,1)S(1)}, u32[]{:S(2)}, u32[]{:S(2)}) async-start(bf16[8,96,512]{2,1,0:T(8,128)(2,1)} %fusion.7), calls=%async_computation | async-start | bytes 1572864 | tf_op jit(solution)/shard_map/all_to_all | solution.py:99
  29.5 27.4 %copy-start.10 = (s32[4]{0:T(128)S(1)}, s32[4]{0:T(128)}, u32[]{:S(2)}) copy-start(s32[4]{0:T(128)} %param.16) | copy-start | bytes 52
  29.5 42.7 %collective-permute-start.1 = (bf16[2,512,512]{2,1,0:T(8,128)(2,1)}, bf16[2,512,512]{2,1,0:T(8,128)(2,1)}, u32[]{:S(2)}, u32[]{:S(2)}) collective-permute-start(bf16[2,512,512]{2,1,0:T(8,128)(2,1)} %pad_maximum_fusion.1), channel_id=1, source_target_pairs={{0,32},{32,64},{64,96},{96,128},{128,160},{160,192},{192,224},{224... | collective-permute-start | bytes 3145736 | tf_op jit(solution)/shard_map/ppermute | solution.py:16
  33.4 56.9 %collective-permute-start = (bf16[2,512,512]{2,1,0:T(8,128)(2,1)}, bf16[2,512,512]{2,1,0:T(8,128)(2,1)}, u32[]{:S(2)}, u32[]{:S(2)}) collective-permute-start(bf16[2,512,512]{2,1,0:T(8,128)(2,1)} %pad_maximum_fusion.1), channel_id=1, source_target_pairs={{0,64},{32,96},{64,128},{96,160},{128,192},{160,224},{192,256},{22... | collective-permute-start | bytes 3145736 | tf_op jit(solution)/shard_map/ppermute | solution.py:16
  53.4 49.0 %all-to-all-start.1 = ((bf16[8,96,512]{2,1,0:T(8,128)(2,1)}), bf16[8,96,512]{2,1,0:T(8,128)(2,1)S(1)}, u32[]{:S(2)}, u32[]{:S(2)}) async-start(bf16[8,96,512]{2,1,0:T(8,128)(2,1)} %broadcast_in_dim.11), calls=%async_computation.1 | async-start | bytes 1572864 | tf_op jit(solution)/shard_map/all_to_all | solution.py:114
  102.4 8.4 %collective-permute-start.3 = (bf16[8,96,512]{2,1,0:T(8,128)(2,1)S(1)}, bf16[8,96,512]{2,1,0:T(8,128)(2,1)S(1)}, u32[]{:S(2)}, u32[]{:S(2)}) collective-permute-start(bf16[8,96,512]{2,1,0:T(8,128)(2,1)S(1)} %all-to-all-done.1), channel_id=1, source_target_pairs={{0,32},{32,0},{64,96},{96,64},{128,160},{160,128},{192,224},{224,1... | collective-permute-start | bytes 2359304 | tf_op jit(solution)/shard_map/ppermute | solution.py:115
  108.1 2.7 %copy-start.3 = (f32[512,1536]{0,1:T(8,128)}, f32[512,1536]{0,1:T(8,128)S(1)}, u32[]{:S(2)}) copy-start(f32[512,1536]{0,1:T(8,128)S(1)} %get-tuple-element.15) | copy-start | bytes 9437188
  112.2 2.4 %copy-start.9 = (f32[512]{0:T(512)S(1)}, f32[512]{0:T(512)}, u32[]{:S(2)}) copy-start(f32[512]{0:T(512)} %param.17) | copy-start | bytes 6148

commit v2 on v1

v2 whole, which is shorter than its diff:
```python
import jax
import jax.numpy as jnp
from jax import lax
from jax.experimental import pallas as pl
from jax.experimental.pallas import tpu as pltpu
from jax.sharding import PartitionSpec as P

WIN = 1024
TOK = 512
CHIPS = 8
COLS = 32
PART = 3 * COLS

momentum_decay = 0.9
step_size = 0.5

PARTNER = [(i, i ^ 1) for i in range(2 * CHIPS)]
NEXT_CHIP = [(i, i + 2) for i in range(2 * CHIPS - 2)]
SAME_CORE = [[c + 2 * k for k in range(CHIPS)] for c in range(2)]

f32 = jnp.float32
bf16 = jnp.bfloat16


def contract(x, y, dims):
    return lax.dot_general(x, y, ((dims[:1], dims[1:]), ((), ())), preferred_element_type=f32)


def grads_kernel(core, keys, values, rates, w_gate, w_up, w_down, mine, other):
    k = keys[...]
    per_token = jnp.broadcast_to(rates[...], (128, TOK)).T
    err = jnp.concatenate(
        [-(per_token * values[:, i : i + 128].astype(f32)) for i in range(0, TOK, 128)], axis=1
    ).astype(bf16)
    gate = contract(k, w_gate[...], (1, 0))
    upper = contract(k, w_up[...], (1, 0))
    back = contract(err, w_down[...], (1, 1))
    sig = jax.nn.sigmoid(gate)
    act = gate * sig
    slope = sig * (1.0 + gate * (1.0 - sig))
    hidden = (act * upper).astype(bf16)
    d_up = (back * act).astype(bf16)
    d_gate = (back * upper * slope).astype(bf16)
    for n, (x, y) in enumerate(((d_gate, k), (d_up, k), (err, hidden))):
        part = contract(x, y, (0, 0)).astype(bf16)
        rows = slice(n * COLS, (n + 1) * COLS)
        halves = [
            [part[(2 * d + c) * COLS : (2 * d + c + 1) * COLS] for d in range(CHIPS)] for c in range(2)
        ]
        for c in range(2):

            @pl.when(core[0] == c)
            def _():
                for d in range(CHIPS):
                    mine[d, rows] = halves[c][d]
                    other[d, rows] = halves[1 - c][d]


BLOCK = 256


def attention_kernel(first, lengths, q, k2, v2, k1, v1, k0, v0, out):
    for b in range(TOK // BLOCK):
        qb = q[b * BLOCK : (b + 1) * BLOCK]
        qpos = first[0] + b * BLOCK + lax.broadcasted_iota(jnp.int32, (BLOCK, 1), 0)
        low = jnp.maximum(qpos - (WIN - 1), 0)
        end = 0
        for n in range(4):
            end = end + lengths[n]
            low = jnp.where(qpos >= end, jnp.maximum(low, end), low)
        pieces = []
        for hop, kref, vref in ((2, k2, v2), (1, k1, v1), (0, k0, v0)):
            lo = max(0, b * BLOCK - WIN + hop * TOK)
            hi = min(TOK, (b + 1) * BLOCK + hop * TOK)
            s = contract(qb, kref[lo:hi], (1, 1)) * (TOK ** (-0.5))
            kpos = first[0] - hop * TOK + lo + lax.broadcasted_iota(jnp.int32, (1, hi - lo), 1)
            s = jnp.where((kpos >= low) & (kpos <= qpos), s, -1e30)
            pieces.append((s, vref[lo:hi]))
        top = pieces[0][0].max(axis=1, keepdims=True)
        for s, _ in pieces[1:]:
            top = jnp.maximum(top, s.max(axis=1, keepdims=True))
        total = 0.0
        acc = 0.0
        for s, v in pieces:
            w = jnp.exp(s - top)
            total = total + w.sum(axis=1, keepdims=True)
            acc = acc + contract(w.astype(bf16), v, (1, 0))
        out[b * BLOCK : (b + 1) * BLOCK] = acc / total


def fast_kernel(core, q, same, swap, attn, gain, out, gate_t, up_t, down_t):
    for side, src in ((core[0], same), (1 - core[0], swap)):
        for d in range(CHIPS):
            at = pl.ds(pl.multiple_of((2 * d + side) * COLS, COLS), COLS)
            for n, dst in enumerate((gate_t, up_t, down_t)):
                dst[at, :] = src[d, n * COLS : (n + 1) * COLS]
    x = q[...]
    qa = contract(x, gate_t[...], (1, 1))
    qb = contract(x, up_t[...], (1, 1))
    qh = (qa * jax.nn.sigmoid(qa) * qb).astype(bf16)
    fast = contract(qh, down_t[...], (1, 1))
    scale = lax.rsqrt(jnp.mean(fast * fast, axis=1, keepdims=True) + 1e-06)
    out[...] = (attn[...] + fast * scale * gain[...]).astype(bf16)


def near_core(x):
    return pltpu.with_memory_space_constraint(x, pltpu.VMEM)


PARAMS = pltpu.CompilerParams(vmem_limit_bytes=24 * 2**20)
SMEM = pl.BlockSpec(memory_space=pltpu.SMEM)
VMEM = pl.BlockSpec(memory_space=pltpu.VMEM)


def local(
    queries,
    keys,
    values,
    rates,
    lengths,
    norm_gain,
    w_gate,
    w_up,
    w_down,
    mom_gate,
    mom_up,
    mom_down,
):
    index = lax.axis_index("seq")
    core = index % 2
    cores = jnp.reshape(core, (1,))
    k2 = lax.ppermute(keys, "seq", NEXT_CHIP)
    v2 = lax.ppermute(values, "seq", NEXT_CHIP)
    piece = jax.ShapeDtypeStruct((CHIPS, PART, TOK), bf16)
    mine, other = pl.pallas_call(
        grads_kernel,
        out_shape=(pltpu.VMEM(piece.shape, bf16),) * 2,
        in_specs=[SMEM] + [VMEM] * 6,
        out_specs=(VMEM, VMEM),
        compiler_params=PARAMS,
    )(cores, keys, values, rates.reshape(1, TOK), w_gate, w_up, w_down)
    got = lax.ppermute(other, "seq", PARTNER)
    both = (mine.astype(f32) + got.astype(f32)).astype(bf16)
    came = lax.all_to_all(both, "seq", 0, 0, axis_index_groups=SAME_CORE)
    near_k = lax.ppermute(jnp.where(core == 0, keys, k2), "seq", PARTNER)
    near_v = lax.ppermute(jnp.where(core == 0, values, v2), "seq", PARTNER)
    attn = pl.pallas_call(
        attention_kernel,
        out_shape=pltpu.VMEM((TOK, TOK), f32),
        in_specs=[SMEM, SMEM] + [VMEM] * 7,
        out_specs=VMEM,
        compiler_params=PARAMS,
    )(
        jnp.reshape(index * TOK, (1,)),
        lengths,
        near_core(queries),
        near_core(k2),
        near_core(v2),
        near_core(near_k),
        near_core(near_v),
        near_core(keys),
        near_core(values),
    )
    scale = float(TOK * lax.axis_size("seq")) ** (-0.5)
    total = jnp.sum(came.astype(f32), axis=0)
    moms = jnp.concatenate((mom_gate.T, mom_up.T, mom_down.T), axis=0)
    weights = jnp.concatenate(
        [lax.dynamic_slice_in_dim(w, index * COLS, COLS, 1).T for w in (w_gate, w_up, w_down)],
        axis=0,
    )
    new_moms = momentum_decay * moms + total * scale
    normed = new_moms * lax.rsqrt(jnp.sum(new_moms * new_moms, axis=1, keepdims=True) + 1e-06)
    shard = (weights.astype(f32) - step_size * normed).astype(bf16)
    spread = jnp.broadcast_to(shard[None], (CHIPS,) + shard.shape)
    same = lax.all_to_all(spread, "seq", 0, 0, axis_index_groups=SAME_CORE)
    swap = lax.ppermute(same, "seq", PARTNER)
    mixed = pl.pallas_call(
        fast_kernel,
        out_shape=jax.ShapeDtypeStruct((TOK, TOK), bf16),
        in_specs=[SMEM] + [VMEM] * 5,
        out_specs=VMEM,
        compiler_params=PARAMS,
        scratch_shapes=[pltpu.VMEM((TOK, TOK), bf16)] * 3,
    )(
        cores,
        near_core(queries),
        near_core(same),
        near_core(swap),
        near_core(attn),
        norm_gain.reshape(1, TOK),
    )
    outs = [new_moms[k * COLS : (k + 1) * COLS].T for k in range(3)]
    return (mixed, *outs)


def solution(mesh):
    in_specs = (
        P(("doc", "seq"), None),
        P(("doc", "seq"), None),
        P(("doc", "seq"), None),
        P(("doc", "seq")),
        P("doc"),
        P("doc"),
        P("doc", None),
        P("doc", None),
        P("doc", None),
        P("doc", "seq"),
        P("doc", "seq"),
        P("doc", "seq"),
    )
    out_specs = (P(("doc", "seq"), None), P("doc", "seq"), P("doc", "seq"), P("doc", "seq"))
    return jax.shard_map(local, mesh=mesh, in_specs=in_specs, out_specs=out_specs, check_vma=False)
```

time: 121 us -> 108 us (0.89)
  matrix products: 20 us -> 0 us
  Pallas kernels: 0 us -> 9.3 us
  other arithmetic: 11.4 us -> 3.15 us
  local copies, waits for them, and re-layouts: 5.4 us -> 10.6 us
  waiting for transfers between devices: 56.4 us -> 51.3 us
  starting transfers between devices: 25.9 us -> 30.8 us
    dot_general x10 -> x0, matrix products: 20 us -> none  [the longest x1 5.43 us: window_attention(): return jnp.dot(probs, vblk, preferred_element_type=jnp.float32)]
    pallas_call x0 -> x3, Pallas kernels: none -> 9.3 us  [the longest x1 3.49 us: local(): pl.pallas_call(attention_kernel, out_shape=pltpu.VMEM((TOK, TOK), f32), i...]
    all_to_all x1, waiting for transfers between devices: 9.07 us -> 0.01 us  [local(): same = lax.all_to_all(spread, 'seq', 0, 0, axis_index_groups=SAME_CORE)]
    all_to_all x1, waiting for transfers between devices: 12.1 us -> 21.1 us  [local(): came = lax.all_to_all(both, 'seq', 0, 0, axis_index_groups=SAME_CORE)]
    unnamed x25 -> x35, local copies, waits for them, and re-layouts: 0.3 us -> 6.83 us
    ppermute x3 -> x5, starting transfers between devices: 9.92 us -> 15 us  [the longest x1 3.73 us: local(): near_k = lax.ppermute(jnp.where(core == 0, keys, k2), 'seq', PARTNER)]
    ppermute x3 -> x5, waiting for transfers between devices: 33 us -> 28.3 us  [the longest x1 21.7 us: local(): k2 = lax.ppermute(keys, 'seq', NEXT_CHIP)]
    concatenate x2 -> x0, other arithmetic: 4.47 us -> none  [the longest x1 2.97 us: local(): buffer = jnp.concatenate(earlier + [paired], axis=1)]
  transfers between devices with their start and end apart: 6 -> 8, of which waited for: 5 -> 5; matrix products, arithmetic and copies ran while one was open for 12% -> 4% of each run, Pallas kernels for 0% -> 3%
where the time goes in v2:
time: 108 us; the launch traced here: 106 us
  waiting for transfers between devices  51.3 us (48%)
  starting transfers between devices  30.8 us (29%)
  local copies, waits for them, and re-layouts  10.6 us (10%)
  Pallas kernels  9.3 us (9%)
  other arithmetic  3.15 us (3%)
    ppermute x1, waiting for transfers between devices, local(): k2 = lax.ppermute(keys, 'seq', NEXT_CHIP)  21.7 us
    all_to_all x1, waiting for transfers between devices, local(): came = lax.all_to_all(both, 'seq', 0, 0, axis_index_groups=SAME_CORE)  21.1 us
    ppermute x1, starting transfers between devices, local(): got = lax.ppermute(other, 'seq', PARTNER)  8.76 us
    unnamed x35, local copies, waits for them, and re-layouts  6.83 us
    ppermute x1, waiting for transfers between devices, local(): v2 = lax.ppermute(values, 'seq', NEXT_CHIP)  4.7 us
    ppermute x1, starting transfers between devices, local(): near_k = lax.ppermute(jnp.where(core == 0, keys, k2), 'seq', PARTNER)  3.73 us
    all_to_all x1, starting transfers between devices, local(): same = lax.all_to_all(spread, 'seq', 0, 0, axis_index_groups=SAME_CORE)  3.55 us
    all_to_all x1, starting transfers between devices, local(): came = lax.all_to_all(both, 'seq', 0, 0, axis_index_groups=SAME_CORE)  3.55 us
  transfers between devices with their start and end apart: 8, of which 5 were waited for; matrix products, arithmetic and copies ran while one was open for 4% of the time, Pallas kernels for 3%

profile of v2, /device:TPU:1, one launch (start us, length us, event | category | flops | bytes accessed | tf_op | source)
XLA Modules:
  0.0 106.1 jit_solution(11404217378230050479)
XLA Ops:
  0.6 0.0 copy-start
  0.7 1.0 copy-done
  1.7 1.0 copy-done.2
  2.7 1.0 copy-done.5
  3.8 1.0 copy-done.6
  4.8 1.0 copy-done.7
  5.9 0.7 copy-done.9
  6.5 2.7 %shard_map.147 = (bf16[8,96,512]{2,1,0:T(8,128)(2,1)S(1)}, bf16[8,96,512]{2,1,0:T(8,128)(2,1)S(1)}) custom-call(s32[1]{0:T(128)} %bitcast.core, bf16[512,512]{1,0:T(8,128)(2,1)S(1)} %copy-done, bf16[512,512]{1,0:T(8,128)(2,1)S(1)} %copy-done.2, f32[1,512]{1,0:T(1,128)S(1)} %bitcast.17, bf16[512,512]{1,0:T(8,128)(2,1)S(1)} %copy-done.5, ...), custom_call_target="tpu_custom_call" | custom-call | tf_op jit(solution)/shard_map/pallas_call | solution.py:135
  9.2 8.8 %collective-permute-start = (bf16[8,96,512]{2,1,0:T(8,128)(2,1)S(1)}, bf16[8,96,512]{2,1,0:T(8,128)(2,1)S(1)}, u32[]{:S(2)}, u32[]{:S(2)}) collective-permute-start(bf16[8,96,512]{2,1,0:T(8,128)(2,1)S(1)} %get-tuple-element.7), channel_id=1, source_target_pairs={{0,32},{32,0},{64,96},{96,64},{128,160},{160,128},{192,224},{224,1... | collective-permute-start | bytes 2359304 | tf_op jit(solution)/shard_map/ppermute | solution.py:142
  18.0 1.9 %collective-permute-done = bf16[8,96,512]{2,1,0:T(8,128)(2,1)S(1)} collective-permute-done((bf16[8,96,512]{2,1,0:T(8,128)(2,1)S(1)}, bf16[8,96,512]{2,1,0:T(8,128)(2,1)S(1)}, u32[]{:S(2)}, u32[]{:S(2)}) %collective-permute-start) | collective-permute-done | bytes 786464 | tf_op jit(solution)/shard_map/ppermute | solution.py:142
  19.9 1.1 %add_convert_fusion = bf16[8,96,512]{2,1,0:T(8,128)(2,1)} fusion(bf16[8,96,512]{2,1,0:T(8,128)(2,1)S(1)} %collective-permute-done, bf16[8,96,512]{2,1,0:T(8,128)(2,1)S(1)} %get-tuple-element.6), kind=kLoop, calls=%fused_computation.1 | loop fusion | flops 1572864 | bytes 2359296 | tf_op jit(solution)/shard_map/convert_element_type | solution.py:143
  21.0 3.5 %all-to-all-start = ((bf16[8,96,512]{2,1,0:T(8,128)(2,1)}), bf16[8,96,512]{2,1,0:T(8,128)(2,1)S(1)}, u32[]{:S(2)}, u32[]{:S(2)}) async-start(bf16[8,96,512]{2,1,0:T(8,128)(2,1)} %add_convert_fusion), calls=%async_computation | async-start | bytes 1572864 | tf_op jit(solution)/shard_map/all_to_all | solution.py:144
  24.5 1.0 constant_dynamic-slice_fusion.2
  25.5 0.0 copy-start.13
  25.6 0.0 copy-start.14
  25.6 0.0 copy-start.15
  25.6 0.1 copy.19
  25.7 1.1 %constant_dynamic-slice_fusion = (bf16[512,32]{1,0:T(8,128)(2,1)S(1)}, bf16[512,32]{1,0:T(8,128)(2,1)S(1)}) fusion(bf16[512,512]{1,0:T(8,128)(2,1)} %w_down.1, s32[]{:T(128)S(6)} %select_n.25, bf16[512,512]{1,0:T(8,128)(2,1)} %w_up.1), kind=kLoop, calls=%fused_computation.11 | loop fusion | bytes 131076 | tf_op jit(solution)/shard_map/dynamic_slice | solution.py:168
  26.8 0.1 copy.21
  26.9 0.1 copy.20
  27.0 21.1 %all-to-all-done = bf16[8,96,512]{2,1,0:T(8,128)(2,1)S(1)} async-done(((bf16[8,96,512]{2,1,0:T(8,128)(2,1)}), bf16[8,96,512]{2,1,0:T(8,128)(2,1)S(1)}, u32[]{:S(2)}, u32[]{:S(2)}) %all-to-all-start) | async-done | bytes 786464 | tf_op jit(solution)/shard_map/all_to_all | solution.py:144
  48.1 0.1 convert_reduce_fusion
  48.2 0.0 copy-done.13
  48.2 0.0 copy-done.14
  48.2 0.1 multiply_reduce_fusion
  48.4 0.7 copy-done.11
  49.0 0.1 subtract_convert_fusion
  49.1 0.0 copy-start.1
  49.1 0.0 copy-start.3
  49.1 0.9 broadcast_in_dim.2
  50.1 3.5 %all-to-all-start.1 = ((bf16[8,96,512]{2,1,0:T(8,128)(2,1)}), bf16[8,96,512]{2,1,0:T(8,128)(2,1)S(1)}, u32[]{:S(2)}, u32[]{:S(2)}) async-start(bf16[8,96,512]{2,1,0:T(8,128)(2,1)} %broadcast_in_dim.2), calls=%async_computation.1 | async-start | bytes 1572864 | tf_op jit(solution)/shard_map/all_to_all | solution.py:175
  53.6 0.0 copy-done.1
  53.6 3.3 %collective-permute-start.2 = (bf16[512,512]{1,0:T(8,128)(2,1)S(1)}, bf16[512,512]{1,0:T(8,128)(2,1)S(1)}, u32[]{:S(2)}, u32[]{:S(2)}) collective-permute-start(bf16[512,512]{1,0:T(8,128)(2,1)S(1)} %copy-done.1), channel_id=1, source_target_pairs={{0,64},{32,96},{64,128},{96,160},{128,192},{160,224},{192,256},{22... | collective-permute-start | bytes 1572872 | tf_op jit(solution)/shard_map/ppermute | solution.py:132
  56.9 3.1 %collective-permute-start.3 = (bf16[512,512]{1,0:T(8,128)(2,1)S(1)}, bf16[512,512]{1,0:T(8,128)(2,1)S(1)}, u32[]{:S(2)}, u32[]{:S(2)}) collective-permute-start(bf16[512,512]{1,0:T(8,128)(2,1)S(1)} %copy-done.3), channel_id=1, source_target_pairs={{0,64},{32,96},{64,128},{96,160},{128,192},{160,224},{192,256},{22... | collective-permute-start | bytes 1572872 | tf_op jit(solution)/shard_map/ppermute | solution.py:133
  60.1 21.7 %collective-permute-done.2.k2 = bf16[512,512]{1,0:T(8,128)(2,1)S(1)} collective-permute-done((bf16[512,512]{1,0:T(8,128)(2,1)S(1)}, bf16[512,512]{1,0:T(8,128)(2,1)S(1)}, u32[]{:S(2)}, u32[]{:S(2)}) %collective-permute-start.2) | collective-permute-done | bytes 524320 | tf_op jit(solution)/shard_map/ppermute | solution.py:132
  81.8 0.8 broadcast_select_fusion.1
  82.6 3.7 %collective-permute-start.4 = (bf16[512,512]{1,0:T(8,128)(2,1)}, bf16[512,512]{1,0:T(8,128)(2,1)}, u32[]{:S(2)}, u32[]{:S(2)}) collective-permute-start(bf16[512,512]{1,0:T(8,128)(2,1)} %broadcast_select_fusion.1), channel_id=1, source_target_pairs={{0,32},{32,0},{64,96},{96,64},{128,160},{160,128},{192,224},{224,1... | collective-permute-start | bytes 1572872 | tf_op jit(solution)/shard_map/ppermute | solution.py:145
  86.4 0.0 all-to-all-done.1.same
  86.4 1.9 %collective-permute-start.1 = (bf16[8,96,512]{2,1,0:T(8,128)(2,1)S(1)}, bf16[8,96,512]{2,1,0:T(8,128)(2,1)}, u32[]{:S(2)}, u32[]{:S(2)}) collective-permute-start(bf16[8,96,512]{2,1,0:T(8,128)(2,1)S(1)} %all-to-all-done.1.same), channel_id=1, source_target_pairs={{0,32},{32,0},{64,96},{96,64},{128,160},{160,128},{192,224},{224,1... | collective-permute-start | bytes 2359304 | tf_op jit(solution)/shard_map/ppermute | solution.py:176
  88.3 4.7 %collective-permute-done.3.v2 = bf16[512,512]{1,0:T(8,128)(2,1)S(1)} collective-permute-done((bf16[512,512]{1,0:T(8,128)(2,1)S(1)}, bf16[512,512]{1,0:T(8,128)(2,1)S(1)}, u32[]{:S(2)}, u32[]{:S(2)}) %collective-permute-start.3) | collective-permute-done | bytes 524320 | tf_op jit(solution)/shard_map/ppermute | solution.py:133
  93.0 0.9 broadcast_select_fusion
  93.9 2.9 %collective-permute-start.5 = (bf16[512,512]{1,0:T(8,128)(2,1)}, bf16[512,512]{1,0:T(8,128)(2,1)}, u32[]{:S(2)}, u32[]{:S(2)}) collective-permute-start(bf16[512,512]{1,0:T(8,128)(2,1)} %broadcast_select_fusion), channel_id=1, source_target_pairs={{0,32},{32,0},{64,96},{96,64},{128,160},{160,128},{192,224},{224,1... | collective-permute-start | bytes 1572872 | tf_op jit(solution)/shard_map/ppermute | solution.py:146
  96.8 0.0 collective-permute-done.4.k1
  96.9 1.8 %collective-permute-done.5.v1 = bf16[512,512]{1,0:T(8,128)(2,1)} collective-permute-done((bf16[512,512]{1,0:T(8,128)(2,1)}, bf16[512,512]{1,0:T(8,128)(2,1)}, u32[]{:S(2)}, u32[]{:S(2)}) %collective-permute-start.5) | collective-permute-done | bytes 524320 | tf_op jit(solution)/shard_map/ppermute | solution.py:146
  98.7 3.5 %shard_map.148.attn = f32[512,512]{1,0:T(8,128)S(1)} custom-call(s32[1]{0:T(128)} %bitcast.8.first, s32[4]{0:T(128)S(1)} %copy-done.10, bf16[512,512]{1,0:T(8,128)(2,1)S(1)} %copy-done.4, bf16[512,512]{1,0:T(8,128)(2,1)S(1)} %collective-permute-done.2.k2, bf16[512,512]{1,0:T(8,128)(2,1)S(1)} %collective-permute-done.3.v2, ...), custom_call_target="tpu_custom_call" | custom-call | tf_op jit(solution)/shard_map/pallas_call | solution.py:147
  102.2 0.7 slice_bitcast_fusion
  102.9 0.0 collective-permute-done.1.swap
  102.9 3.2 %shard_map.149 = bf16[512,512]{1,0:T(8,128)(2,1)} custom-call(s32[1]{0:T(128)} %bitcast.core, bf16[512,512]{1,0:T(8,128)(2,1)S(1)} %copy-done.4, bf16[8,96,512]{2,1,0:T(8,128)(2,1)S(1)} %all-to-all-done.1.same, bf16[8,96,512]{2,1,0:T(8,128)(2,1)} %collective-permute-done.1.swap, f32[512,512]{1,0:T(8,128)S(1)} %shard_map.148.attn, f32[1,512]{1,0:T(1,128)S(1)} %bitcast.16), custom_call_target="tpu_custom_call" | custom-call | tf_op jit(solution)/shard_map/pallas_call | solution.py:177
  (17 shorter events, 0.0 us)
Async XLA Ops:
  0.6 1.0 copy-start
  1.7 1.0 copy-start.2
  2.7 1.0 copy-start.5
  3.8 1.0 copy-start.6
  4.8 1.0 copy-start.7
  5.9 0.7 copy-start.9
  9.2 10.7 %collective-permute-start = (bf16[8,96,512]{2,1,0:T(8,128)(2,1)S(1)}, bf16[8,96,512]{2,1,0:T(8,128)(2,1)S(1)}, u32[]{:S(2)}, u32[]{:S(2)}) collective-permute-start(bf16[8,96,512]{2,1,0:T(8,128)(2,1)S(1)} %get-tuple-element.7), channel_id=1, source_target_pairs={{0,32},{32,0},{64,96},{96,64},{128,160},{160,128},{192,224},{224,1... | collective-permute-start | bytes 2359304 | tf_op jit(solution)/shard_map/ppermute | solution.py:142
  21.0 27.1 %all-to-all-start = ((bf16[8,96,512]{2,1,0:T(8,128)(2,1)}), bf16[8,96,512]{2,1,0:T(8,128)(2,1)S(1)}, u32[]{:S(2)}, u32[]{:S(2)}) async-start(bf16[8,96,512]{2,1,0:T(8,128)(2,1)} %add_convert_fusion), calls=%async_computation | async-start | bytes 1572864 | tf_op jit(solution)/shard_map/all_to_all | solution.py:144
  25.5 22.6 %copy-start.13 = (f32[512,32]{0,1:T(8,128)S(1)}, f32[512,32]{0,1:T(8,128)}, u32[]{:S(2)}) copy-start(f32[512,32]{0,1:T(8,128)} %param.23) | copy-start | bytes 196612
  25.6 22.6 %copy-start.14 = (f32[512,32]{0,1:T(8,128)S(1)}, f32[512,32]{0,1:T(8,128)}, u32[]{:S(2)}) copy-start(f32[512,32]{0,1:T(8,128)} %param.22) | copy-start | bytes 196612
  25.6 22.6 %copy-start.15 = (f32[512,32]{0,1:T(8,128)S(1)}, f32[512,32]{0,1:T(8,128)}, u32[]{:S(2)}) copy-start(f32[512,32]{0,1:T(8,128)} %param.21) | copy-start | bytes 196612
  48.3 0.7 copy-start.11
  49.1 4.5 %copy-start.1 = (bf16[512,512]{1,0:T(8,128)(2,1)S(1)}, bf16[512,512]{1,0:T(8,128)(2,1)}, u32[]{:S(2)}) copy-start(bf16[512,512]{1,0:T(8,128)(2,1)} %k0.1) | copy-start | bytes 1572868
  49.1 7.8 %copy-start.3 = (bf16[512,512]{1,0:T(8,128)(2,1)S(1)}, bf16[512,512]{1,0:T(8,128)(2,1)}, u32[]{:S(2)}) copy-start(bf16[512,512]{1,0:T(8,128)(2,1)} %v0.1) | copy-start | bytes 1572868
  50.1 36.3 %all-to-all-start.1 = ((bf16[8,96,512]{2,1,0:T(8,128)(2,1)}), bf16[8,96,512]{2,1,0:T(8,128)(2,1)S(1)}, u32[]{:S(2)}, u32[]{:S(2)}) async-start(bf16[8,96,512]{2,1,0:T(8,128)(2,1)} %broadcast_in_dim.2), calls=%async_computation.1 | async-start | bytes 1572864 | tf_op jit(solution)/shard_map/all_to_all | solution.py:175
  53.6 28.1 %collective-permute-start.2 = (bf16[512,512]{1,0:T(8,128)(2,1)S(1)}, bf16[512,512]{1,0:T(8,128)(2,1)S(1)}, u32[]{:S(2)}, u32[]{:S(2)}) collective-permute-start(bf16[512,512]{1,0:T(8,128)(2,1)S(1)} %copy-done.1), channel_id=1, source_target_pairs={{0,64},{32,96},{64,128},{96,160},{128,192},{160,224},{192,256},{22... | collective-permute-start | bytes 1572872 | tf_op jit(solution)/shard_map/ppermute | solution.py:132
  56.9 36.1 %collective-permute-start.3 = (bf16[512,512]{1,0:T(8,128)(2,1)S(1)}, bf16[512,512]{1,0:T(8,128)(2,1)S(1)}, u32[]{:S(2)}, u32[]{:S(2)}) collective-permute-start(bf16[512,512]{1,0:T(8,128)(2,1)S(1)} %copy-done.3), channel_id=1, source_target_pairs={{0,64},{32,96},{64,128},{96,160},{128,192},{160,224},{192,256},{22... | collective-permute-start | bytes 1572872 | tf_op jit(solution)/shard_map/ppermute | solution.py:133
  82.6 16.1 %copy-start.4 = (bf16[512,512]{1,0:T(8,128)(2,1)S(1)}, bf16[512,512]{1,0:T(8,128)(2,1)}, u32[]{:S(2)}) copy-start(bf16[512,512]{1,0:T(8,128)(2,1)} %q.3) | copy-start | bytes 1572868
  82.6 16.1 %copy-start.10 = (s32[4]{0:T(128)S(1)}, s32[4]{0:T(128)}, u32[]{:S(2)}) copy-start(s32[4]{0:T(128)} %lengths.1) | copy-start | bytes 52
  82.6 14.2 %collective-permute-start.4 = (bf16[512,512]{1,0:T(8,128)(2,1)}, bf16[512,512]{1,0:T(8,128)(2,1)}, u32[]{:S(2)}, u32[]{:S(2)}) collective-permute-start(bf16[512,512]{1,0:T(8,128)(2,1)} %broadcast_select_fusion.1), channel_id=1, source_target_pairs={{0,32},{32,0},{64,96},{96,64},{128,160},{160,128},{192,224},{224,1... | collective-permute-start | bytes 1572872 | tf_op jit(solution)/shard_map/ppermute | solution.py:145
  86.4 16.5 %collective-permute-start.1 = (bf16[8,96,512]{2,1,0:T(8,128)(2,1)S(1)}, bf16[8,96,512]{2,1,0:T(8,128)(2,1)}, u32[]{:S(2)}, u32[]{:S(2)}) collective-permute-start(bf16[8,96,512]{2,1,0:T(8,128)(2,1)S(1)} %all-to-all-done.1.same), channel_id=1, source_target_pairs={{0,32},{32,0},{64,96},{96,64},{128,160},{160,128},{192,224},{224,1... | collective-permute-start | bytes 2359304 | tf_op jit(solution)/shard_map/ppermute | solution.py:176
  93.9 4.8 %collective-permute-start.5 = (bf16[512,512]{1,0:T(8,128)(2,1)}, bf16[512,512]{1,0:T(8,128)(2,1)}, u32[]{:S(2)}, u32[]{:S(2)}) collective-permute-start(bf16[512,512]{1,0:T(8,128)(2,1)} %broadcast_select_fusion), channel_id=1, source_target_pairs={{0,32},{32,0},{64,96},{96,64},{128,160},{160,128},{192,224},{224,1... | collective-permute-start | bytes 1572872 | tf_op jit(solution)/shard_map/ppermute | solution.py:146
  98.7 3.5 %copy-start.12 = (f32[96,512]{1,0:T(8,128)S(1)}, f32[96,512]{1,0:T(8,128)}, u32[]{:S(2)}) copy-start(f32[96,512]{1,0:T(8,128)} %copy-done.11) | copy-start | bytes 589828
  98.7 4.2 %copy-start.8 = (f32[512]{0:T(512)S(1)}, f32[512]{0:T(512)}, u32[]{:S(2)}) copy-start(f32[512]{0:T(512)} %param.17) | copy-start | bytes 6148

commit v3 on v2

--- a/solution.py
+++ b/solution.py
@@ -10,6 +10,7 @@
 CHIPS = 8
 COLS = 32
 PART = 3 * COLS
+GRAD_SCALE = float(2 * CHIPS * TOK) ** (-0.5)
 
 momentum_decay = 0.9
 step_size = 0.5
@@ -26,15 +27,28 @@
     return lax.dot_general(x, y, ((dims[:1], dims[1:]), ((), ())), preferred_element_type=f32)
 
 
-def grads_kernel(core, keys, values, rates, w_gate, w_up, w_down, mine, other):
-    k = keys[...]
+def grads_kernel(core, keys, values, rates, w_gate, w_up, w_down, mine, other, *refs):
+    bufs, sems = refs[:5], refs[5]
+    copies = [
+        pltpu.make_async_copy(src, dst, sems.at[n])
+        for n, (src, dst) in enumerate(zip((keys, w_gate, values, w_up, w_down), bufs))
+    ]
+    for copy in copies:
+        copy.start()
+    k_buf, gate_buf, v_buf, up_buf, down_buf = bufs
     per_token = jnp.broadcast_to(rates[...], (128, TOK)).T
+    copies[0].wait()
+    copies[1].wait()
+    k = k_buf[...]
+    gate = contract(k, gate_buf[...], (1, 0))
+    copies[2].wait()
     err = jnp.concatenate(
-        [-(per_token * values[:, i : i + 128].astype(f32)) for i in range(0, TOK, 128)], axis=1
+        [-(per_token * v_buf[:, i : i + 128].astype(f32)) for i in range(0, TOK, 128)], axis=1
     ).astype(bf16)
-    gate = contract(k, w_gate[...], (1, 0))
-    upper = contract(k, w_up[...], (1, 0))
-    back = contract(err, w_down[...], (1, 1))
+    copies[3].wait()
+    upper = contract(k, up_buf[...], (1, 0))
+    copies[4].wait()
+    back = contract(err, down_buf[...], (1, 1))
     sig = jax.nn.sigmoid(gate)
     act = gate * sig
     slope = sig * (1.0 + gate * (1.0 - sig))
@@ -56,10 +70,38 @@
                     other[d, rows] = halves[1 - c][d]
 
 
+def pair_kernel(mine, got, out):
+    for d in range(CHIPS):
+        out[d] = (mine[d].astype(f32) + got[d].astype(f32)).astype(bf16)
+
+
+def update_kernel(came, *refs):
+    weights, moms, news, spread = refs[0], refs[1:4], refs[4:7], refs[7]
+    bufs, sems = refs[8:11], refs[11]
+    copies = [pltpu.make_async_copy(moms[n], bufs[n], sems.at[n]) for n in range(3)]
+    for copy in copies:
+        copy.start()
+    for n in range(3):
+        rows = slice(n * COLS, (n + 1) * COLS)
+        total = came[0, rows].astype(f32)
+        for d in range(1, CHIPS):
+            total = total + came[d, rows].astype(f32)
+        copies[n].wait()
+        new = momentum_decay * bufs[n][...] + total * GRAD_SCALE
+        news[n][...] = new
+        normed = new * lax.rsqrt(jnp.sum(new * new, axis=1, keepdims=True) + 1e-06)
+        shard = (weights[rows].astype(f32) - step_size * normed).astype(bf16)
+        for d in range(CHIPS):
+            spread[d, rows] = shard
+
+
 BLOCK = 256
 
 
-def attention_kernel(first, lengths, q, k2, v2, k1, v1, k0, v0, out):
+def attention_kernel(
+    first, lengths, q, k2, v2, k1, v1, k0, v0, weights, out, out_weights
+):
+    out_weights[...] = weights[...]
     for b in range(TOK // BLOCK):
         qb = q[b * BLOCK : (b + 1) * BLOCK]
         qpos = first[0] + b * BLOCK + lax.broadcasted_iota(jnp.int32, (BLOCK, 1), 0)
@@ -107,9 +149,14 @@
     return pltpu.with_memory_space_constraint(x, pltpu.VMEM)
 
 
+def far(x):
+    return pltpu.with_memory_space_constraint(x, pltpu.HBM)
+
+
 PARAMS = pltpu.CompilerParams(vmem_limit_bytes=24 * 2**20)
 SMEM = pl.BlockSpec(memory_space=pltpu.SMEM)
 VMEM = pl.BlockSpec(memory_space=pltpu.VMEM)
+HBM = pl.BlockSpec(memory_space=pltpu.HBM)
 
 
 def local(
@@ -135,20 +182,32 @@
     mine, other = pl.pallas_call(
         grads_kernel,
         out_shape=(pltpu.VMEM(piece.shape, bf16),) * 2,
-        in_specs=[SMEM] + [VMEM] * 6,
+        in_specs=[SMEM, HBM, HBM, VMEM, HBM, HBM, HBM],
         out_specs=(VMEM, VMEM),
-        compiler_params=PARAMS,
-    )(cores, keys, values, rates.reshape(1, TOK), w_gate, w_up, w_down)
+        scratch_shapes=[pltpu.VMEM((TOK, TOK), bf16)] * 5 + [pltpu.SemaphoreType.DMA((5,))],
+        compiler_params=PARAMS,
+    )(cores, far(keys), far(values), rates.reshape(1, TOK), far(w_gate), far(w_up), far(w_down))
     got = lax.ppermute(other, "seq", PARTNER)
-    both = (mine.astype(f32) + got.astype(f32)).astype(bf16)
+    both = pl.pallas_call(
+        pair_kernel,
+        out_shape=pltpu.VMEM(piece.shape, bf16),
+        in_specs=[VMEM] * 2,
+        out_specs=VMEM,
+        compiler_params=PARAMS,
+    )(near_core(mine), near_core(got))
     came = lax.all_to_all(both, "seq", 0, 0, axis_index_groups=SAME_CORE)
     near_k = lax.ppermute(jnp.where(core == 0, keys, k2), "seq", PARTNER)
     near_v = lax.ppermute(jnp.where(core == 0, values, v2), "seq", PARTNER)
-    attn = pl.pallas_call(
+    weights = [lax.dynamic_slice_in_dim(w, index * COLS, COLS, 1) for w in (w_gate, w_up, w_down)]
+    weights = jnp.concatenate(weights, axis=1).T
+    attn, weights = pl.pallas_call(
         attention_kernel,
-        out_shape=pltpu.VMEM((TOK, TOK), f32),
-        in_specs=[SMEM, SMEM] + [VMEM] * 7,
-        out_specs=VMEM,
+        out_shape=(
+            jax.ShapeDtypeStruct((TOK, TOK), f32),
+            pltpu.VMEM((PART, TOK), bf16),
+        ),
+        in_specs=[SMEM, SMEM] + [VMEM] * 8,
+        out_specs=(VMEM,) * 2,
         compiler_params=PARAMS,
     )(
         jnp.reshape(index * TOK, (1,)),
@@ -160,18 +219,16 @@
         near_core(near_v),
         near_core(keys),
         near_core(values),
+        weights,
     )
-    scale = float(TOK * lax.axis_size("seq")) ** (-0.5)
-    total = jnp.sum(came.astype(f32), axis=0)
-    moms = jnp.concatenate((mom_gate.T, mom_up.T, mom_down.T), axis=0)
-    weights = jnp.concatenate(
-        [lax.dynamic_slice_in_dim(w, index * COLS, COLS, 1).T for w in (w_gate, w_up, w_down)],
-        axis=0,
-    )
-    new_moms = momentum_decay * moms + total * scale
-    normed = new_moms * lax.rsqrt(jnp.sum(new_moms * new_moms, axis=1, keepdims=True) + 1e-06)
-    shard = (weights.astype(f32) - step_size * normed).astype(bf16)
-    spread = jnp.broadcast_to(shard[None], (CHIPS,) + shard.shape)
+    *news, spread = pl.pallas_call(
+        update_kernel,
+        out_shape=(jax.ShapeDtypeStruct((COLS, TOK), f32),) * 3 + (pltpu.VMEM(piece.shape, bf16),),
+        in_specs=[VMEM] * 2 + [HBM] * 3,
+        out_specs=(VMEM,) * 4,
+        scratch_shapes=[pltpu.VMEM((COLS, TOK), f32)] * 3 + [pltpu.SemaphoreType.DMA((3,))],
+        compiler_params=PARAMS,
+    )(near_core(came), near_core(weights), far(mom_gate.T), far(mom_up.T), far(mom_down.T))
     same = lax.all_to_all(spread, "seq", 0, 0, axis_index_groups=SAME_CORE)
     swap = lax.ppermute(same, "seq", PARTNER)
     mixed = pl.pallas_call(
@@ -189,8 +246,7 @@
         near_core(attn),
         norm_gain.reshape(1, TOK),
     )
-    outs = [new_moms[k * COLS : (k + 1) * COLS].T for k in range(3)]
-    return (mixed, *outs)
+    return (mixed, *[new.T for new in news])
 
 
 def solution(mesh):

time: 108 us -> 108 us (level); the launches traced: 106 us -> 108 us
  blocking collectives: 0 us -> 29 us
  waiting for transfers between devices: 51.3 us -> 28.8 us
  starting transfers between devices: 30.8 us -> 25.7 us
  Pallas kernels: 9.3 us -> 12.9 us
  local copies, waits for them, and re-layouts: 10.6 us -> 8.1 us
    all_to_all x0 -> x1, blocking collectives: none -> 29 us  [local(): same = lax.all_to_all(spread, 'seq', 0, 0, axis_index_groups=SAME_CORE)]
    all_to_all x1, waiting for transfers between devices: 21.1 us -> 0.01 us  [local(): came = lax.all_to_all(both, 'seq', 0, 0, axis_index_groups=SAME_CORE)]
    ppermute x1, waiting for transfers between devices: 21.7 us -> 7.56 us  [local(): k2 = lax.ppermute(keys, 'seq', NEXT_CHIP)]
    ppermute x1, waiting for transfers between devices: 4.7 us -> 18.8 us  [local(): v2 = lax.ppermute(values, 'seq', NEXT_CHIP)]
    all_to_all x1 -> x0, starting transfers between devices: 3.55 us -> none  [local(): same = lax.all_to_all(spread, 'seq', 0, 0, axis_index_groups=SAME_CORE)]
    pallas_call x1 -> x3, Pallas kernels: 3.49 us -> 6.38 us  [the longest x1 3.45 us: local(): pl.pallas_call(attention_kernel, out_shape=(jax.ShapeDtypeStruct((TOK, TO...]
    ppermute x1, starting transfers between devices: 3.28 us -> 1.32 us  [local(): k2 = lax.ppermute(keys, 'seq', NEXT_CHIP)]
    ppermute x1, waiting for transfers between devices: 0.01 us -> 1.89 us  [local(): swap = lax.ppermute(same, 'seq', PARTNER)]
  transfers between devices with their start and end apart: 8 -> 7, of which waited for: 5 -> 4; matrix products, arithmetic and copies ran while one was open for 4% -> 8% of each run, Pallas kernels for 3% -> 4%
where the time goes in v3:
time: 108 us
  blocking collectives  29 us (27%)
  waiting for transfers between devices  28.8 us (27%)
  starting transfers between devices  25.7 us (24%)
  Pallas kernels  12.9 us (12%)
  local copies, waits for them, and re-layouts  8.1 us (8%)
  other arithmetic  2.5 us (2%)
    all_to_all x1, blocking collectives, local(): same = lax.all_to_all(spread, 'seq', 0, 0, axis_index_groups=SAME_CORE)  29 us
    ppermute x1, waiting for transfers between devices, local(): v2 = lax.ppermute(values, 'seq', NEXT_CHIP)  18.8 us
    ppermute x1, starting transfers between devices, local(): got = lax.ppermute(other, 'seq', PARTNER)  8.75 us
    ppermute x1, waiting for transfers between devices, local(): k2 = lax.ppermute(keys, 'seq', NEXT_CHIP)  7.56 us
    unnamed x19, local copies, waits for them, and re-layouts  5.29 us
    pallas_call x1, Pallas kernels, local(): pl.pallas_call(grads_kernel, out_shape=(pltpu.VMEM(piece.shape, bf16),) *...  4.48 us
    ppermute x1, starting transfers between devices, local(): near_k = lax.ppermute(jnp.where(core == 0, keys, k2), 'seq', PARTNER)  3.7 us
    all_to_all x1, starting transfers between devices, local(): came = lax.all_to_all(both, 'seq', 0, 0, axis_index_groups=SAME_CORE)  3.68 us
  transfers between devices with their start and end apart: 7, of which 4 were waited for; matrix products, arithmetic and copies ran while one was open for 8% of the time, Pallas kernels for 4%

profile of v3, /device:TPU:1, one launch (start us, length us, event | category | flops | bytes accessed | tf_op | source)
XLA Modules:
  0.0 107.9 jit_solution(6759644415683787193)
XLA Ops:
  0.6 0.0 copy-start.6
  0.7 0.7 copy-done.6
  1.3 0.0 copy-start
  1.3 4.5 %shard_map.147 = (bf16[8,96,512]{2,1,0:T(8,128)(2,1)S(1)}, bf16[8,96,512]{2,1,0:T(8,128)(2,1)S(1)}) custom-call(s32[1]{0:T(128)} %bitcast.core, bf16[512,512]{1,0:T(8,128)(2,1)} %k0.1, bf16[512,512]{1,0:T(8,128)(2,1)} %v0.1, f32[1,512]{1,0:T(1,128)S(1)} %bitcast.13, bf16[512,512]{1,0:T(8,128)(2,1)} %w_gate.1, bf16[512,512]{1,0:T(8,128)(2,1)} %w_up.1, ...), custom_call_target="tpu_custom_call" | custom-call | tf_op jit(solution)/shard_map/pallas_call | solution.py:182
  5.8 8.8 %collective-permute-start = (bf16[8,96,512]{2,1,0:T(8,128)(2,1)S(1)}, bf16[8,96,512]{2,1,0:T(8,128)(2,1)S(1)}, u32[]{:S(2)}, u32[]{:S(2)}) collective-permute-start(bf16[8,96,512]{2,1,0:T(8,128)(2,1)S(1)} %get-tuple-element.13), channel_id=1, source_target_pairs={{0,32},{32,0},{64,96},{96,64},{128,160},{160,128},{192,224},{224,1... | collective-permute-start | bytes 2359304 | tf_op jit(solution)/shard_map/ppermute | solution.py:190
  14.6 0.0 copy-done
  14.6 1.3 %collective-permute-start.1 = (bf16[512,512]{1,0:T(8,128)(2,1)S(1)}, bf16[512,512]{1,0:T(8,128)(2,1)S(1)}, u32[]{:S(2)}, u32[]{:S(2)}) collective-permute-start(bf16[512,512]{1,0:T(8,128)(2,1)S(1)} %copy-done), channel_id=1, source_target_pairs={{0,64},{32,96},{64,128},{96,160},{128,192},{160,224},{192,256},{22... | collective-permute-start | bytes 1572872 | tf_op jit(solution)/shard_map/ppermute | solution.py:179
  15.9 0.5 collective-permute-done.got
  16.5 1.1 %shard_map.148 = bf16[8,96,512]{2,1,0:T(8,128)(2,1)} custom-call(bf16[8,96,512]{2,1,0:T(8,128)(2,1)S(1)} %get-tuple-element.12.mine, bf16[8,96,512]{2,1,0:T(8,128)(2,1)S(1)} %collective-permute-done.got), custom_call_target="tpu_custom_call" | custom-call | tf_op jit(solution)/shard_map/pallas_call | solution.py:191
  17.6 0.0 copy-start.1
  17.6 3.7 %all-to-all-start = ((bf16[8,96,512]{2,1,0:T(8,128)(2,1)}), bf16[8,96,512]{2,1,0:T(8,128)(2,1)S(1)}, u32[]{:S(2)}, u32[]{:S(2)}) async-start(bf16[8,96,512]{2,1,0:T(8,128)(2,1)} %shard_map.148), calls=%async_computation | async-start | bytes 1572864 | tf_op jit(solution)/shard_map/all_to_all | solution.py:198
  21.3 0.0 copy-done.1
  21.3 3.3 %collective-permute-start.2 = (bf16[512,512]{1,0:T(8,128)(2,1)S(1)}, bf16[512,512]{1,0:T(8,128)(2,1)S(1)}, u32[]{:S(2)}, u32[]{:S(2)}) collective-permute-start(bf16[512,512]{1,0:T(8,128)(2,1)S(1)} %copy-done.1), channel_id=1, source_target_pairs={{0,64},{32,96},{64,128},{96,160},{128,192},{160,224},{192,256},{22... | collective-permute-start | bytes 1572872 | tf_op jit(solution)/shard_map/ppermute | solution.py:180
  24.6 7.6 %collective-permute-done.1.k2 = bf16[512,512]{1,0:T(8,128)(2,1)S(1)} collective-permute-done((bf16[512,512]{1,0:T(8,128)(2,1)S(1)}, bf16[512,512]{1,0:T(8,128)(2,1)S(1)}, u32[]{:S(2)}, u32[]{:S(2)}) %collective-permute-start.1) | collective-permute-done | bytes 524320 | tf_op jit(solution)/shard_map/ppermute | solution.py:179
  32.1 0.8 broadcast_select_fusion.1
  33.0 3.7 %collective-permute-start.3 = (bf16[512,512]{1,0:T(8,128)(2,1)}, bf16[512,512]{1,0:T(8,128)(2,1)}, u32[]{:S(2)}, u32[]{:S(2)}) collective-permute-start(bf16[512,512]{1,0:T(8,128)(2,1)} %broadcast_select_fusion.1), channel_id=1, source_target_pairs={{0,32},{32,0},{64,96},{96,64},{128,160},{160,128},{192,224},{224,1... | collective-permute-start | bytes 1572872 | tf_op jit(solution)/shard_map/ppermute | solution.py:199
  36.7 18.8 %collective-permute-done.2.v2 = bf16[512,512]{1,0:T(8,128)(2,1)S(1)} collective-permute-done((bf16[512,512]{1,0:T(8,128)(2,1)S(1)}, bf16[512,512]{1,0:T(8,128)(2,1)S(1)}, u32[]{:S(2)}, u32[]{:S(2)}) %collective-permute-start.2) | collective-permute-done | bytes 524320 | tf_op jit(solution)/shard_map/ppermute | solution.py:180
  55.5 0.9 broadcast_select_fusion
  56.4 2.5 %collective-permute-start.4 = (bf16[512,512]{1,0:T(8,128)(2,1)}, bf16[512,512]{1,0:T(8,128)(2,1)}, u32[]{:S(2)}, u32[]{:S(2)}) collective-permute-start(bf16[512,512]{1,0:T(8,128)(2,1)} %broadcast_select_fusion), channel_id=1, source_target_pairs={{0,32},{32,0},{64,96},{96,64},{128,160},{160,128},{192,224},{224,1... | collective-permute-start | bytes 1572872 | tf_op jit(solution)/shard_map/ppermute | solution.py:200
  58.9 1.0 constant_dynamic-slice_fusion.2
  59.9 0.7 copy.19
  60.6 0.0 copy-start.2
  60.6 1.8 %constant_dynamic-slice_fusion = (bf16[512,32]{1,0:T(8,128)(2,1)}, bf16[512,32]{1,0:T(8,128)(2,1)S(1)}) fusion(bf16[512,512]{1,0:T(8,128)(2,1)} %w_down.1, s32[]{:T(128)S(6)} %select_n.28, bf16[512,512]{1,0:T(8,128)(2,1)} %w_up.1), kind=kLoop, calls=%fused_computation.3 | loop fusion | bytes 131076 | tf_op jit(solution)/shard_map/dynamic_slice | solution.py:201
  62.4 1.6 %copy.21 = bf16[512,32]{0,1:T(8,128)(2,1)} copy(bf16[512,32]{1,0:T(8,128)(2,1)} %get-tuple-element.20) | data formatting | bytes 65536
  64.0 0.7 copy.20
  64.7 0.8 maximum_bitcast_fusion.weights
  65.5 0.0 copy-start.7
  65.5 0.0 collective-permute-done.3.k1
  65.5 0.0 collective-permute-done.4.v1
  65.5 0.0 copy-done.2
  65.5 0.6 copy-done.7
  66.1 3.4 %shard_map.149 = (f32[512,512]{1,0:T(8,128)S(1)}, bf16[96,512]{1,0:T(8,128)(2,1)S(1)}) custom-call(s32[1]{0:T(128)} %bitcast.2.first, s32[4]{0:T(128)S(1)} %copy-done.7, bf16[512,512]{1,0:T(8,128)(2,1)S(1)} %copy-done.2, bf16[512,512]{1,0:T(8,128)(2,1)S(1)} %collective-permute-done.1.k2, bf16[512,512]{1,0:T(8,128)(2,1)S(1)} %collective-permute-done.2.v2, ...), custom_call_target="tpu_custom_call" | custom-call | tf_op jit(solution)/shard_map/pallas_call | solution.py:203
  69.6 0.0 copy-start.3
  69.6 1.0 copy-done.3
  70.6 0.0 all-to-all-done.came
  70.6 1.8 %shard_map.150 = (f32[32,512]{1,0:T(8,128)}, f32[32,512]{1,0:T(8,128)}, f32[32,512]{1,0:T(8,128)}, bf16[8,96,512]{2,1,0:T(8,128)(2,1)S(1)}) custom-call(bf16[8,96,512]{2,1,0:T(8,128)(2,1)S(1)} %all-to-all-done.came, bf16[96,512]{1,0:T(8,128)(2,1)S(1)} %get-tuple-element.14.refs_0_, f32[32,512]{1,0:T(8,128)} %bitcast.14, f32[32,512]{1,0:T(8,128)} %bitcast.15, ...), custom_call_target="tpu_custom_call" | custom-call | tf_op jit(solution)/shard_map/pallas_call | solution.py:224
  72.4 0.0 copy-start.4
  72.4 29.0 %all_to_all.10.same = bf16[8,96,512]{2,1,0:T(8,128)(2,1)S(1)} all-to-all(bf16[8,96,512]{2,1,0:T(8,128)(2,1)S(1)} %get-tuple-element.15), channel_id=1, replica_groups={{0,64,128,192,256,320,384,448},{32,96,160,224,288,352,416,480},{1,65,12..., dimensions={0} | all-to-all | bytes 1572864 | tf_op jit(solution)/shard_map/all_to_all | solution.py:232
  101.5 0.0 copy-start.5
  101.5 2.5 %collective-permute-start.5 = (bf16[8,96,512]{2,1,0:T(8,128)(2,1)S(1)}, bf16[8,96,512]{2,1,0:T(8,128)(2,1)S(1)}, u32[]{:S(2)}, u32[]{:S(2)}) collective-permute-start(bf16[8,96,512]{2,1,0:T(8,128)(2,1)S(1)} %all_to_all.10.same), channel_id=1, source_target_pairs={{0,32},{32,0},{64,96},{96,64},{128,160},{160,128},{192,224},{224,1... | collective-permute-start | bytes 2359304 | tf_op jit(solution)/shard_map/ppermute | solution.py:233
  104.0 1.9 %collective-permute-done.5.swap = bf16[8,96,512]{2,1,0:T(8,128)(2,1)S(1)} collective-permute-done((bf16[8,96,512]{2,1,0:T(8,128)(2,1)S(1)}, bf16[8,96,512]{2,1,0:T(8,128)(2,1)S(1)}, u32[]{:S(2)}, u32[]{:S(2)}) %collective-permute-start.5) | collective-permute-done | bytes 786464 | tf_op jit(solution)/shard_map/ppermute | solution.py:233
  105.9 0.0 copy-done.4
  105.9 0.0 copy-done.5
  105.9 2.0 %shard_map.151 = bf16[512,512]{1,0:T(8,128)(2,1)} custom-call(s32[1]{0:T(128)} %bitcast.core, bf16[512,512]{1,0:T(8,128)(2,1)S(1)} %copy-done.2, bf16[8,96,512]{2,1,0:T(8,128)(2,1)S(1)} %all_to_all.10.same, bf16[8,96,512]{2,1,0:T(8,128)(2,1)S(1)} %collective-permute-done.5.swap, f32[512,512]{1,0:T(8,128)S(1)} %copy-done.4, f32[1,512]{1,0:T(1,128)S(1)} %bitcast.12), custom_call_target="tpu_custom_call" | custom-call | tf_op jit(solution)/shard_map/pallas_call | solution.py:234
Async XLA Ops:
  0.6 0.7 copy-start.6
  1.3 13.3 %copy-start = (bf16[512,512]{1,0:T(8,128)(2,1)S(1)}, bf16[512,512]{1,0:T(8,128)(2,1)}, u32[]{:S(2)}) copy-start(bf16[512,512]{1,0:T(8,128)(2,1)} %k0.1) | copy-start | bytes 1572868
  5.8 10.7 %collective-permute-start = (bf16[8,96,512]{2,1,0:T(8,128)(2,1)S(1)}, bf16[8,96,512]{2,1,0:T(8,128)(2,1)S(1)}, u32[]{:S(2)}, u32[]{:S(2)}) collective-permute-start(bf16[8,96,512]{2,1,0:T(8,128)(2,1)S(1)} %get-tuple-element.13), channel_id=1, source_target_pairs={{0,32},{32,0},{64,96},{96,64},{128,160},{160,128},{192,224},{224,1... | collective-permute-start | bytes 2359304 | tf_op jit(solution)/shard_map/ppermute | solution.py:190
  14.6 17.5 %collective-permute-start.1 = (bf16[512,512]{1,0:T(8,128)(2,1)S(1)}, bf16[512,512]{1,0:T(8,128)(2,1)S(1)}, u32[]{:S(2)}, u32[]{:S(2)}) collective-permute-start(bf16[512,512]{1,0:T(8,128)(2,1)S(1)} %copy-done), channel_id=1, source_target_pairs={{0,64},{32,96},{64,128},{96,160},{128,192},{160,224},{192,256},{22... | collective-permute-start | bytes 1572872 | tf_op jit(solution)/shard_map/ppermute | solution.py:179
  17.6 3.7 %copy-start.1 = (bf16[512,512]{1,0:T(8,128)(2,1)S(1)}, bf16[512,512]{1,0:T(8,128)(2,1)}, u32[]{:S(2)}) copy-start(bf16[512,512]{1,0:T(8,128)(2,1)} %v0.1) | copy-start | bytes 1572868
  17.6 53.0 %all-to-all-start = ((bf16[8,96,512]{2,1,0:T(8,128)(2,1)}), bf16[8,96,512]{2,1,0:T(8,128)(2,1)S(1)}, u32[]{:S(2)}, u32[]{:S(2)}) async-start(bf16[8,96,512]{2,1,0:T(8,128)(2,1)} %shard_map.148), calls=%async_computation | async-start | bytes 1572864 | tf_op jit(solution)/shard_map/all_to_all | solution.py:198
  21.3 34.2 %collective-permute-start.2 = (bf16[512,512]{1,0:T(8,128)(2,1)S(1)}, bf16[512,512]{1,0:T(8,128)(2,1)S(1)}, u32[]{:S(2)}, u32[]{:S(2)}) collective-permute-start(bf16[512,512]{1,0:T(8,128)(2,1)S(1)} %copy-done.1), channel_id=1, source_target_pairs={{0,64},{32,96},{64,128},{96,160},{128,192},{160,224},{192,256},{22... | collective-permute-start | bytes 1572872 | tf_op jit(solution)/shard_map/ppermute | solution.py:180
  33.0 32.5 %collective-permute-start.3 = (bf16[512,512]{1,0:T(8,128)(2,1)}, bf16[512,512]{1,0:T(8,128)(2,1)}, u32[]{:S(2)}, u32[]{:S(2)}) collective-permute-start(bf16[512,512]{1,0:T(8,128)(2,1)} %broadcast_select_fusion.1), channel_id=1, source_target_pairs={{0,32},{32,0},{64,96},{96,64},{128,160},{160,128},{192,224},{224,1... | collective-permute-start | bytes 1572872 | tf_op jit(solution)/shard_map/ppermute | solution.py:199
  56.4 9.1 %collective-permute-start.4 = (bf16[512,512]{1,0:T(8,128)(2,1)}, bf16[512,512]{1,0:T(8,128)(2,1)}, u32[]{:S(2)}, u32[]{:S(2)}) collective-permute-start(bf16[512,512]{1,0:T(8,128)(2,1)} %broadcast_select_fusion), channel_id=1, source_target_pairs={{0,32},{32,0},{64,96},{96,64},{128,160},{160,128},{192,224},{224,1... | collective-permute-start | bytes 1572872 | tf_op jit(solution)/shard_map/ppermute | solution.py:200
  60.6 4.9 %copy-start.2 = (bf16[512,512]{1,0:T(8,128)(2,1)S(1)}, bf16[512,512]{1,0:T(8,128)(2,1)}, u32[]{:S(2)}) copy-start(bf16[512,512]{1,0:T(8,128)(2,1)} %q.3) | copy-start | bytes 1572868
  65.5 0.7 copy-start.7
  69.6 1.0 copy-start.3
  72.4 33.4 %copy-start.4 = (f32[512,512]{1,0:T(8,128)S(1)}, f32[512,512]{1,0:T(8,128)}, u32[]{:S(2)}) copy-start(f32[512,512]{1,0:T(8,128)} %copy-done.3) | copy-start | bytes 3145732
  101.5 4.4 %copy-start.5 = (f32[512]{0:T(512)S(1)}, f32[512]{0:T(512)}, u32[]{:S(2)}) copy-start(f32[512]{0:T(512)} %param.17) | copy-start | bytes 6148
  101.5 4.4 %collective-permute-start.5 = (bf16[8,96,512]{2,1,0:T(8,128)(2,1)S(1)}, bf16[8,96,512]{2,1,0:T(8,128)(2,1)S(1)}, u32[]{:S(2)}, u32[]{:S(2)}) collective-permute-start(bf16[8,96,512]{2,1,0:T(8,128)(2,1)S(1)} %all_to_all.10.same), channel_id=1, source_target_pairs={{0,32},{32,0},{64,96},{96,64},{128,160},{160,128},{192,224},{224,1... | collective-permute-start | bytes 2359304 | tf_op jit(solution)/shard_map/ppermute | solution.py:233

commit v4 on v3

--- a/solution.py
+++ b/solution.py
@@ -28,26 +28,27 @@
 
 
 def grads_kernel(core, keys, values, rates, w_gate, w_up, w_down, mine, other, *refs):
-    bufs, sems = refs[:5], refs[5]
+    bufs, sems = refs[:6], refs[6]
     copies = [
         pltpu.make_async_copy(src, dst, sems.at[n])
-        for n, (src, dst) in enumerate(zip((keys, w_gate, values, w_up, w_down), bufs))
+        for n, (src, dst) in enumerate(zip((keys, w_gate, rates, values, w_up, w_down), bufs))
     ]
     for copy in copies:
         copy.start()
-    k_buf, gate_buf, v_buf, up_buf, down_buf = bufs
-    per_token = jnp.broadcast_to(rates[...], (128, TOK)).T
+    k_buf, gate_buf, rate_buf, v_buf, up_buf, down_buf = bufs
     copies[0].wait()
     copies[1].wait()
     k = k_buf[...]
     gate = contract(k, gate_buf[...], (1, 0))
     copies[2].wait()
+    per_token = jnp.broadcast_to(rate_buf[...], (128, TOK)).T
+    copies[3].wait()
     err = jnp.concatenate(
         [-(per_token * v_buf[:, i : i + 128].astype(f32)) for i in range(0, TOK, 128)], axis=1
     ).astype(bf16)
-    copies[3].wait()
+    copies[4].wait()
     upper = contract(k, up_buf[...], (1, 0))
-    copies[4].wait()
+    copies[5].wait()
     back = contract(err, down_buf[...], (1, 1))
     sig = jax.nn.sigmoid(gate)
     act = gate * sig
@@ -98,10 +99,7 @@
 BLOCK = 256
 
 
-def attention_kernel(
-    first, lengths, q, k2, v2, k1, v1, k0, v0, weights, out, out_weights
-):
-    out_weights[...] = weights[...]
+def attention_kernel(first, lengths, q, k2, v2, k1, v1, k0, v0, out):
     for b in range(TOK // BLOCK):
         qb = q[b * BLOCK : (b + 1) * BLOCK]
         qpos = first[0] + b * BLOCK + lax.broadcasted_iota(jnp.int32, (BLOCK, 1), 0)
@@ -182,11 +180,22 @@
     mine, other = pl.pallas_call(
         grads_kernel,
         out_shape=(pltpu.VMEM(piece.shape, bf16),) * 2,
-        in_specs=[SMEM, HBM, HBM, VMEM, HBM, HBM, HBM],
+        in_specs=[SMEM] + [HBM] * 6,
         out_specs=(VMEM, VMEM),
-        scratch_shapes=[pltpu.VMEM((TOK, TOK), bf16)] * 5 + [pltpu.SemaphoreType.DMA((5,))],
-        compiler_params=PARAMS,
-    )(cores, far(keys), far(values), rates.reshape(1, TOK), far(w_gate), far(w_up), far(w_down))
+        scratch_shapes=[pltpu.VMEM((TOK, TOK), bf16)] * 2
+        + [pltpu.VMEM((1, TOK), f32)]
+        + [pltpu.VMEM((TOK, TOK), bf16)] * 3
+        + [pltpu.SemaphoreType.DMA((6,))],
+        compiler_params=PARAMS,
+    )(
+        cores,
+        far(keys),
+        far(values),
+        far(rates.reshape(1, TOK)),
+        far(w_gate),
+        far(w_up),
+        far(w_down),
+    )
     got = lax.ppermute(other, "seq", PARTNER)
     both = pl.pallas_call(
         pair_kernel,
@@ -196,18 +205,24 @@
         compiler_params=PARAMS,
     )(near_core(mine), near_core(got))
     came = lax.all_to_all(both, "seq", 0, 0, axis_index_groups=SAME_CORE)
+    weights = [lax.dynamic_slice_in_dim(w, index * COLS, COLS, 1) for w in (w_gate, w_up, w_down)]
+    weights = jnp.concatenate(weights, axis=1).T
+    *news, spread = pl.pallas_call(
+        update_kernel,
+        out_shape=(jax.ShapeDtypeStruct((COLS, TOK), f32),) * 3 + (pltpu.VMEM(piece.shape, bf16),),
+        in_specs=[VMEM] * 2 + [HBM] * 3,
+        out_specs=(VMEM,) * 4,
+        scratch_shapes=[pltpu.VMEM((COLS, TOK), f32)] * 3 + [pltpu.SemaphoreType.DMA((3,))],
+        compiler_params=PARAMS,
+    )(near_core(came), near_core(weights), far(mom_gate.T), far(mom_up.T), far(mom_down.T))
+    same = lax.all_to_all(spread, "seq", 0, 0, axis_index_groups=SAME_CORE)
     near_k = lax.ppermute(jnp.where(core == 0, keys, k2), "seq", PARTNER)
     near_v = lax.ppermute(jnp.where(core == 0, values, v2), "seq", PARTNER)
-    weights = [lax.dynamic_slice_in_dim(w, index * COLS, COLS, 1) for w in (w_gate, w_up, w_down)]
-    weights = jnp.concatenate(weights, axis=1).T
-    attn, weights = pl.pallas_call(
+    attn = pl.pallas_call(
         attention_kernel,
-        out_shape=(
-            jax.ShapeDtypeStruct((TOK, TOK), f32),
-            pltpu.VMEM((PART, TOK), bf16),
-        ),
-        in_specs=[SMEM, SMEM] + [VMEM] * 8,
-        out_specs=(VMEM,) * 2,
+        out_shape=jax.ShapeDtypeStruct((TOK, TOK), f32),
+        in_specs=[SMEM, SMEM] + [VMEM] * 7,
+        out_specs=VMEM,
         compiler_params=PARAMS,
     )(
         jnp.reshape(index * TOK, (1,)),
@@ -219,17 +234,7 @@
         near_core(near_v),
         near_core(keys),
         near_core(values),
-        weights,
-    )
-    *news, spread = pl.pallas_call(
-        update_kernel,
-        out_shape=(jax.ShapeDtypeStruct((COLS, TOK), f32),) * 3 + (pltpu.VMEM(piece.shape, bf16),),
-        in_specs=[VMEM] * 2 + [HBM] * 3,
-        out_specs=(VMEM,) * 4,
-        scratch_shapes=[pltpu.VMEM((COLS, TOK), f32)] * 3 + [pltpu.SemaphoreType.DMA((3,))],
-        compiler_params=PARAMS,
-    )(near_core(came), near_core(weights), far(mom_gate.T), far(mom_up.T), far(mom_down.T))
-    same = lax.all_to_all(spread, "seq", 0, 0, axis_index_groups=SAME_CORE)
+    )
     swap = lax.ppermute(same, "seq", PARTNER)
     mixed = pl.pallas_call(
         fast_kernel,

time: 108 us -> 103 us (0.954); the launches traced: 108 us -> 102 us
  blocking collectives: 29 us -> 0 us
  waiting for transfers between devices: 28.8 us -> 51.3 us
  local copies, waits for them, and re-layouts: 8.1 us -> 2.39 us
  starting transfers between devices: 25.7 us -> 31 us
  Pallas kernels: 12.9 us -> 14.4 us
    all_to_all x1 -> x0, blocking collectives: 29 us -> none  [local(): same = lax.all_to_all(spread, 'seq', 0, 0, axis_index_groups=SAME_CORE)]
    all_to_all x1, waiting for transfers between devices: 0.01 us -> 21.1 us  [local(): came = lax.all_to_all(both, 'seq', 0, 0, axis_index_groups=SAME_CORE)]
    ppermute x1, waiting for transfers between devices: 7.56 us -> 21.7 us  [local(): k2 = lax.ppermute(keys, 'seq', NEXT_CHIP)]
    ppermute x1, waiting for transfers between devices: 18.8 us -> 4.7 us  [local(): v2 = lax.ppermute(values, 'seq', NEXT_CHIP)]
    unnamed x19 -> x13, local copies, waits for them, and re-layouts: 5.29 us -> 0.27 us
    all_to_all x0 -> x1, starting transfers between devices: none -> 3.69 us  [local(): same = lax.all_to_all(spread, 'seq', 0, 0, axis_index_groups=SAME_CORE)]
    ppermute x1, starting transfers between devices: 1.32 us -> 3.28 us  [local(): k2 = lax.ppermute(keys, 'seq', NEXT_CHIP)]
    ppermute x1, waiting for transfers between devices: 1.89 us -> 0.01 us  [local(): swap = lax.ppermute(same, 'seq', PARTNER)]
  transfers between devices with their start and end apart: 7 -> 8, of which waited for: 4 -> 5; matrix products, arithmetic and copies ran while one was open for 8% -> 4% of each run, Pallas kernels for 4% -> 3%
where the time goes in v4:
time: 103 us; the launch traced here: 102 us
  waiting for transfers between devices  51.3 us (50%)
  starting transfers between devices  31 us (30%)
  Pallas kernels  14.4 us (14%)
  local copies, waits for them, and re-layouts  2.39 us (2%)
  other arithmetic  1.7 us (2%)
    ppermute x1, waiting for transfers between devices, local(): k2 = lax.ppermute(keys, 'seq', NEXT_CHIP)  21.7 us
    all_to_all x1, waiting for transfers between devices, local(): came = lax.all_to_all(both, 'seq', 0, 0, axis_index_groups=SAME_CORE)  21.1 us
    ppermute x1, starting transfers between devices, local(): got = lax.ppermute(other, 'seq', PARTNER)  8.76 us
    ppermute x1, waiting for transfers between devices, local(): v2 = lax.ppermute(values, 'seq', NEXT_CHIP)  4.7 us
    pallas_call x1, Pallas kernels, local(): pl.pallas_call(grads_kernel, out_shape=(pltpu.VMEM(piece.shape, bf16),) *...  4.57 us
    ppermute x1, starting transfers between devices, local(): near_k = lax.ppermute(jnp.where(core == 0, keys, k2), 'seq', PARTNER)  3.73 us
    all_to_all x1, starting transfers between devices, local(): same = lax.all_to_all(spread, 'seq', 0, 0, axis_index_groups=SAME_CORE)  3.69 us
    all_to_all x1, starting transfers between devices, local(): came = lax.all_to_all(both, 'seq', 0, 0, axis_index_groups=SAME_CORE)  3.55 us
  transfers between devices with their start and end apart: 8, of which 5 were waited for; matrix products, arithmetic and copies ran while one was open for 4% of the time, Pallas kernels for 3%

profile of v4, /device:TPU:1, one launch (start us, length us, event | category | flops | bytes accessed | tf_op | source)
XLA Modules:
  0.0 101.6 jit_solution(11516876201167593309)
XLA Ops:
  0.6 4.6 %shard_map.147 = (bf16[8,96,512]{2,1,0:T(8,128)(2,1)S(1)}, bf16[8,96,512]{2,1,0:T(8,128)(2,1)S(1)}) custom-call(s32[1]{0:T(128)} %bitcast.core, bf16[512,512]{1,0:T(8,128)(2,1)} %k0.1, bf16[512,512]{1,0:T(8,128)(2,1)} %v0.1, f32[1,512]{1,0:T(1,128)} %bitcast.16, bf16[512,512]{1,0:T(8,128)(2,1)} %w_gate.1, bf16[512,512]{1,0:T(8,128)(2,1)} %w_up.1, ...), custom_call_target="tpu_custom_call" | custom-call | tf_op jit(solution)/shard_map/pallas_call | solution.py:180
  5.2 8.8 %collective-permute-start = (bf16[8,96,512]{2,1,0:T(8,128)(2,1)S(1)}, bf16[8,96,512]{2,1,0:T(8,128)(2,1)S(1)}, u32[]{:S(2)}, u32[]{:S(2)}) collective-permute-start(bf16[8,96,512]{2,1,0:T(8,128)(2,1)S(1)} %get-tuple-element.11), channel_id=1, source_target_pairs={{0,32},{32,0},{64,96},{96,64},{128,160},{160,128},{192,224},{224,1... | collective-permute-start | bytes 2359304 | tf_op jit(solution)/shard_map/ppermute | solution.py:199
  14.0 1.9 %collective-permute-done.got = bf16[8,96,512]{2,1,0:T(8,128)(2,1)S(1)} collective-permute-done((bf16[8,96,512]{2,1,0:T(8,128)(2,1)S(1)}, bf16[8,96,512]{2,1,0:T(8,128)(2,1)S(1)}, u32[]{:S(2)}, u32[]{:S(2)}) %collective-permute-start) | collective-permute-done | bytes 786464 | tf_op jit(solution)/shard_map/ppermute | solution.py:199
  15.9 1.1 %shard_map.148 = bf16[8,96,512]{2,1,0:T(8,128)(2,1)} custom-call(bf16[8,96,512]{2,1,0:T(8,128)(2,1)S(1)} %get-tuple-element.10.mine, bf16[8,96,512]{2,1,0:T(8,128)(2,1)S(1)} %collective-permute-done.got), custom_call_target="tpu_custom_call" | custom-call | tf_op jit(solution)/shard_map/pallas_call | solution.py:200
  17.0 3.5 %all-to-all-start = ((bf16[8,96,512]{2,1,0:T(8,128)(2,1)}), bf16[8,96,512]{2,1,0:T(8,128)(2,1)S(1)}, u32[]{:S(2)}, u32[]{:S(2)}) async-start(bf16[8,96,512]{2,1,0:T(8,128)(2,1)} %shard_map.148), calls=%async_computation | async-start | bytes 1572864 | tf_op jit(solution)/shard_map/all_to_all | solution.py:207
  20.5 1.0 constant_dynamic-slice_fusion.2
  21.5 0.1 copy.19
  21.6 1.1 %constant_dynamic-slice_fusion = (bf16[512,32]{1,0:T(8,128)(2,1)S(1)}, bf16[512,32]{1,0:T(8,128)(2,1)S(1)}) fusion(bf16[512,512]{1,0:T(8,128)(2,1)} %w_down.1, s32[]{:T(128)S(6)} %select_n.25, bf16[512,512]{1,0:T(8,128)(2,1)} %w_up.1), kind=kLoop, calls=%fused_computation.3 | loop fusion | bytes 131076 | tf_op jit(solution)/shard_map/dynamic_slice | solution.py:208
  22.7 0.1 copy.21
  22.8 0.1 copy.20
  22.9 21.1 %all-to-all-done.came = bf16[8,96,512]{2,1,0:T(8,128)(2,1)S(1)} async-done(((bf16[8,96,512]{2,1,0:T(8,128)(2,1)}), bf16[8,96,512]{2,1,0:T(8,128)(2,1)S(1)}, u32[]{:S(2)}, u32[]{:S(2)}) %all-to-all-start) | async-done | bytes 786464 | tf_op jit(solution)/shard_map/all_to_all | solution.py:207
  44.1 2.2 %shard_map.149 = (f32[32,512]{1,0:T(8,128)}, f32[32,512]{1,0:T(8,128)}, f32[32,512]{1,0:T(8,128)}, bf16[8,96,512]{2,1,0:T(8,128)(2,1)}) custom-call(bf16[8,96,512]{2,1,0:T(8,128)(2,1)S(1)} %all-to-all-done.came, bf16[96,512]{1,0:T(8,128)(2,1)S(1)} %maximum_bitcast_fusion.refs_0_, f32[32,512]{1,0:T(8,128)} %bitcast.13, f32[32,512]{1,0:T(8,128)} %bitcast.14, ...), custom_call_target="tpu_custom_call" | custom-call | tf_op jit(solution)/shard_map/pallas_call | solution.py:210
  46.2 0.0 copy-start
  46.3 0.0 copy-start.1
  46.3 3.7 %all-to-all-start.1 = ((bf16[8,96,512]{2,1,0:T(8,128)(2,1)}), bf16[8,96,512]{2,1,0:T(8,128)(2,1)S(1)}, u32[]{:S(2)}, u32[]{:S(2)}) async-start(bf16[8,96,512]{2,1,0:T(8,128)(2,1)} %get-tuple-element.12), calls=%async_computation.1 | async-start | bytes 1572864 | tf_op jit(solution)/shard_map/all_to_all | solution.py:218
  50.0 0.0 copy-done
  50.0 3.3 %collective-permute-start.2 = (bf16[512,512]{1,0:T(8,128)(2,1)S(1)}, bf16[512,512]{1,0:T(8,128)(2,1)S(1)}, u32[]{:S(2)}, u32[]{:S(2)}) collective-permute-start(bf16[512,512]{1,0:T(8,128)(2,1)S(1)} %copy-done), channel_id=1, source_target_pairs={{0,64},{32,96},{64,128},{96,160},{128,192},{160,224},{192,256},{22... | collective-permute-start | bytes 1572872 | tf_op jit(solution)/shard_map/ppermute | solution.py:177
  53.3 0.0 copy-done.1
  53.3 3.1 %collective-permute-start.3 = (bf16[512,512]{1,0:T(8,128)(2,1)S(1)}, bf16[512,512]{1,0:T(8,128)(2,1)S(1)}, u32[]{:S(2)}, u32[]{:S(2)}) collective-permute-start(bf16[512,512]{1,0:T(8,128)(2,1)S(1)} %copy-done.1), channel_id=1, source_target_pairs={{0,64},{32,96},{64,128},{96,160},{128,192},{160,224},{192,256},{22... | collective-permute-start | bytes 1572872 | tf_op jit(solution)/shard_map/ppermute | solution.py:178
  56.4 21.7 %collective-permute-done.2.k2 = bf16[512,512]{1,0:T(8,128)(2,1)S(1)} collective-permute-done((bf16[512,512]{1,0:T(8,128)(2,1)S(1)}, bf16[512,512]{1,0:T(8,128)(2,1)S(1)}, u32[]{:S(2)}, u32[]{:S(2)}) %collective-permute-start.2) | collective-permute-done | bytes 524320 | tf_op jit(solution)/shard_map/ppermute | solution.py:177
  78.1 0.8 broadcast_select_fusion.1
  79.0 0.0 copy-start.2
  79.0 3.7 %collective-permute-start.4 = (bf16[512,512]{1,0:T(8,128)(2,1)}, bf16[512,512]{1,0:T(8,128)(2,1)}, u32[]{:S(2)}, u32[]{:S(2)}) collective-permute-start(bf16[512,512]{1,0:T(8,128)(2,1)} %broadcast_select_fusion.1), channel_id=1, source_target_pairs={{0,32},{32,0},{64,96},{96,64},{128,160},{160,128},{192,224},{224,1... | collective-permute-start | bytes 1572872 | tf_op jit(solution)/shard_map/ppermute | solution.py:219
  82.7 0.0 all-to-all-done.1.same
  82.7 1.9 %collective-permute-start.1 = (bf16[8,96,512]{2,1,0:T(8,128)(2,1)S(1)}, bf16[8,96,512]{2,1,0:T(8,128)(2,1)}, u32[]{:S(2)}, u32[]{:S(2)}) collective-permute-start(bf16[8,96,512]{2,1,0:T(8,128)(2,1)S(1)} %all-to-all-done.1.same), channel_id=1, source_target_pairs={{0,32},{32,0},{64,96},{96,64},{128,160},{160,128},{192,224},{224,1... | collective-permute-start | bytes 2359304 | tf_op jit(solution)/shard_map/ppermute | solution.py:238
  84.6 4.7 %collective-permute-done.3.v2 = bf16[512,512]{1,0:T(8,128)(2,1)S(1)} collective-permute-done((bf16[512,512]{1,0:T(8,128)(2,1)S(1)}, bf16[512,512]{1,0:T(8,128)(2,1)S(1)}, u32[]{:S(2)}, u32[]{:S(2)}) %collective-permute-start.3) | collective-permute-done | bytes 524320 | tf_op jit(solution)/shard_map/ppermute | solution.py:178
  89.3 0.8 broadcast_select_fusion
  90.2 2.9 %collective-permute-start.5 = (bf16[512,512]{1,0:T(8,128)(2,1)}, bf16[512,512]{1,0:T(8,128)(2,1)}, u32[]{:S(2)}, u32[]{:S(2)}) collective-permute-start(bf16[512,512]{1,0:T(8,128)(2,1)} %broadcast_select_fusion), channel_id=1, source_target_pairs={{0,32},{32,0},{64,96},{96,64},{128,160},{160,128},{192,224},{224,1... | collective-permute-start | bytes 1572872 | tf_op jit(solution)/shard_map/ppermute | solution.py:220
  93.1 0.0 copy-start.4
  93.2 0.0 collective-permute-done.4.k1
  93.2 1.8 %collective-permute-done.5.v1 = bf16[512,512]{1,0:T(8,128)(2,1)} collective-permute-done((bf16[512,512]{1,0:T(8,128)(2,1)}, bf16[512,512]{1,0:T(8,128)(2,1)}, u32[]{:S(2)}, u32[]{:S(2)}) %collective-permute-start.5) | collective-permute-done | bytes 524320 | tf_op jit(solution)/shard_map/ppermute | solution.py:220
  95.0 0.0 copy-done.2
  95.0 0.0 copy-done.4
  95.0 0.0 copy-start.3
  95.0 3.5 %shard_map.150.attn = f32[512,512]{1,0:T(8,128)S(1)} custom-call(s32[1]{0:T(128)} %bitcast.6.first, s32[4]{0:T(128)S(1)} %copy-done.4, bf16[512,512]{1,0:T(8,128)(2,1)S(1)} %copy-done.2, bf16[512,512]{1,0:T(8,128)(2,1)S(1)} %collective-permute-done.2.k2, bf16[512,512]{1,0:T(8,128)(2,1)S(1)} %collective-permute-done.3.v2, ...), custom_call_target="tpu_custom_call" | custom-call | tf_op jit(solution)/shard_map/pallas_call | solution.py:221
  98.5 0.0 collective-permute-done.1.swap
  98.5 0.0 copy-done.3
  98.5 3.2 %shard_map.151 = bf16[512,512]{1,0:T(8,128)(2,1)} custom-call(s32[1]{0:T(128)} %bitcast.core, bf16[512,512]{1,0:T(8,128)(2,1)S(1)} %copy-done.2, bf16[8,96,512]{2,1,0:T(8,128)(2,1)S(1)} %all-to-all-done.1.same, bf16[8,96,512]{2,1,0:T(8,128)(2,1)} %collective-permute-done.1.swap, f32[512,512]{1,0:T(8,128)S(1)} %shard_map.150.attn, f32[1,512]{1,0:T(1,128)S(1)} %bitcast.12), custom_call_target="tpu_custom_call" | custom-call | tf_op jit(solution)/shard_map/pallas_call | solution.py:239
  (1 shorter events, 0.0 us)
Async XLA Ops:
  5.2 10.7 %collective-permute-start = (bf16[8,96,512]{2,1,0:T(8,128)(2,1)S(1)}, bf16[8,96,512]{2,1,0:T(8,128)(2,1)S(1)}, u32[]{:S(2)}, u32[]{:S(2)}) collective-permute-start(bf16[8,96,512]{2,1,0:T(8,128)(2,1)S(1)} %get-tuple-element.11), channel_id=1, source_target_pairs={{0,32},{32,0},{64,96},{96,64},{128,160},{160,128},{192,224},{224,1... | collective-permute-start | bytes 2359304 | tf_op jit(solution)/shard_map/ppermute | solution.py:199
  17.0 27.1 %all-to-all-start = ((bf16[8,96,512]{2,1,0:T(8,128)(2,1)}), bf16[8,96,512]{2,1,0:T(8,128)(2,1)S(1)}, u32[]{:S(2)}, u32[]{:S(2)}) async-start(bf16[8,96,512]{2,1,0:T(8,128)(2,1)} %shard_map.148), calls=%async_computation | async-start | bytes 1572864 | tf_op jit(solution)/shard_map/all_to_all | solution.py:207
  46.2 3.7 %copy-start = (bf16[512,512]{1,0:T(8,128)(2,1)S(1)}, bf16[512,512]{1,0:T(8,128)(2,1)}, u32[]{:S(2)}) copy-start(bf16[512,512]{1,0:T(8,128)(2,1)} %k0.1) | copy-start | bytes 1572868
  46.3 7.0 %copy-start.1 = (bf16[512,512]{1,0:T(8,128)(2,1)S(1)}, bf16[512,512]{1,0:T(8,128)(2,1)}, u32[]{:S(2)}) copy-start(bf16[512,512]{1,0:T(8,128)(2,1)} %v0.1) | copy-start | bytes 1572868
  46.3 36.4 %all-to-all-start.1 = ((bf16[8,96,512]{2,1,0:T(8,128)(2,1)}), bf16[8,96,512]{2,1,0:T(8,128)(2,1)S(1)}, u32[]{:S(2)}, u32[]{:S(2)}) async-start(bf16[8,96,512]{2,1,0:T(8,128)(2,1)} %get-tuple-element.12), calls=%async_computation.1 | async-start | bytes 1572864 | tf_op jit(solution)/shard_map/all_to_all | solution.py:218
  50.0 28.1 %collective-permute-start.2 = (bf16[512,512]{1,0:T(8,128)(2,1)S(1)}, bf16[512,512]{1,0:T(8,128)(2,1)S(1)}, u32[]{:S(2)}, u32[]{:S(2)}) collective-permute-start(bf16[512,512]{1,0:T(8,128)(2,1)S(1)} %copy-done), channel_id=1, source_target_pairs={{0,64},{32,96},{64,128},{96,160},{128,192},{160,224},{192,256},{22... | collective-permute-start | bytes 1572872 | tf_op jit(solution)/shard_map/ppermute | solution.py:177
  53.3 36.1 %collective-permute-start.3 = (bf16[512,512]{1,0:T(8,128)(2,1)S(1)}, bf16[512,512]{1,0:T(8,128)(2,1)S(1)}, u32[]{:S(2)}, u32[]{:S(2)}) collective-permute-start(bf16[512,512]{1,0:T(8,128)(2,1)S(1)} %copy-done.1), channel_id=1, source_target_pairs={{0,64},{32,96},{64,128},{96,160},{128,192},{160,224},{192,256},{22... | collective-permute-start | bytes 1572872 | tf_op jit(solution)/shard_map/ppermute | solution.py:178
  79.0 16.0 %copy-start.2 = (bf16[512,512]{1,0:T(8,128)(2,1)S(1)}, bf16[512,512]{1,0:T(8,128)(2,1)}, u32[]{:S(2)}) copy-start(bf16[512,512]{1,0:T(8,128)(2,1)} %q.3) | copy-start | bytes 1572868
  79.0 14.2 %collective-permute-start.4 = (bf16[512,512]{1,0:T(8,128)(2,1)}, bf16[512,512]{1,0:T(8,128)(2,1)}, u32[]{:S(2)}, u32[]{:S(2)}) collective-permute-start(bf16[512,512]{1,0:T(8,128)(2,1)} %broadcast_select_fusion.1), channel_id=1, source_target_pairs={{0,32},{32,0},{64,96},{96,64},{128,160},{160,128},{192,224},{224,1... | collective-permute-start | bytes 1572872 | tf_op jit(solution)/shard_map/ppermute | solution.py:219
  82.7 15.8 %collective-permute-start.1 = (bf16[8,96,512]{2,1,0:T(8,128)(2,1)S(1)}, bf16[8,96,512]{2,1,0:T(8,128)(2,1)}, u32[]{:S(2)}, u32[]{:S(2)}) collective-permute-start(bf16[8,96,512]{2,1,0:T(8,128)(2,1)S(1)} %all-to-all-done.1.same), channel_id=1, source_target_pairs={{0,32},{32,0},{64,96},{96,64},{128,160},{160,128},{192,224},{224,1... | collective-permute-start | bytes 2359304 | tf_op jit(solution)/shard_map/ppermute | solution.py:238
  90.2 4.8 %collective-permute-start.5 = (bf16[512,512]{1,0:T(8,128)(2,1)}, bf16[512,512]{1,0:T(8,128)(2,1)}, u32[]{:S(2)}, u32[]{:S(2)}) collective-permute-start(bf16[512,512]{1,0:T(8,128)(2,1)} %broadcast_select_fusion), channel_id=1, source_target_pairs={{0,32},{32,0},{64,96},{96,64},{128,160},{160,128},{192,224},{224,1... | collective-permute-start | bytes 1572872 | tf_op jit(solution)/shard_map/ppermute | solution.py:220
  93.1 1.9 %copy-start.4 = (s32[4]{0:T(128)S(1)}, s32[4]{0:T(128)}, u32[]{:S(2)}) copy-start(s32[4]{0:T(128)} %lengths.1) | copy-start | bytes 52
  95.0 3.5 %copy-start.3 = (f32[512]{0:T(512)S(1)}, f32[512]{0:T(512)}, u32[]{:S(2)}) copy-start(f32[512]{0:T(512)} %param.17) | copy-start | bytes 6148

commit v5 on v4

--- a/solution.py
+++ b/solution.py
@@ -17,7 +17,10 @@
 
 PARTNER = [(i, i ^ 1) for i in range(2 * CHIPS)]
 NEXT_CHIP = [(i, i + 2) for i in range(2 * CHIPS - 2)]
+RIGHT = [(i, (i + 2) % (2 * CHIPS)) for i in range(2 * CHIPS)]
+LEFT = [(i, (i - 2) % (2 * CHIPS)) for i in range(2 * CHIPS)]
 SAME_CORE = [[c + 2 * k for k in range(CHIPS)] for c in range(2)]
+SAME_PARITY = [[c + 2 * (2 * k + p) for k in range(CHIPS // 2)] for p in range(2) for c in range(2)]
 
 f32 = jnp.float32
 bf16 = jnp.bfloat16
@@ -92,14 +95,21 @@
         news[n][...] = new
         normed = new * lax.rsqrt(jnp.sum(new * new, axis=1, keepdims=True) + 1e-06)
         shard = (weights[rows].astype(f32) - step_size * normed).astype(bf16)
-        for d in range(CHIPS):
+        for d in range(CHIPS // 2):
             spread[d, rows] = shard
 
 
 BLOCK = 256
 
 
-def attention_kernel(first, lengths, q, k2, v2, k1, v1, k0, v0, out):
+def attention_kernel(first, lengths, *refs):
+    out, bufs, sems = refs[7], refs[8:15], refs[15]
+    copies = [pltpu.make_async_copy(refs[n], bufs[n], sems.at[n]) for n in range(7)]
+    for copy in copies:
+        copy.start()
+    for copy in copies:
+        copy.wait()
+    q, k2, v2, k1, v1, k0, v0 = bufs
     for b in range(TOK // BLOCK):
         qb = q[b * BLOCK : (b + 1) * BLOCK]
         qpos = first[0] + b * BLOCK + lax.broadcasted_iota(jnp.int32, (BLOCK, 1), 0)
@@ -128,12 +138,22 @@
         out[b * BLOCK : (b + 1) * BLOCK] = acc / total
 
 
-def fast_kernel(core, q, same, swap, attn, gain, out, gate_t, up_t, down_t):
-    for side, src in ((core[0], same), (1 - core[0], swap)):
-        for d in range(CHIPS):
-            at = pl.ds(pl.multiple_of((2 * d + side) * COLS, COLS), COLS)
-            for n, dst in enumerate((gate_t, up_t, down_t)):
-                dst[at, :] = src[d, n * COLS : (n + 1) * COLS]
+def pick_kernel(chip, same, right, left):
+    at = chip[0] // 2
+    for out, step in ((right, 3), (left, 1)):
+        out[0] = same[at]
+        out[1] = same[(at + step) % (CHIPS // 2)]
+
+
+def fast_kernel(core, chip, q, same, sides, same_swap, sides_swap, attn, gain, out, *dsts):
+    for side, blocks, beside in ((core[0], same, sides), (1 - core[0], same_swap, sides_swap)):
+        sources = [(blocks, d, 2 * d + chip[0] % 2) for d in range(CHIPS // 2)]
+        sources += [(beside, n, (chip[0] + off) % CHIPS) for n, off in enumerate((7, 5, 1, 3))]
+        for src, n, owner in sources:
+            at = pl.ds(pl.multiple_of((2 * owner + side) * COLS, COLS), COLS)
+            for k, dst in enumerate(dsts):
+                dst[at, :] = src[n, k * COLS : (k + 1) * COLS]
+    gate_t, up_t, down_t = dsts
     x = q[...]
     qa = contract(x, gate_t[...], (1, 1))
     qb = contract(x, up_t[...], (1, 1))
@@ -174,6 +194,7 @@
     index = lax.axis_index("seq")
     core = index % 2
     cores = jnp.reshape(core, (1,))
+    chips = jnp.reshape(index // 2, (1,))
     k2 = lax.ppermute(keys, "seq", NEXT_CHIP)
     v2 = lax.ppermute(values, "seq", NEXT_CHIP)
     piece = jax.ShapeDtypeStruct((CHIPS, PART, TOK), bf16)
@@ -207,48 +228,59 @@
     came = lax.all_to_all(both, "seq", 0, 0, axis_index_groups=SAME_CORE)
     weights = [lax.dynamic_slice_in_dim(w, index * COLS, COLS, 1) for w in (w_gate, w_up, w_down)]
     weights = jnp.concatenate(weights, axis=1).T
-    *news, spread = pl.pallas_call(
-        update_kernel,
-        out_shape=(jax.ShapeDtypeStruct((COLS, TOK), f32),) * 3 + (pltpu.VMEM(piece.shape, bf16),),
-        in_specs=[VMEM] * 2 + [HBM] * 3,
-        out_specs=(VMEM,) * 4,
-        scratch_shapes=[pltpu.VMEM((COLS, TOK), f32)] * 3 + [pltpu.SemaphoreType.DMA((3,))],
-        compiler_params=PARAMS,
-    )(near_core(came), near_core(weights), far(mom_gate.T), far(mom_up.T), far(mom_down.T))
-    same = lax.all_to_all(spread, "seq", 0, 0, axis_index_groups=SAME_CORE)
     near_k = lax.ppermute(jnp.where(core == 0, keys, k2), "seq", PARTNER)
     near_v = lax.ppermute(jnp.where(core == 0, values, v2), "seq", PARTNER)
     attn = pl.pallas_call(
         attention_kernel,
         out_shape=jax.ShapeDtypeStruct((TOK, TOK), f32),
-        in_specs=[SMEM, SMEM] + [VMEM] * 7,
+        in_specs=[SMEM, SMEM] + [HBM] * 7,
         out_specs=VMEM,
+        scratch_shapes=[pltpu.VMEM((TOK, TOK), bf16)] * 7 + [pltpu.SemaphoreType.DMA((7,))],
         compiler_params=PARAMS,
     )(
         jnp.reshape(index * TOK, (1,)),
         lengths,
-        near_core(queries),
-        near_core(k2),
-        near_core(v2),
-        near_core(near_k),
-        near_core(near_v),
-        near_core(keys),
-        near_core(values),
+        far(queries),
+        far(k2),
+        far(v2),
+        far(near_k),
+        far(near_v),
+        far(keys),
+        far(values),
     )
-    swap = lax.ppermute(same, "seq", PARTNER)
+    *news, spread = pl.pallas_call(
+        update_kernel,
+        out_shape=(jax.ShapeDtypeStruct((COLS, TOK), f32),) * 3
+        + (pltpu.VMEM((CHIPS // 2, PART, TOK), bf16),),
+        in_specs=[VMEM] * 2 + [HBM] * 3,
+        out_specs=(VMEM,) * 4,
+        scratch_shapes=[pltpu.VMEM((COLS, TOK), f32)] * 3 + [pltpu.SemaphoreType.DMA((3,))],
+        compiler_params=PARAMS,
+    )(near_core(came), near_core(weights), far(mom_gate.T), far(mom_up.T), far(mom_down.T))
+    same = lax.all_to_all(spread, "seq", 0, 0, axis_index_groups=SAME_PARITY)
+    to_right, to_left = pl.pallas_call(
+        pick_kernel,
+        out_shape=(pltpu.VMEM((2, PART, TOK), bf16),) * 2,
+        in_specs=[SMEM, VMEM],
+        out_specs=(VMEM,) * 2,
+        compiler_params=PARAMS,
+    )(chips, near_core(same))
+    from_left = lax.ppermute(to_right, "seq", RIGHT)
+    from_right = lax.ppermute(to_left, "seq", LEFT)
+    same_swap = lax.ppermute(same, "seq", PARTNER)
+    sides = jnp.concatenate((from_left, from_right), axis=0)
+    sides_swap = lax.ppermute(sides, "seq", PARTNER)
     mixed = pl.pallas_call(
         fast_kernel,
         out_shape=jax.ShapeDtypeStruct((TOK, TOK), bf16),
-        in_specs=[SMEM] + [VMEM] * 5,
+        in_specs=[SMEM, SMEM] + [VMEM] * 7,
         out_specs=VMEM,
         compiler_params=PARAMS,
         scratch_shapes=[pltpu.VMEM((TOK, TOK), bf16)] * 3,
     )(
         cores,
-        near_core(queries),
-        near_core(same),
-        near_core(swap),
-        near_core(attn),
+        chips,
+        *[near_core(x) for x in (queries, same, sides, same_swap, sides_swap, attn)],
         norm_gain.reshape(1, TOK),
     )
     return (mixed, *[new.T for new in news])

time: 103 us -> 88.2 us (0.86)
  waiting for transfers between devices: 51.3 us -> 27 us
  starting transfers between devices: 31 us -> 39.9 us
  local copies, waits for them, and re-layouts: 2.39 us -> 4.18 us
    ppermute x1, waiting for transfers between devices: 21.7 us -> 0.01 us  [local(): k2 = lax.ppermute(keys, 'seq', NEXT_CHIP)]
    ppermute x1 -> x4, starting transfers between devices: 1.92 us -> 10.8 us  [the longest x1 4.57 us: local(): from_right = lax.ppermute(to_left, 'seq', LEFT)]
    all_to_all x1, waiting for transfers between devices: 0.01 us -> 6.2 us  [local(): same = lax.all_to_all(spread, 'seq', 0, 0, axis_index_groups=SAME_PARITY)]
    ppermute x1, waiting for transfers between devices: 4.7 us -> 1.02 us  [local(): v2 = lax.ppermute(values, 'seq', NEXT_CHIP)]
    all_to_all x1, waiting for transfers between devices: 21.1 us -> 17.8 us  [local(): came = lax.all_to_all(both, 'seq', 0, 0, axis_index_groups=SAME_CORE)]
    ppermute x1, starting transfers between devices: 2.95 us -> 4.97 us  [local(): near_v = lax.ppermute(jnp.where(core == 0, values, v2), 'seq', PARTNER)]
    ppermute x1, waiting for transfers between devices: 1.83 us -> 0.01 us  [local(): near_v = lax.ppermute(jnp.where(core == 0, values, v2), 'seq', PARTNER)]
    unnamed x13 -> x22, local copies, waits for them, and re-layouts: 0.27 us -> 2.04 us
  transfers between devices with their start and end apart: 8 -> 11, of which waited for: 5 -> 4; matrix products, arithmetic and copies ran while one was open for 4% -> 4% of each run, Pallas kernels for 3% -> 8%
where the time goes in v5:
time: 88.2 us; the launch traced here: 87.6 us
  starting transfers between devices  39.9 us (45%)
  waiting for transfers between devices  27 us (31%)
  Pallas kernels  14.5 us (16%)
  local copies, waits for them, and re-layouts  4.18 us (5%)
  other arithmetic  0.99 us (1%)
  between operations  0.99 us (1%)
    all_to_all x1, waiting for transfers between devices, local(): came = lax.all_to_all(both, 'seq', 0, 0, axis_index_groups=SAME_CORE)  17.8 us
    ppermute x1, starting transfers between devices, local(): got = lax.ppermute(other, 'seq', PARTNER)  8.75 us
    all_to_all x1, waiting for transfers between devices, local(): same = lax.all_to_all(spread, 'seq', 0, 0, axis_index_groups=SAME_PARITY)  6.2 us
    ppermute x1, starting transfers between devices, local(): near_v = lax.ppermute(jnp.where(core == 0, values, v2), 'seq', PARTNER)  4.97 us
    pallas_call x1, Pallas kernels, local(): pl.pallas_call(attention_kernel, out_shape=jax.ShapeDtypeStruct((TOK, TOK...  4.83 us
    pallas_call x1, Pallas kernels, local(): pl.pallas_call(grads_kernel, out_shape=(pltpu.VMEM(piece.shape, bf16),) *...  4.58 us
    ppermute x1, starting transfers between devices, local(): from_right = lax.ppermute(to_left, 'seq', LEFT)  4.57 us
    all_to_all x1, starting transfers between devices, local(): came = lax.all_to_all(both, 'seq', 0, 0, axis_index_groups=SAME_CORE)  3.68 us
  transfers between devices with their start and end apart: 11, of which 4 were waited for; matrix products, arithmetic and copies ran while one was open for 4% of the time, Pallas kernels for 8%

profile of v5, /device:TPU:1, one launch (start us, length us, event | category | flops | bytes accessed | tf_op | source)
XLA Modules:
  0.0 87.6 jit_solution(4181187508069837605)
XLA Ops:
  0.6 4.6 %shard_map.147 = (bf16[8,96,512]{2,1,0:T(8,128)(2,1)S(1)}, bf16[8,96,512]{2,1,0:T(8,128)(2,1)S(1)}) custom-call(s32[1]{0:T(128)} %bitcast.core, bf16[512,512]{1,0:T(8,128)(2,1)} %refs_5_.1, bf16[512,512]{1,0:T(8,128)(2,1)} %refs_6_.1, f32[1,512]{1,0:T(1,128)} %bitcast.17, bf16[512,512]{1,0:T(8,128)(2,1)} %w_gate.1, bf16[512,512]{1,0:T(8,128)(2,1)} %w_up.1, ...), custom_call_target="tpu_custom_call" | custom-call | tf_op jit(solution)/shard_map/pallas_call | solution.py:201
  5.2 8.8 %collective-permute-start = (bf16[8,96,512]{2,1,0:T(8,128)(2,1)S(1)}, bf16[8,96,512]{2,1,0:T(8,128)(2,1)S(1)}, u32[]{:S(2)}, u32[]{:S(2)}) collective-permute-start(bf16[8,96,512]{2,1,0:T(8,128)(2,1)S(1)} %get-tuple-element.13), channel_id=1, source_target_pairs={{0,32},{32,0},{64,96},{96,64},{128,160},{160,128},{192,224},{224,1... | collective-permute-start | bytes 2359304 | tf_op jit(solution)/shard_map/ppermute | solution.py:220
  14.0 1.9 %collective-permute-done.got = bf16[8,96,512]{2,1,0:T(8,128)(2,1)S(1)} collective-permute-done((bf16[8,96,512]{2,1,0:T(8,128)(2,1)S(1)}, bf16[8,96,512]{2,1,0:T(8,128)(2,1)S(1)}, u32[]{:S(2)}, u32[]{:S(2)}) %collective-permute-start) | collective-permute-done | bytes 786464 | tf_op jit(solution)/shard_map/ppermute | solution.py:220
  15.9 1.1 %shard_map.148 = bf16[8,96,512]{2,1,0:T(8,128)(2,1)} custom-call(bf16[8,96,512]{2,1,0:T(8,128)(2,1)S(1)} %get-tuple-element.12.mine, bf16[8,96,512]{2,1,0:T(8,128)(2,1)S(1)} %collective-permute-done.got), custom_call_target="tpu_custom_call" | custom-call | tf_op jit(solution)/shard_map/pallas_call | solution.py:221
  16.9 3.7 %all-to-all-start = ((bf16[8,96,512]{2,1,0:T(8,128)(2,1)}), bf16[8,96,512]{2,1,0:T(8,128)(2,1)S(1)}, u32[]{:S(2)}, u32[]{:S(2)}) async-start(bf16[8,96,512]{2,1,0:T(8,128)(2,1)} %shard_map.148), calls=%async_computation | async-start | bytes 1572864 | tf_op jit(solution)/shard_map/all_to_all | solution.py:228
  20.6 0.0 copy-done.3
  20.6 3.3 %collective-permute-start.5 = (bf16[512,512]{1,0:T(8,128)(2,1)S(1)}, bf16[512,512]{1,0:T(8,128)(2,1)S(1)}, u32[]{:S(2)}, u32[]{:S(2)}) collective-permute-start(bf16[512,512]{1,0:T(8,128)(2,1)S(1)} %copy-done.3), channel_id=1, source_target_pairs={{0,64},{32,96},{64,128},{96,160},{128,192},{160,224},{192,256},{22... | collective-permute-start | bytes 1572872 | tf_op jit(solution)/shard_map/ppermute | solution.py:198
  23.9 1.0 %constant_dynamic-slice_fusion.2 = bf16[512,32]{1,0:T(8,128)(2,1)S(1)} fusion(bf16[512,512]{1,0:T(8,128)(2,1)} %w_gate.1, s32[]{:T(128)S(6)} %select_n.30), kind=kLoop, calls=%fused_computation.7 | loop fusion | bytes 65540 | tf_op jit(solution)/shard_map/dynamic_slice | solution.py:229
  24.9 0.1 copy.19
  25.0 1.1 %constant_dynamic-slice_fusion = (bf16[512,32]{1,0:T(8,128)(2,1)S(1)}, bf16[512,32]{1,0:T(8,128)(2,1)S(1)}) fusion(bf16[512,512]{1,0:T(8,128)(2,1)} %w_down.1, s32[]{:T(128)S(6)} %select_n.30, bf16[512,512]{1,0:T(8,128)(2,1)} %w_up.1), kind=kLoop, calls=%fused_computation.5 | loop fusion | bytes 131076 | tf_op jit(solution)/shard_map/dynamic_slice | solution.py:229
  26.2 0.1 copy.21
  26.2 0.1 copy.20
  26.3 17.8 %all-to-all-done.came = bf16[8,96,512]{2,1,0:T(8,128)(2,1)S(1)} async-done(((bf16[8,96,512]{2,1,0:T(8,128)(2,1)}), bf16[8,96,512]{2,1,0:T(8,128)(2,1)S(1)}, u32[]{:S(2)}, u32[]{:S(2)}) %all-to-all-start) | async-done | bytes 786464 | tf_op jit(solution)/shard_map/all_to_all | solution.py:228
  44.2 2.0 %shard_map.149 = (f32[32,512]{1,0:T(8,128)}, f32[32,512]{1,0:T(8,128)}, f32[32,512]{1,0:T(8,128)}, bf16[4,96,512]{2,1,0:T(8,128)(2,1)}) custom-call(bf16[8,96,512]{2,1,0:T(8,128)(2,1)S(1)} %all-to-all-done.came, bf16[96,512]{1,0:T(8,128)(2,1)S(1)} %maximum_bitcast_fusion.refs_0_, f32[32,512]{1,0:T(8,128)} %bitcast.14, f32[32,512]{1,0:T(8,128)} %bitcast.15, ...), custom_call_target="tpu_custom_call" | custom-call | tf_op jit(solution)/shard_map/pallas_call | solution.py:251
  46.2 0.0 copy-start.4
  46.2 3.6 %all-to-all-start.1 = ((bf16[4,96,512]{2,1,0:T(8,128)(2,1)}), bf16[4,96,512]{2,1,0:T(8,128)(2,1)S(1)}, u32[]{:S(2)}, u32[]{:S(2)}) async-start(bf16[4,96,512]{2,1,0:T(8,128)(2,1)} %get-tuple-element.14), calls=%async_computation.1 | async-start | bytes 786432 | tf_op jit(solution)/shard_map/all_to_all | solution.py:260
  49.8 0.0 copy-done.4
  49.8 1.4 %collective-permute-start.6 = (bf16[512,512]{1,0:T(8,128)(2,1)S(1)}, bf16[512,512]{1,0:T(8,128)(2,1)S(1)}, u32[]{:S(2)}, u32[]{:S(2)}) collective-permute-start(bf16[512,512]{1,0:T(8,128)(2,1)S(1)} %copy-done.4), channel_id=1, source_target_pairs={{0,64},{32,96},{64,128},{96,160},{128,192},{160,224},{192,256},{22... | collective-permute-start | bytes 1572872 | tf_op jit(solution)/shard_map/ppermute | solution.py:199
  51.3 0.0 collective-permute-done.5.refs_1_
  51.3 0.0 copy-start.5
  51.3 0.9 %broadcast_select_fusion.1 = bf16[512,512]{1,0:T(8,128)(2,1)} fusion(bf16[512,512]{1,0:T(8,128)(2,1)S(1)} %copy-done.3, bf16[512,512]{1,0:T(8,128)(2,1)S(1)} %collective-permute-done.5.refs_1_, pred[]{:T(512)S(6)} %eq.6), kind=kLoop, calls=%fused_computation.1 | loop fusion | flops 262144 | bytes 1572865 | tf_op jit(solution)/shard_map/jit(_where)/select_n | solution.py:231
  52.2 0.0 copy-done.5
  52.2 3.4 %collective-permute-start.7 = (bf16[512,512]{1,0:T(8,128)(2,1)}, bf16[512,512]{1,0:T(8,128)(2,1)S(1)}, u32[]{:S(2)}, u32[]{:S(2)}) collective-permute-start(bf16[512,512]{1,0:T(8,128)(2,1)} %broadcast_select_fusion.1), channel_id=1, source_target_pairs={{0,32},{32,0},{64,96},{96,64},{128,160},{160,128},{192,224},{224,1... | collective-permute-start | bytes 1572872 | tf_op jit(solution)/shard_map/ppermute | solution.py:231
  55.6 6.2 %all-to-all-done.1.same = bf16[4,96,512]{2,1,0:T(8,128)(2,1)S(1)} async-done(((bf16[4,96,512]{2,1,0:T(8,128)(2,1)}), bf16[4,96,512]{2,1,0:T(8,128)(2,1)S(1)}, u32[]{:S(2)}, u32[]{:S(2)}) %all-to-all-start.1) | async-done | bytes 393248 | tf_op jit(solution)/shard_map/all_to_all | solution.py:260
  61.9 1.9 %collective-permute-start.1 = (bf16[2,96,512]{2,1,0:T(8,128)(2,1)S(1)}, bf16[2,96,512]{2,1,0:T(8,128)(2,1)S(1)}, u32[]{:S(2)}, u32[]{:S(2)}) collective-permute-start(bf16[2,96,512]{2,1,0:T(8,128)(2,1)S(1)} %get-tuple-element.15), channel_id=1, source_target_pairs={{0,64},{32,96},{64,128},{96,160},{128,192},{160,224},{192,256},{22... | collective-permute-start | bytes 589832 | tf_op jit(solution)/shard_map/ppermute | solution.py:268
  63.8 4.6 %collective-permute-start.2 = (bf16[2,96,512]{2,1,0:T(8,128)(2,1)S(1)}, bf16[2,96,512]{2,1,0:T(8,128)(2,1)S(1)}, u32[]{:S(2)}, u32[]{:S(2)}) collective-permute-start(bf16[2,96,512]{2,1,0:T(8,128)(2,1)S(1)} %get-tuple-element.16), channel_id=1, source_target_pairs={{0,448},{32,480},{64,0},{96,32},{128,64},{160,96},{192,128},{224,1... | collective-permute-start | bytes 589832 | tf_op jit(solution)/shard_map/ppermute | solution.py:269
  68.4 1.0 %collective-permute-done.6.refs_2_ = bf16[512,512]{1,0:T(8,128)(2,1)S(1)} collective-permute-done((bf16[512,512]{1,0:T(8,128)(2,1)S(1)}, bf16[512,512]{1,0:T(8,128)(2,1)S(1)}, u32[]{:S(2)}, u32[]{:S(2)}) %collective-permute-start.6) | collective-permute-done | bytes 524320 | tf_op jit(solution)/shard_map/ppermute | solution.py:199
  69.4 0.1 broadcast_select_fusion
  69.5 0.7 copy-done.6
  70.2 5.0 %collective-permute-start.8 = (bf16[512,512]{1,0:T(8,128)(2,1)S(1)}, bf16[512,512]{1,0:T(8,128)(2,1)S(1)}, u32[]{:S(2)}, u32[]{:S(2)}) collective-permute-start(bf16[512,512]{1,0:T(8,128)(2,1)S(1)} %broadcast_select_fusion), channel_id=1, source_target_pairs={{0,32},{32,0},{64,96},{96,64},{128,160},{160,128},{192,224},{224,1... | collective-permute-start | bytes 1572872 | tf_op jit(solution)/shard_map/ppermute | solution.py:232
  75.2 1.9 %collective-permute-start.3 = (bf16[4,96,512]{2,1,0:T(8,128)(2,1)S(1)}, bf16[4,96,512]{2,1,0:T(8,128)(2,1)S(1)}, u32[]{:S(2)}, u32[]{:S(2)}) collective-permute-start(bf16[4,96,512]{2,1,0:T(8,128)(2,1)S(1)} %all-to-all-done.1.same), channel_id=1, source_target_pairs={{0,32},{32,0},{64,96},{96,64},{128,160},{160,128},{192,224},{224,1... | collective-permute-start | bytes 1179656 | tf_op jit(solution)/shard_map/ppermute | solution.py:270
  77.1 0.0 collective-permute-done.1
  77.1 0.0 collective-permute-done.2
  77.2 2.4 %collective-permute-start.4 = (bf16[4,96,512]{2,1,0:T(8,128)(2,1)S(1)}, bf16[4,96,512]{2,1,0:T(8,128)(2,1)S(1)}, u32[]{:S(2)}, u32[]{:S(2)}) collective-permute-start(bf16[4,96,512]{2,1,0:T(8,128)(2,1)S(1)} %constant_dynamic-update-slice_fusion.sides), channel_id=1, source_target_pairs={{0,32},{32,0},{64,96},{96,64},{128,160},{160,128},{192,224},{224,1... | collective-permute-start | bytes 1179656 | tf_op jit(solution)/shard_map/ppermute | solution.py:272
  79.6 0.0 copy-start.2
  79.6 0.0 collective-permute-done.7.refs_3_
  79.6 0.0 copy-start.7
  79.6 0.0 collective-permute-done.8.refs_4_
  79.6 0.0 copy-start.8
  79.7 0.8 copy-done.7
  80.4 0.2 copy-done.8
  80.6 0.0 copy-done.2
  80.6 4.8 %shard_map.151.attn = f32[512,512]{1,0:T(8,128)S(1)} custom-call(s32[1]{0:T(128)} %bitcast.7.first, s32[4]{0:T(128)S(1)} %copy-done.2, bf16[512,512]{1,0:T(8,128)(2,1)} %q.1, bf16[512,512]{1,0:T(8,128)(2,1)} %copy-done.5, bf16[512,512]{1,0:T(8,128)(2,1)} %copy-done.6, bf16[512,512]{1,0:T(8,128)(2,1)} %copy-done.7, bf16[512,512]{1,0:T(8,128)(2,1)} %copy-done.8, ...), custom_call_target="tpu_custom_call" | custom-call | tf_op jit(solution)/shard_map/pallas_call | solution.py:233
  85.5 0.0 collective-permute-done.3.same_swap
  85.5 0.0 collective-permute-done.4.sides_swap
  85.5 0.0 copy-done
  85.5 0.0 copy-done.1
  85.5 2.1 %shard_map.152 = bf16[512,512]{1,0:T(8,128)(2,1)} custom-call(s32[1]{0:T(128)} %bitcast.core, s32[1]{0:T(128)} %bitcast.1.chip, bf16[512,512]{1,0:T(8,128)(2,1)S(1)} %copy-done, bf16[4,96,512]{2,1,0:T(8,128)(2,1)S(1)} %all-to-all-done.1.same, bf16[4,96,512]{2,1,0:T(8,128)(2,1)S(1)} %constant_dynamic-update-slice_fusion.sides, ...), custom_call_target="tpu_custom_call" | custom-call | tf_op jit(solution)/shard_map/pallas_call | solution.py:273
  (8 shorter events, 0.1 us)
Async XLA Ops:
  5.2 10.7 %collective-permute-start = (bf16[8,96,512]{2,1,0:T(8,128)(2,1)S(1)}, bf16[8,96,512]{2,1,0:T(8,128)(2,1)S(1)}, u32[]{:S(2)}, u32[]{:S(2)}) collective-permute-start(bf16[8,96,512]{2,1,0:T(8,128)(2,1)S(1)} %get-tuple-element.13), channel_id=1, source_target_pairs={{0,32},{32,0},{64,96},{96,64},{128,160},{160,128},{192,224},{224,1... | collective-permute-start | bytes 2359304 | tf_op jit(solution)/shard_map/ppermute | solution.py:220
  16.9 3.7 %copy-start.3 = (bf16[512,512]{1,0:T(8,128)(2,1)S(1)}, bf16[512,512]{1,0:T(8,128)(2,1)}, u32[]{:S(2)}) copy-start(bf16[512,512]{1,0:T(8,128)(2,1)} %refs_5_.1) | copy-start | bytes 1572868
  16.9 27.3 %all-to-all-start = ((bf16[8,96,512]{2,1,0:T(8,128)(2,1)}), bf16[8,96,512]{2,1,0:T(8,128)(2,1)S(1)}, u32[]{:S(2)}, u32[]{:S(2)}) async-start(bf16[8,96,512]{2,1,0:T(8,128)(2,1)} %shard_map.148), calls=%async_computation | async-start | bytes 1572864 | tf_op jit(solution)/shard_map/all_to_all | solution.py:228
  20.6 30.6 %collective-permute-start.5 = (bf16[512,512]{1,0:T(8,128)(2,1)S(1)}, bf16[512,512]{1,0:T(8,128)(2,1)S(1)}, u32[]{:S(2)}, u32[]{:S(2)}) collective-permute-start(bf16[512,512]{1,0:T(8,128)(2,1)S(1)} %copy-done.3), channel_id=1, source_target_pairs={{0,64},{32,96},{64,128},{96,160},{128,192},{160,224},{192,256},{22... | collective-permute-start | bytes 1572872 | tf_op jit(solution)/shard_map/ppermute | solution.py:198
  46.2 3.6 %copy-start.4 = (bf16[512,512]{1,0:T(8,128)(2,1)S(1)}, bf16[512,512]{1,0:T(8,128)(2,1)}, u32[]{:S(2)}) copy-start(bf16[512,512]{1,0:T(8,128)(2,1)} %refs_6_.1) | copy-start | bytes 1572868
  46.2 15.7 %all-to-all-start.1 = ((bf16[4,96,512]{2,1,0:T(8,128)(2,1)}), bf16[4,96,512]{2,1,0:T(8,128)(2,1)S(1)}, u32[]{:S(2)}, u32[]{:S(2)}) async-start(bf16[4,96,512]{2,1,0:T(8,128)(2,1)} %get-tuple-element.14), calls=%async_computation.1 | async-start | bytes 786432 | tf_op jit(solution)/shard_map/all_to_all | solution.py:260
  49.8 19.6 %collective-permute-start.6 = (bf16[512,512]{1,0:T(8,128)(2,1)S(1)}, bf16[512,512]{1,0:T(8,128)(2,1)S(1)}, u32[]{:S(2)}, u32[]{:S(2)}) collective-permute-start(bf16[512,512]{1,0:T(8,128)(2,1)S(1)} %copy-done.4), channel_id=1, source_target_pairs={{0,64},{32,96},{64,128},{96,160},{128,192},{160,224},{192,256},{22... | collective-permute-start | bytes 1572872 | tf_op jit(solution)/shard_map/ppermute | solution.py:199
  51.3 1.0 %copy-start.5 = (bf16[512,512]{1,0:T(8,128)(2,1)}, bf16[512,512]{1,0:T(8,128)(2,1)S(1)}, u32[]{:S(2)}) copy-start(bf16[512,512]{1,0:T(8,128)(2,1)S(1)} %collective-permute-done.5.refs_1_) | copy-start | bytes 1572868
  52.2 27.4 %collective-permute-start.7 = (bf16[512,512]{1,0:T(8,128)(2,1)}, bf16[512,512]{1,0:T(8,128)(2,1)S(1)}, u32[]{:S(2)}, u32[]{:S(2)}) collective-permute-start(bf16[512,512]{1,0:T(8,128)(2,1)} %broadcast_select_fusion.1), channel_id=1, source_target_pairs={{0,32},{32,0},{64,96},{96,64},{128,160},{160,128},{192,224},{224,1... | collective-permute-start | bytes 1572872 | tf_op jit(solution)/shard_map/ppermute | solution.py:231
  61.9 15.2 %collective-permute-start.1 = (bf16[2,96,512]{2,1,0:T(8,128)(2,1)S(1)}, bf16[2,96,512]{2,1,0:T(8,128)(2,1)S(1)}, u32[]{:S(2)}, u32[]{:S(2)}) collective-permute-start(bf16[2,96,512]{2,1,0:T(8,128)(2,1)S(1)} %get-tuple-element.15), channel_id=1, source_target_pairs={{0,64},{32,96},{64,128},{96,160},{128,192},{160,224},{192,256},{22... | collective-permute-start | bytes 589832 | tf_op jit(solution)/shard_map/ppermute | solution.py:268
  63.8 13.3 %collective-permute-start.2 = (bf16[2,96,512]{2,1,0:T(8,128)(2,1)S(1)}, bf16[2,96,512]{2,1,0:T(8,128)(2,1)S(1)}, u32[]{:S(2)}, u32[]{:S(2)}) collective-permute-start(bf16[2,96,512]{2,1,0:T(8,128)(2,1)S(1)} %get-tuple-element.16), channel_id=1, source_target_pairs={{0,448},{32,480},{64,0},{96,32},{128,64},{160,96},{192,128},{224,1... | collective-permute-start | bytes 589832 | tf_op jit(solution)/shard_map/ppermute | solution.py:269
  69.4 0.8 copy-start.6
  70.2 9.4 %collective-permute-start.8 = (bf16[512,512]{1,0:T(8,128)(2,1)S(1)}, bf16[512,512]{1,0:T(8,128)(2,1)S(1)}, u32[]{:S(2)}, u32[]{:S(2)}) collective-permute-start(bf16[512,512]{1,0:T(8,128)(2,1)S(1)} %broadcast_select_fusion), channel_id=1, source_target_pairs={{0,32},{32,0},{64,96},{96,64},{128,160},{160,128},{192,224},{224,1... | collective-permute-start | bytes 1572872 | tf_op jit(solution)/shard_map/ppermute | solution.py:232
  75.2 10.3 %collective-permute-start.3 = (bf16[4,96,512]{2,1,0:T(8,128)(2,1)S(1)}, bf16[4,96,512]{2,1,0:T(8,128)(2,1)S(1)}, u32[]{:S(2)}, u32[]{:S(2)}) collective-permute-start(bf16[4,96,512]{2,1,0:T(8,128)(2,1)S(1)} %all-to-all-done.1.same), channel_id=1, source_target_pairs={{0,32},{32,0},{64,96},{96,64},{128,160},{160,128},{192,224},{224,1... | collective-permute-start | bytes 1179656 | tf_op jit(solution)/shard_map/ppermute | solution.py:270
  77.2 8.3 %collective-permute-start.4 = (bf16[4,96,512]{2,1,0:T(8,128)(2,1)S(1)}, bf16[4,96,512]{2,1,0:T(8,128)(2,1)S(1)}, u32[]{:S(2)}, u32[]{:S(2)}) collective-permute-start(bf16[4,96,512]{2,1,0:T(8,128)(2,1)S(1)} %constant_dynamic-update-slice_fusion.sides), channel_id=1, source_target_pairs={{0,32},{32,0},{64,96},{96,64},{128,160},{160,128},{192,224},{224,1... | collective-permute-start | bytes 1179656 | tf_op jit(solution)/shard_map/ppermute | solution.py:272
  79.6 1.0 %copy-start.2 = (s32[4]{0:T(128)S(1)}, s32[4]{0:T(128)}, u32[]{:S(2)}) copy-start(s32[4]{0:T(128)} %lengths.1) | copy-start | bytes 52
  79.6 0.8 copy-start.7
  79.6 1.0 %copy-start.8 = (bf16[512,512]{1,0:T(8,128)(2,1)}, bf16[512,512]{1,0:T(8,128)(2,1)S(1)}, u32[]{:S(2)}) copy-start(bf16[512,512]{1,0:T(8,128)(2,1)S(1)} %collective-permute-done.8.refs_4_) | copy-start | bytes 1572868
  80.6 4.9 %copy-start = (bf16[512,512]{1,0:T(8,128)(2,1)S(1)}, bf16[512,512]{1,0:T(8,128)(2,1)}, u32[]{:S(2)}) copy-start(bf16[512,512]{1,0:T(8,128)(2,1)} %q.1) | copy-start | bytes 1572868
  80.6 4.9 %copy-start.1 = (f32[512]{0:T(512)S(1)}, f32[512]{0:T(512)}, u32[]{:S(2)}) copy-start(f32[512]{0:T(512)} %param.17) | copy-start | bytes 6148

commit v6 on v4

--- a/solution.py
+++ b/solution.py
@@ -99,7 +99,14 @@
 BLOCK = 256
 
 
-def attention_kernel(first, lengths, q, k2, v2, k1, v1, k0, v0, out):
+def attention_kernel(first, lengths, *refs):
+    out, bufs, sems = refs[7], refs[8:15], refs[15]
+    copies = [pltpu.make_async_copy(refs[n], bufs[n], sems.at[n]) for n in range(7)]
+    for copy in copies:
+        copy.start()
+    for copy in copies:
+        copy.wait()
+    q, k2, v2, k1, v1, k0, v0 = bufs
     for b in range(TOK // BLOCK):
         qb = q[b * BLOCK : (b + 1) * BLOCK]
         qpos = first[0] + b * BLOCK + lax.broadcasted_iota(jnp.int32, (BLOCK, 1), 0)
@@ -207,34 +214,35 @@
     came = lax.all_to_all(both, "seq", 0, 0, axis_index_groups=SAME_CORE)
     weights = [lax.dynamic_slice_in_dim(w, index * COLS, COLS, 1) for w in (w_gate, w_up, w_down)]
     weights = jnp.concatenate(weights, axis=1).T
-    *news, spread = pl.pallas_call(
-        update_kernel,
-        out_shape=(jax.ShapeDtypeStruct((COLS, TOK), f32),) * 3 + (pltpu.VMEM(piece.shape, bf16),),
-        in_specs=[VMEM] * 2 + [HBM] * 3,
-        out_specs=(VMEM,) * 4,
-        scratch_shapes=[pltpu.VMEM((COLS, TOK), f32)] * 3 + [pltpu.SemaphoreType.DMA((3,))],
-        compiler_params=PARAMS,
-    )(near_core(came), near_core(weights), far(mom_gate.T), far(mom_up.T), far(mom_down.T))
-    same = lax.all_to_all(spread, "seq", 0, 0, axis_index_groups=SAME_CORE)
     near_k = lax.ppermute(jnp.where(core == 0, keys, k2), "seq", PARTNER)
     near_v = lax.ppermute(jnp.where(core == 0, values, v2), "seq", PARTNER)
     attn = pl.pallas_call(
         attention_kernel,
         out_shape=jax.ShapeDtypeStruct((TOK, TOK), f32),
-        in_specs=[SMEM, SMEM] + [VMEM] * 7,
+        in_specs=[SMEM, SMEM] + [HBM] * 7,
         out_specs=VMEM,
+        scratch_shapes=[pltpu.VMEM((TOK, TOK), bf16)] * 7 + [pltpu.SemaphoreType.DMA((7,))],
         compiler_params=PARAMS,
     )(
         jnp.reshape(index * TOK, (1,)),
         lengths,
-        near_core(queries),
-        near_core(k2),
-        near_core(v2),
-        near_core(near_k),
-        near_core(near_v),
-        near_core(keys),
-        near_core(values),
-    )
+        far(queries),
+        far(k2),
+        far(v2),
+        far(near_k),
+        far(near_v),
+        far(keys),
+        far(values),
+    )
+    *news, spread = pl.pallas_call(
+        update_kernel,
+        out_shape=(pltpu.VMEM((COLS, TOK), f32),) * 3 + (pltpu.VMEM(piece.shape, bf16),),
+        in_specs=[VMEM] * 2 + [HBM] * 3,
+        out_specs=(VMEM,) * 4,
+        scratch_shapes=[pltpu.VMEM((COLS, TOK), f32)] * 3 + [pltpu.SemaphoreType.DMA((3,))],
+        compiler_params=PARAMS,
+    )(near_core(came), near_core(weights), far(mom_gate.T), far(mom_up.T), far(mom_down.T))
+    same = lax.all_to_all(spread, "seq", 0, 0, axis_index_groups=SAME_CORE)
     swap = lax.ppermute(same, "seq", PARTNER)
     mixed = pl.pallas_call(
         fast_kernel,

time: 103 us -> 106 us (1.029)
  local copies, waits for them, and re-layouts: 2.39 us -> 5.16 us
    unnamed x13 -> x22, local copies, waits for them, and re-layouts: 0.27 us -> 3.03 us
    pallas_call x1, Pallas kernels: 3.46 us -> 4.83 us  [local(): pl.pallas_call(attention_kernel, out_shape=jax.ShapeDtypeStruct((TOK, TOK...]
    pallas_call x1, Pallas kernels: 3.16 us -> 2.05 us  [local(): pl.pallas_call(fast_kernel, out_shape=jax.ShapeDtypeStruct((TOK, TOK), bf...]
  transfers between devices with their start and end apart: 8 -> 8, of which waited for: 5 -> 5; matrix products, arithmetic and copies ran while one was open for 4% -> 6% of each run, Pallas kernels for 3% -> 5%
where the time goes in v6:
time: 106 us; the launch traced here: 104 us
  waiting for transfers between devices  50.5 us (48%)
  starting transfers between devices  30.6 us (29%)
  Pallas kernels  14.7 us (14%)
  local copies, waits for them, and re-layouts  5.16 us (5%)
  other arithmetic  2.02 us (2%)
    all_to_all x1, waiting for transfers between devices, local(): came = lax.all_to_all(both, 'seq', 0, 0, axis_index_groups=SAME_CORE)  21.1 us
    ppermute x1, waiting for transfers between devices, local(): k2 = lax.ppermute(keys, 'seq', NEXT_CHIP)  21 us
    ppermute x1, starting transfers between devices, local(): got = lax.ppermute(other, 'seq', PARTNER)  8.75 us
    pallas_call x1, Pallas kernels, local(): pl.pallas_call(attention_kernel, out_shape=jax.ShapeDtypeStruct((TOK, TOK...  4.83 us
    ppermute x1, waiting for transfers between devices, local(): v2 = lax.ppermute(values, 'seq', NEXT_CHIP)  4.72 us
    pallas_call x1, Pallas kernels, local(): pl.pallas_call(grads_kernel, out_shape=(pltpu.VMEM(piece.shape, bf16),) *...  4.59 us
    ppermute x1, starting transfers between devices, local(): v2 = lax.ppermute(values, 'seq', NEXT_CHIP)  3.88 us
    all_to_all x1, starting transfers between devices, local(): same = lax.all_to_all(spread, 'seq', 0, 0, axis_index_groups=SAME_CORE)  3.69 us
  transfers between devices with their start and end apart: 8, of which 5 were waited for; matrix products, arithmetic and copies ran while one was open for 6% of the time, Pallas kernels for 5%

profile of v6, /device:TPU:1, one launch (start us, length us, event | category | flops | bytes accessed | tf_op | source)
XLA Modules:
  0.0 103.8 jit_solution(809405948470601590)
XLA Ops:
  0.6 4.6 %shard_map.147 = (bf16[8,96,512]{2,1,0:T(8,128)(2,1)S(1)}, bf16[8,96,512]{2,1,0:T(8,128)(2,1)S(1)}) custom-call(s32[1]{0:T(128)} %bitcast.core, bf16[512,512]{1,0:T(8,128)(2,1)} %refs_5_.1, bf16[512,512]{1,0:T(8,128)(2,1)} %refs_6_.1, f32[1,512]{1,0:T(1,128)} %bitcast.19, bf16[512,512]{1,0:T(8,128)(2,1)} %w_gate.1, bf16[512,512]{1,0:T(8,128)(2,1)} %w_up.1, ...), custom_call_target="tpu_custom_call" | custom-call | tf_op jit(solution)/shard_map/pallas_call | solution.py:187
  5.2 8.7 %collective-permute-start = (bf16[8,96,512]{2,1,0:T(8,128)(2,1)S(1)}, bf16[8,96,512]{2,1,0:T(8,128)(2,1)S(1)}, u32[]{:S(2)}, u32[]{:S(2)}) collective-permute-start(bf16[8,96,512]{2,1,0:T(8,128)(2,1)S(1)} %get-tuple-element.11), channel_id=1, source_target_pairs={{0,32},{32,0},{64,96},{96,64},{128,160},{160,128},{192,224},{224,1... | collective-permute-start | bytes 2359304 | tf_op jit(solution)/shard_map/ppermute | solution.py:206
  14.0 1.9 %collective-permute-done.got = bf16[8,96,512]{2,1,0:T(8,128)(2,1)S(1)} collective-permute-done((bf16[8,96,512]{2,1,0:T(8,128)(2,1)S(1)}, bf16[8,96,512]{2,1,0:T(8,128)(2,1)S(1)}, u32[]{:S(2)}, u32[]{:S(2)}) %collective-permute-start) | collective-permute-done | bytes 786464 | tf_op jit(solution)/shard_map/ppermute | solution.py:206
  15.9 1.1 %shard_map.148 = bf16[8,96,512]{2,1,0:T(8,128)(2,1)} custom-call(bf16[8,96,512]{2,1,0:T(8,128)(2,1)S(1)} %get-tuple-element.10.mine, bf16[8,96,512]{2,1,0:T(8,128)(2,1)S(1)} %collective-permute-done.got), custom_call_target="tpu_custom_call" | custom-call | tf_op jit(solution)/shard_map/pallas_call | solution.py:207
  16.9 3.5 %all-to-all-start = ((bf16[8,96,512]{2,1,0:T(8,128)(2,1)}), bf16[8,96,512]{2,1,0:T(8,128)(2,1)S(1)}, u32[]{:S(2)}, u32[]{:S(2)}) async-start(bf16[8,96,512]{2,1,0:T(8,128)(2,1)} %shard_map.148), calls=%async_computation | async-start | bytes 1572864 | tf_op jit(solution)/shard_map/all_to_all | solution.py:214
  20.5 1.0 constant_dynamic-slice_fusion.2
  21.5 0.1 copy.19
  21.6 1.1 %constant_dynamic-slice_fusion = (bf16[512,32]{1,0:T(8,128)(2,1)S(1)}, bf16[512,32]{1,0:T(8,128)(2,1)S(1)}) fusion(bf16[512,512]{1,0:T(8,128)(2,1)} %w_down.1, s32[]{:T(128)S(6)} %select_n.25, bf16[512,512]{1,0:T(8,128)(2,1)} %w_up.1), kind=kLoop, calls=%fused_computation.3 | loop fusion | bytes 131076 | tf_op jit(solution)/shard_map/dynamic_slice | solution.py:215
  22.7 0.1 copy.21
  22.8 0.1 copy.20
  22.9 21.1 %all-to-all-done.came = bf16[8,96,512]{2,1,0:T(8,128)(2,1)S(1)} async-done(((bf16[8,96,512]{2,1,0:T(8,128)(2,1)}), bf16[8,96,512]{2,1,0:T(8,128)(2,1)S(1)}, u32[]{:S(2)}, u32[]{:S(2)}) %all-to-all-start) | async-done | bytes 786464 | tf_op jit(solution)/shard_map/all_to_all | solution.py:214
  44.0 2.2 %shard_map.149 = (f32[32,512]{1,0:T(8,128)S(1)}, f32[32,512]{1,0:T(8,128)S(1)}, f32[32,512]{1,0:T(8,128)S(1)}, bf16[8,96,512]{2,1,0:T(8,128)(2,1)}) custom-call(bf16[8,96,512]{2,1,0:T(8,128)(2,1)S(1)} %all-to-all-done.came, bf16[96,512]{1,0:T(8,128)(2,1)S(1)} %maximum_bitcast_fusion.refs_0_, f32[32,512]{1,0:T(8,128)} %bitcast.16, f32[32,512]{1,0:T(8,128)} %bitcast.17, ...), custom_call_target="tpu_custom_call" | custom-call | tf_op jit(solution)/shard_map/pallas_call | solution.py:237
  46.2 0.0 copy-start.3
  46.2 0.0 copy-start.4
  46.2 3.7 %all-to-all-start.1 = ((bf16[8,96,512]{2,1,0:T(8,128)(2,1)}), bf16[8,96,512]{2,1,0:T(8,128)(2,1)S(1)}, u32[]{:S(2)}, u32[]{:S(2)}) async-start(bf16[8,96,512]{2,1,0:T(8,128)(2,1)} %get-tuple-element.12), calls=%async_computation.1 | async-start | bytes 1572864 | tf_op jit(solution)/shard_map/all_to_all | solution.py:245
  49.9 0.0 copy-done.3
  49.9 3.3 %collective-permute-start.2 = (bf16[512,512]{1,0:T(8,128)(2,1)S(1)}, bf16[512,512]{1,0:T(8,128)(2,1)S(1)}, u32[]{:S(2)}, u32[]{:S(2)}) collective-permute-start(bf16[512,512]{1,0:T(8,128)(2,1)S(1)} %copy-done.3), channel_id=1, source_target_pairs={{0,64},{32,96},{64,128},{96,160},{128,192},{160,224},{192,256},{22... | collective-permute-start | bytes 1572872 | tf_op jit(solution)/shard_map/ppermute | solution.py:184
  53.2 0.0 copy-done.4
  53.2 3.9 %collective-permute-start.3 = (bf16[512,512]{1,0:T(8,128)(2,1)S(1)}, bf16[512,512]{1,0:T(8,128)(2,1)}, u32[]{:S(2)}, u32[]{:S(2)}) collective-permute-start(bf16[512,512]{1,0:T(8,128)(2,1)S(1)} %copy-done.4), channel_id=1, source_target_pairs={{0,64},{32,96},{64,128},{96,160},{128,192},{160,224},{192,256},{22... | collective-permute-start | bytes 1572872 | tf_op jit(solution)/shard_map/ppermute | solution.py:185
  57.1 21.0 %collective-permute-done.2.refs_1_ = bf16[512,512]{1,0:T(8,128)(2,1)S(1)} collective-permute-done((bf16[512,512]{1,0:T(8,128)(2,1)S(1)}, bf16[512,512]{1,0:T(8,128)(2,1)S(1)}, u32[]{:S(2)}, u32[]{:S(2)}) %collective-permute-start.2) | collective-permute-done | bytes 524320 | tf_op jit(solution)/shard_map/ppermute | solution.py:184
  78.1 0.0 copy-start.5
  78.1 0.9 broadcast_select_fusion.1
  79.0 0.0 copy-done.5
  79.0 3.6 %collective-permute-start.4 = (bf16[512,512]{1,0:T(8,128)(2,1)}, bf16[512,512]{1,0:T(8,128)(2,1)S(1)}, u32[]{:S(2)}, u32[]{:S(2)}) collective-permute-start(bf16[512,512]{1,0:T(8,128)(2,1)} %broadcast_select_fusion.1), channel_id=1, source_target_pairs={{0,32},{32,0},{64,96},{96,64},{128,160},{160,128},{192,224},{224,1... | collective-permute-start | bytes 1572872 | tf_op jit(solution)/shard_map/ppermute | solution.py:217
  82.6 0.0 all-to-all-done.1.same
  82.7 1.9 %collective-permute-start.1 = (bf16[8,96,512]{2,1,0:T(8,128)(2,1)S(1)}, bf16[8,96,512]{2,1,0:T(8,128)(2,1)S(1)}, u32[]{:S(2)}, u32[]{:S(2)}) collective-permute-start(bf16[8,96,512]{2,1,0:T(8,128)(2,1)S(1)} %all-to-all-done.1.same), channel_id=1, source_target_pairs={{0,32},{32,0},{64,96},{96,64},{128,160},{160,128},{192,224},{224,1... | collective-permute-start | bytes 2359304 | tf_op jit(solution)/shard_map/ppermute | solution.py:246
  84.6 4.7 %collective-permute-done.3.refs_2_ = bf16[512,512]{1,0:T(8,128)(2,1)} collective-permute-done((bf16[512,512]{1,0:T(8,128)(2,1)S(1)}, bf16[512,512]{1,0:T(8,128)(2,1)}, u32[]{:S(2)}, u32[]{:S(2)}) %collective-permute-start.3) | collective-permute-done | bytes 524320 | tf_op jit(solution)/shard_map/ppermute | solution.py:185
  89.3 1.1 %broadcast_select_fusion = bf16[512,512]{1,0:T(8,128)(2,1)S(1)} fusion(bf16[512,512]{1,0:T(8,128)(2,1)S(1)} %copy-done.4, bf16[512,512]{1,0:T(8,128)(2,1)} %collective-permute-done.3.refs_2_, pred[]{:T(512)S(6)} %eq.6), kind=kLoop, calls=%fused_computation | loop fusion | flops 262144 | bytes 1572865 | tf_op jit(solution)/shard_map/jit(_where)/select_n | solution.py:218
  90.4 1.9 %collective-permute-start.5 = (bf16[512,512]{1,0:T(8,128)(2,1)S(1)}, bf16[512,512]{1,0:T(8,128)(2,1)S(1)}, u32[]{:S(2)}, u32[]{:S(2)}) collective-permute-start(bf16[512,512]{1,0:T(8,128)(2,1)S(1)} %broadcast_select_fusion), channel_id=1, source_target_pairs={{0,32},{32,0},{64,96},{96,64},{128,160},{160,128},{192,224},{224,1... | collective-permute-start | bytes 1572872 | tf_op jit(solution)/shard_map/ppermute | solution.py:218
  92.3 0.0 copy-start.2
  92.4 0.0 collective-permute-done.4.refs_3_
  92.4 0.0 copy-start.6
  92.4 1.8 %collective-permute-done.5.refs_4_ = bf16[512,512]{1,0:T(8,128)(2,1)S(1)} collective-permute-done((bf16[512,512]{1,0:T(8,128)(2,1)S(1)}, bf16[512,512]{1,0:T(8,128)(2,1)S(1)}, u32[]{:S(2)}, u32[]{:S(2)}) %collective-permute-start.5) | collective-permute-done | bytes 524320 | tf_op jit(solution)/shard_map/ppermute | solution.py:218
  94.2 0.0 copy-start.7
  94.2 0.0 copy-done.6
  94.2 0.8 copy-done.7
  95.0 0.0 copy-done.2
  95.0 0.0 copy-start
  95.0 4.8 %shard_map.150.attn = f32[512,512]{1,0:T(8,128)S(1)} custom-call(s32[1]{0:T(128)} %bitcast.6.first, s32[4]{0:T(128)S(1)} %copy-done.2, bf16[512,512]{1,0:T(8,128)(2,1)} %q.1, bf16[512,512]{1,0:T(8,128)(2,1)} %copy-done.5, bf16[512,512]{1,0:T(8,128)(2,1)} %collective-permute-done.3.refs_2_, bf16[512,512]{1,0:T(8,128)(2,1)} %copy-done.6, ...), custom_call_target="tpu_custom_call" | custom-call | tf_op jit(solution)/shard_map/pallas_call | solution.py:219
  99.8 0.6 copy.22
  100.5 0.6 copy.23
  101.1 0.0 copy-start.1
  101.1 0.6 copy.24
  101.7 0.0 collective-permute-done.1.swap
  101.7 0.0 copy-done
  101.7 0.0 copy-done.1
  101.8 2.0 %shard_map.151 = bf16[512,512]{1,0:T(8,128)(2,1)} custom-call(s32[1]{0:T(128)} %bitcast.core, bf16[512,512]{1,0:T(8,128)(2,1)S(1)} %copy-done, bf16[8,96,512]{2,1,0:T(8,128)(2,1)S(1)} %all-to-all-done.1.same, bf16[8,96,512]{2,1,0:T(8,128)(2,1)S(1)} %collective-permute-done.1.swap, f32[512,512]{1,0:T(8,128)S(1)} %shard_map.150.attn, f32[1,512]{1,0:T(1,128)S(1)} %bitcast.15), custom_call_target="tpu_custom_call" | custom-call | tf_op jit(solution)/shard_map/pallas_call | solution.py:247
  (1 shorter events, 0.0 us)
Async XLA Ops:
  5.2 10.6 %collective-permute-start = (bf16[8,96,512]{2,1,0:T(8,128)(2,1)S(1)}, bf16[8,96,512]{2,1,0:T(8,128)(2,1)S(1)}, u32[]{:S(2)}, u32[]{:S(2)}) collective-permute-start(bf16[8,96,512]{2,1,0:T(8,128)(2,1)S(1)} %get-tuple-element.11), channel_id=1, source_target_pairs={{0,32},{32,0},{64,96},{96,64},{128,160},{160,128},{192,224},{224,1... | collective-permute-start | bytes 2359304 | tf_op jit(solution)/shard_map/ppermute | solution.py:206
  16.9 27.1 %all-to-all-start = ((bf16[8,96,512]{2,1,0:T(8,128)(2,1)}), bf16[8,96,512]{2,1,0:T(8,128)(2,1)S(1)}, u32[]{:S(2)}, u32[]{:S(2)}) async-start(bf16[8,96,512]{2,1,0:T(8,128)(2,1)} %shard_map.148), calls=%async_computation | async-start | bytes 1572864 | tf_op jit(solution)/shard_map/all_to_all | solution.py:214
  46.2 3.7 %copy-start.3 = (bf16[512,512]{1,0:T(8,128)(2,1)S(1)}, bf16[512,512]{1,0:T(8,128)(2,1)}, u32[]{:S(2)}) copy-start(bf16[512,512]{1,0:T(8,128)(2,1)} %refs_5_.1) | copy-start | bytes 1572868
  46.2 7.0 %copy-start.4 = (bf16[512,512]{1,0:T(8,128)(2,1)S(1)}, bf16[512,512]{1,0:T(8,128)(2,1)}, u32[]{:S(2)}) copy-start(bf16[512,512]{1,0:T(8,128)(2,1)} %refs_6_.1) | copy-start | bytes 1572868
  46.2 36.4 %all-to-all-start.1 = ((bf16[8,96,512]{2,1,0:T(8,128)(2,1)}), bf16[8,96,512]{2,1,0:T(8,128)(2,1)S(1)}, u32[]{:S(2)}, u32[]{:S(2)}) async-start(bf16[8,96,512]{2,1,0:T(8,128)(2,1)} %get-tuple-element.12), calls=%async_computation.1 | async-start | bytes 1572864 | tf_op jit(solution)/shard_map/all_to_all | solution.py:245
  49.9 28.1 %collective-permute-start.2 = (bf16[512,512]{1,0:T(8,128)(2,1)S(1)}, bf16[512,512]{1,0:T(8,128)(2,1)S(1)}, u32[]{:S(2)}, u32[]{:S(2)}) collective-permute-start(bf16[512,512]{1,0:T(8,128)(2,1)S(1)} %copy-done.3), channel_id=1, source_target_pairs={{0,64},{32,96},{64,128},{96,160},{128,192},{160,224},{192,256},{22... | collective-permute-start | bytes 1572872 | tf_op jit(solution)/shard_map/ppermute | solution.py:184
  53.2 36.1 %collective-permute-start.3 = (bf16[512,512]{1,0:T(8,128)(2,1)S(1)}, bf16[512,512]{1,0:T(8,128)(2,1)}, u32[]{:S(2)}, u32[]{:S(2)}) collective-permute-start(bf16[512,512]{1,0:T(8,128)(2,1)S(1)} %copy-done.4), channel_id=1, source_target_pairs={{0,64},{32,96},{64,128},{96,160},{128,192},{160,224},{192,256},{22... | collective-permute-start | bytes 1572872 | tf_op jit(solution)/shard_map/ppermute | solution.py:185
  78.1 1.0 copy-start.5
  79.0 13.3 %collective-permute-start.4 = (bf16[512,512]{1,0:T(8,128)(2,1)}, bf16[512,512]{1,0:T(8,128)(2,1)S(1)}, u32[]{:S(2)}, u32[]{:S(2)}) collective-permute-start(bf16[512,512]{1,0:T(8,128)(2,1)} %broadcast_select_fusion.1), channel_id=1, source_target_pairs={{0,32},{32,0},{64,96},{96,64},{128,160},{160,128},{192,224},{224,1... | collective-permute-start | bytes 1572872 | tf_op jit(solution)/shard_map/ppermute | solution.py:217
  82.7 19.1 %collective-permute-start.1 = (bf16[8,96,512]{2,1,0:T(8,128)(2,1)S(1)}, bf16[8,96,512]{2,1,0:T(8,128)(2,1)S(1)}, u32[]{:S(2)}, u32[]{:S(2)}) collective-permute-start(bf16[8,96,512]{2,1,0:T(8,128)(2,1)S(1)} %all-to-all-done.1.same), channel_id=1, source_target_pairs={{0,32},{32,0},{64,96},{96,64},{128,160},{160,128},{192,224},{224,1... | collective-permute-start | bytes 2359304 | tf_op jit(solution)/shard_map/ppermute | solution.py:246
  90.4 3.8 %collective-permute-start.5 = (bf16[512,512]{1,0:T(8,128)(2,1)S(1)}, bf16[512,512]{1,0:T(8,128)(2,1)S(1)}, u32[]{:S(2)}, u32[]{:S(2)}) collective-permute-start(bf16[512,512]{1,0:T(8,128)(2,1)S(1)} %broadcast_select_fusion), channel_id=1, source_target_pairs={{0,32},{32,0},{64,96},{96,64},{128,160},{160,128},{192,224},{224,1... | collective-permute-start | bytes 1572872 | tf_op jit(solution)/shard_map/ppermute | solution.py:218
  92.3 2.7 %copy-start.2 = (s32[4]{0:T(128)S(1)}, s32[4]{0:T(128)}, u32[]{:S(2)}) copy-start(s32[4]{0:T(128)} %lengths.1) | copy-start | bytes 52
  92.4 1.9 %copy-start.6 = (bf16[512,512]{1,0:T(8,128)(2,1)}, bf16[512,512]{1,0:T(8,128)(2,1)S(1)}, u32[]{:S(2)}) copy-start(bf16[512,512]{1,0:T(8,128)(2,1)S(1)} %collective-permute-done.4.refs_3_) | copy-start | bytes 1572868
  94.2 0.8 copy-start.7
  95.0 6.7 %copy-start = (bf16[512,512]{1,0:T(8,128)(2,1)S(1)}, bf16[512,512]{1,0:T(8,128)(2,1)}, u32[]{:S(2)}) copy-start(bf16[512,512]{1,0:T(8,128)(2,1)} %q.1) | copy-start | bytes 1572868
  101.1 0.7 copy-start.1
